TPU v7x, 512 devices: a whole 4x8x8 slice. The times are simulated.
512 devices in a mesh: frame: 16 (over y, z_hi), seq: 32 (over z_lo, x, core).
Axes of the slice: x: 4, y: 8, z: 8 (z_hi: 2, z_lo: 4; z = z_hi * 4 + z_lo), core: 2. Of those that a mesh axis runs over, the one named last changes fastest.
Arguments:
- vid_q: bfloat16 [16, 1024, 2048], P('frame', 'seq'), may hold values from -6 to 6
- vid_k: bfloat16 [16, 1024, 2048], P('frame', 'seq'), may hold values from -6 to 6
- vid_v: bfloat16 [16, 1024, 2048], P('frame', 'seq'), may hold values from -6 to 6
- vid_dout: bfloat16 [16, 1024, 2048], P('frame', 'seq'), may hold values from -6 to 6
- aud_q: bfloat16 [16, 3072, 2048], P('frame', 'seq'), may hold values from -6 to 6
- aud_k: bfloat16 [16, 3072, 2048], P('frame', 'seq'), may hold values from -6 to 6
- aud_v: bfloat16 [16, 3072, 2048], P('frame', 'seq'), may hold values from -6 to 6
- aud_dout: bfloat16 [16, 3072, 2048], P('frame', 'seq'), may hold values from -6 to 6
- aud_len: int32 [16, 32], replicated, may hold values from 32 to 96, as said below
- match: int32 [16], replicated, may hold values from 0 to 15, each once
Outputs:
- d_vid_q: bfloat16 [16, 1024, 2048], P('frame', 'seq')
- d_vid_k: bfloat16 [16, 1024, 2048], P('frame', 'seq')
- d_vid_v: bfloat16 [16, 1024, 2048], P('frame', 'seq')
- d_aud_q: bfloat16 [16, 3072, 2048], P('frame', 'seq')
- d_aud_k: bfloat16 [16, 3072, 2048], P('frame', 'seq')
- d_aud_v: bfloat16 [16, 3072, 2048], P('frame', 'seq')
Inputs may be any that keep to these rules, and one draw needn't show every extreme that they name: `aud_len`: every entry is a whole multiple of 32; in every frame group one time block has 96 live slots and another has 32. match names every frame group once.
All inputs are finite; a program needn't handle non-finite values.
Results may differ from a plain program's by a relative error of at most 0.012.
The roundings to bfloat16 on the way count: a program that leaves them out, or rounds other values in their place, can miss the bound.
Values may be sent and summed in bfloat16 or wider, within the bound.
No kernel may reach another device: no remote copies, remote signals or barrier semaphores. Data moves between devices by JAX's collectives and lax.ppermute only.
A program may use at most 64 MiB of HBM per device.

v0:
```python
import jax
import jax.numpy as jnp
from jax import lax
from jax.sharding import PartitionSpec as P

HD = 128
BAND = 2


NEG_BIG = -1e30


def from_behind(x, axis, by):
    peers = lax.axis_size(axis)
    pairs = [(i, i + by) for i in range(peers) if 0 <= i + by < peers]
    return lax.ppermute(x, axis, pairs)


def query_side(queries, key_rows, val_rows, grad_out, key_mask):
    factor = HD ** (-0.5)
    scores = (
        jnp.einsum("fhqd,fhkd->fhqk", queries, key_rows, preferred_element_type=jnp.float32)
        * factor
    )
    scores = jnp.where(key_mask[:, None, None, :], scores, NEG_BIG)
    largest = jnp.max(scores, axis=-1, keepdims=True)
    exponent = jnp.exp(scores - largest)
    totals = jnp.sum(exponent, axis=-1, keepdims=True)
    weights = exponent / totals
    weights_half = weights.astype(jnp.bfloat16)
    output = jnp.einsum(
        "fhqk,fhkd->fhqd", weights_half, val_rows, preferred_element_type=jnp.float32
    )
    deltas = jnp.sum(grad_out.astype(jnp.float32) * output, axis=-1, keepdims=True)
    grad_weights = jnp.einsum(
        "fhqd,fhkd->fhqk", grad_out, val_rows, preferred_element_type=jnp.float32
    )
    grad_scores = (weights * (grad_weights - deltas)).astype(jnp.bfloat16)
    grad_query = (
        jnp.einsum("fhqk,fhkd->fhqd", grad_scores, key_rows, preferred_element_type=jnp.float32)
        * factor
    )
    return (grad_query, weights_half, grad_scores, largest[..., 0], totals[..., 0], deltas[..., 0])


def shards(vid_q, vid_k, vid_v, vid_dout, aud_q, aud_k, aud_v, aud_dout, aud_len, match):
    frames = lax.axis_size("frame")
    seq_count = lax.axis_size("seq")
    here = lax.axis_index("seq")
    moved = (
        lax.all_to_all(vid_q, "frame", split_axis=2, concat_axis=0, tiled=True),
        lax.all_to_all(vid_k, "frame", split_axis=2, concat_axis=0, tiled=True),
        lax.all_to_all(vid_v, "frame", split_axis=2, concat_axis=0, tiled=True),
        lax.all_to_all(vid_dout, "frame", split_axis=2, concat_axis=0, tiled=True),
        lax.all_to_all(aud_q, "frame", split_axis=2, concat_axis=0, tiled=True),
        lax.all_to_all(aud_k, "frame", split_axis=2, concat_axis=0, tiled=True),
        lax.all_to_all(aud_v, "frame", split_axis=2, concat_axis=0, tiled=True),
        lax.all_to_all(aud_dout, "frame", split_axis=2, concat_axis=0, tiled=True),
    )
    order = jnp.arange(frames, dtype=jnp.int32)
    inverse = jnp.sum(jnp.where(match[None, :] == order[:, None], order[None, :], 0), axis=1)
    video_query, video_key, video_value, video_grad = (moved[0], moved[1], moved[2], moved[3])
    audio_query = jnp.take(moved[4], match, axis=0)
    audio_key = jnp.take(moved[5], match, axis=0)
    audio_value = jnp.take(moved[6], match, axis=0)
    audio_grad = jnp.take(moved[7], match, axis=0)
    lengths = jnp.take(aud_len, match, axis=0)
    video_rows = video_query.shape[1]
    audio_rows = audio_query.shape[1]
    width_here = video_query.shape[2]
    heads_here = width_here // HD
    slots = lax.broadcasted_iota(jnp.int32, (frames, audio_rows), 1)

    def inside(offset):
        target = here + offset
        return (target >= 0) & (target < seq_count)

    def audio_mask(offset):
        column = lax.dynamic_index_in_dim(
            lengths, jnp.clip(here + offset, 0, seq_count - 1), 1, keepdims=True
        )
        return (slots < column) & inside(offset)

    def video_mask(offset):
        return jnp.broadcast_to(inside(offset), (frames, video_rows))

    def split(array):
        shaped = array.reshape(array.shape[:-1] + (heads_here, HD))
        return jnp.moveaxis(shaped, -2, -3)

    def joined(array):
        moved_back = jnp.moveaxis(array, -3, -2)
        return moved_back.reshape(moved_back.shape[:-2] + (width_here,))

    offsets = list(range(-BAND, BAND + 1))
    audio_grad = jnp.where(audio_mask(0)[:, :, None], audio_grad, jnp.zeros((), jnp.bfloat16))
    audio_keys_mask = jnp.concatenate([audio_mask(offset) for offset in offsets], axis=1)
    video_keys_mask = jnp.concatenate([video_mask(offset) for offset in offsets], axis=1)
    factor = HD ** (-0.5)
    packed = jnp.concatenate(
        [jnp.stack([video_key, video_value]), jnp.stack([audio_key, audio_value])], axis=2
    )
    nearby = []
    for offset in offsets:
        if offset == 0:
            nearby.append(packed)
        else:
            nearby.append(from_behind(packed, "seq", -offset))
    video_window = jnp.concatenate([member[:, :, :video_rows] for member in nearby], axis=2)
    audio_window = jnp.concatenate([member[:, :, video_rows:] for member in nearby], axis=2)
    video_side = query_side(
        split(video_query),
        split(audio_window[0]),
        split(audio_window[1]),
        split(video_grad),
        audio_keys_mask,
    )
    audio_side = query_side(
        split(audio_query),
        split(video_window[0]),
        split(video_window[1]),
        split(audio_grad),
        video_keys_mask,
    )
    grad_vq = joined(video_side[0])
    grad_aq = joined(audio_side[0])
    audio_key_terms = (
        jnp.einsum(
            "fhqk,fhqd->fhkd", video_side[2], split(video_query), preferred_element_type=jnp.float32
        )
        * factor
    )
    audio_value_terms = jnp.einsum(
        "fhqk,fhqd->fhkd", video_side[1], split(video_grad), preferred_element_type=jnp.float32
    )
    video_key_terms = (
        jnp.einsum(
            "fhqk,fhqd->fhkd", audio_side[2], split(audio_query), preferred_element_type=jnp.float32
        )
        * factor
    )
    video_value_terms = jnp.einsum(
        "fhqk,fhqd->fhkd", audio_side[1], split(audio_grad), preferred_element_type=jnp.float32
    )
    video_terms = jnp.stack(
        [
            joined(video_key_terms).astype(jnp.bfloat16),
            joined(video_value_terms).astype(jnp.bfloat16),
        ]
    )
    audio_terms = jnp.stack(
        [
            joined(audio_key_terms).astype(jnp.bfloat16),
            joined(audio_value_terms).astype(jnp.bfloat16),
        ]
    )
    summed = jnp.zeros((2, frames, video_rows + audio_rows, width_here), jnp.float32)
    for position, offset in enumerate(offsets):
        piece = jnp.concatenate(
            [
                video_terms[:, :, position * video_rows : (position + 1) * video_rows],
                audio_terms[:, :, position * audio_rows : (position + 1) * audio_rows],
            ],
            axis=2,
        )
        if offset == 0:
            summed = summed + piece.astype(jnp.float32)
        else:
            summed = summed + from_behind(piece, "seq", offset).astype(jnp.float32)
    grad_vk = summed[0, :, :video_rows]
    grad_vv = summed[1, :, :video_rows]
    grad_ak = summed[0, :, video_rows:]
    grad_av = summed[1, :, video_rows:]
    grad_aq = jnp.take(grad_aq, inverse, axis=0)
    grad_ak = jnp.take(grad_ak, inverse, axis=0)
    grad_av = jnp.take(grad_av, inverse, axis=0)
    returned = (
        lax.all_to_all(
            grad_vq.astype(jnp.bfloat16), "frame", split_axis=0, concat_axis=2, tiled=True
        ),
        lax.all_to_all(
            grad_vk.astype(jnp.bfloat16), "frame", split_axis=0, concat_axis=2, tiled=True
        ),
        lax.all_to_all(
            grad_vv.astype(jnp.bfloat16), "frame", split_axis=0, concat_axis=2, tiled=True
        ),
        lax.all_to_all(
            grad_aq.astype(jnp.bfloat16), "frame", split_axis=0, concat_axis=2, tiled=True
        ),
        lax.all_to_all(
            grad_ak.astype(jnp.bfloat16), "frame", split_axis=0, concat_axis=2, tiled=True
        ),
        lax.all_to_all(
            grad_av.astype(jnp.bfloat16), "frame", split_axis=0, concat_axis=2, tiled=True
        ),
    )
    return (returned[0], returned[1], returned[2], returned[3], returned[4], returned[5])


def solution(mesh):
    return jax.shard_map(
        shards,
        mesh=mesh,
        in_specs=(
            P("frame", "seq", None),
            P("frame", "seq", None),
            P("frame", "seq", None),
            P("frame", "seq", None),
            P("frame", "seq", None),
            P("frame", "seq", None),
            P("frame", "seq", None),
            P("frame", "seq", None),
            P(),
            P(),
        ),
        out_specs=(
            P("frame", "seq", None),
            P("frame", "seq", None),
            P("frame", "seq", None),
            P("frame", "seq", None),
            P("frame", "seq", None),
            P("frame", "seq", None),
        ),
        check_vma=False,
    )
```

profile of v0, /device:TPU:6, one launch (start us, length us, event | category | flops | bytes accessed | tf_op | source)
XLA Modules:
  0.0 465.5 jit_solution(14384253326329043053)
XLA Ops:
  3.3 11.5 %reduce.23 = bf16[2048,32]{1,0:T(8,128)(2,1)S(1)} reduce(bf16[2048,1,32]{2,1,0:T(2,128)(2,1)S(1)} %bitcast.231, bf16[]{:T(256)} %broadcast.159), dimensions={1}, to_apply=%bitcast.178.reduce_sub_computation | reduce | bytes 262146
  16.0 16.1 %all-to-all-start = ((bf16[16,2,2048]{2,1,0:T(2,128)(2,1)}), bf16[16,2,2048]{2,1,0:T(2,128)(2,1)S(1)}, u32[]{:S(2)}, u32[]{:S(2)}) async-start(bf16[16,2,2048]{2,1,0:T(2,128)(2,1)} %reshape.304), calls=%async_computation | async-start | bytes 262144 | tf_op jit(solution)/shard_map/all_to_all | solution.py:52
  32.8 11.5 %reduce.24 = bf16[2048,32]{1,0:T(8,128)(2,1)S(1)} reduce(bf16[2048,1,32]{2,1,0:T(2,128)(2,1)S(1)} %bitcast.237, bf16[]{:T(256)} %broadcast.159), dimensions={1}, to_apply=%bitcast.176.reduce_sub_computation | reduce | bytes 262146
  45.6 12.2 %all-to-all-start.1 = ((bf16[16,2,2048]{2,1,0:T(2,128)(2,1)}), bf16[16,2,2048]{2,1,0:T(2,128)(2,1)S(1)}, u32[]{:S(2)}, u32[]{:S(2)}) async-start(bf16[16,2,2048]{2,1,0:T(2,128)(2,1)} %reshape.302), calls=%async_computation.1 | async-start | bytes 262144 | tf_op jit(solution)/shard_map/all_to_all | solution.py:53
  58.6 11.5 %reduce.25 = bf16[2048,32]{1,0:T(8,128)(2,1)S(1)} reduce(bf16[2048,1,32]{2,1,0:T(2,128)(2,1)S(1)} %bitcast.238, bf16[]{:T(256)} %broadcast.159), dimensions={1}, to_apply=%bitcast.182.reduce_sub_computation | reduce | bytes 262146
  71.4 12.4 %all-to-all-start.4 = ((bf16[16,2,2048]{2,1,0:T(2,128)(2,1)}), bf16[16,2,2048]{2,1,0:T(2,128)(2,1)S(1)}, u32[]{:S(2)}, u32[]{:S(2)}) async-start(bf16[16,2,2048]{2,1,0:T(2,128)(2,1)} %reshape.308), calls=%async_computation.4 | async-start | bytes 262144 | tf_op jit(solution)/shard_map/all_to_all | solution.py:51
  84.5 11.5 %reduce.26 = bf16[2048,32]{1,0:T(8,128)(2,1)S(1)} reduce(bf16[2048,1,32]{2,1,0:T(2,128)(2,1)S(1)} %bitcast.239, bf16[]{:T(256)} %broadcast.159), dimensions={1}, to_apply=%bitcast.180.reduce_sub_computation | reduce | bytes 262146
  97.4 12.5 %all-to-all-start.5 = ((bf16[16,2,2048]{2,1,0:T(2,128)(2,1)}), bf16[16,2,2048]{2,1,0:T(2,128)(2,1)S(1)}, u32[]{:S(2)}, u32[]{:S(2)}) async-start(bf16[16,2,2048]{2,1,0:T(2,128)(2,1)} %reshape.306), calls=%async_computation.5 | async-start | bytes 262144 | tf_op jit(solution)/shard_map/all_to_all | solution.py:54
  110.7 11.6 %reduce.21 = bf16[2048,96]{1,0:T(8,128)(2,1)S(1)} reduce(bf16[2048,1,96]{2,1,0:T(2,128)(2,1)S(1)} %bitcast.240, bf16[]{:T(256)} %broadcast.159), dimensions={1}, to_apply=%bitcast.174.reduce_sub_computation | reduce | bytes 786434
  124.5 12.3 %all-to-all-start.2 = ((bf16[16,2,6144]{2,1,0:T(2,128)(2,1)}), bf16[16,2,6144]{2,1,0:T(2,128)(2,1)S(1)}, u32[]{:S(2)}, u32[]{:S(2)}) async-start(bf16[16,2,6144]{2,1,0:T(2,128)(2,1)} %reshape.300), calls=%async_computation.2 | async-start | bytes 786432 | tf_op jit(solution)/shard_map/all_to_all | solution.py:56
  137.6 11.6 %reduce.22 = bf16[2048,96]{1,0:T(8,128)(2,1)S(1)} reduce(bf16[2048,1,96]{2,1,0:T(2,128)(2,1)S(1)} %bitcast.241, bf16[]{:T(256)} %broadcast.159), dimensions={1}, to_apply=%bitcast.172.reduce_sub_computation | reduce | bytes 786434
  153.5 9.6 %all-to-all-start.3 = ((bf16[16,2,6144]{2,1,0:T(2,128)(2,1)}), bf16[16,2,6144]{2,1,0:T(2,128)(2,1)S(1)}, u32[]{:S(2)}, u32[]{:S(2)}) async-start(bf16[16,2,6144]{2,1,0:T(2,128)(2,1)} %reshape.298), calls=%async_computation.3 | async-start | bytes 786432 | tf_op jit(solution)/shard_map/all_to_all | solution.py:57
  163.9 11.5 %reduce.27 = bf16[2048,96]{1,0:T(8,128)(2,1)S(1)} reduce(bf16[2048,1,96]{2,1,0:T(2,128)(2,1)S(1)} %bitcast.242, bf16[]{:T(256)} %broadcast.159), dimensions={1}, to_apply=%bitcast.184.reduce_sub_computation | reduce | bytes 786434
  179.6 12.1 %all-to-all-start.8 = ((bf16[16,2,6144]{2,1,0:T(2,128)(2,1)}), bf16[16,2,6144]{2,1,0:T(2,128)(2,1)S(1)}, u32[]{:S(2)}, u32[]{:S(2)}) async-start(bf16[16,2,6144]{2,1,0:T(2,128)(2,1)} %reshape.310), calls=%async_computation.8 | async-start | bytes 786432 | tf_op jit(solution)/shard_map/all_to_all | solution.py:58
  196.6 3.5 collective-permute-start
  201.5 11.5 %reduce.28 = bf16[2048,96]{1,0:T(8,128)(2,1)S(1)} reduce(bf16[2048,1,96]{2,1,0:T(2,128)(2,1)S(1)} %bitcast.234, bf16[]{:T(256)} %broadcast.159), dimensions={1}, to_apply=%bitcast.186.reduce_sub_computation | reduce | bytes 786434
  216.9 12.0 %all-to-all-start.7 = ((bf16[16,2,6144]{2,1,0:T(2,128)(2,1)}), bf16[16,2,6144]{2,1,0:T(2,128)(2,1)S(1)}, u32[]{:S(2)}, u32[]{:S(2)}) async-start(bf16[16,2,6144]{2,1,0:T(2,128)(2,1)} %reshape.312), calls=%async_computation.7 | async-start | bytes 786432 | tf_op jit(solution)/shard_map/all_to_all | solution.py:55
  243.6 4.8 %all-to-all-done.7 = bf16[16,2,6144]{2,1,0:T(2,128)(2,1)S(1)} async-done(((bf16[16,2,6144]{2,1,0:T(2,128)(2,1)}), bf16[16,2,6144]{2,1,0:T(2,128)(2,1)S(1)}, u32[]{:S(2)}, u32[]{:S(2)}) %all-to-all-start.7) | async-done | bytes 393248 | tf_op jit(solution)/shard_map/all_to_all | solution.py:55
  256.1 22.4 %collective-permute-done.3 = bf16[2,16,128,128]{3,2,1,0:T(8,128)(2,1)} collective-permute-done((bf16[2,16,128,128]{3,2,1,0:T(8,128)(2,1)}, bf16[2,16,128,128]{3,2,1,0:T(8,128)(2,1)}, u32[]{:S(2)}, u32[]{:S(2)}) %collective-permute-start.3) | collective-permute-done | bytes 1048608 | tf_op jit(solution)/shard_map/ppermute | solution.py:16
  316.0 3.6 collective-permute-start.5
  320.8 3.9 collective-permute-start.4
  325.9 11.2 %all-to-all-start.6 = ((bf16[16,32,128]{2,1,0:T(8,128)(2,1)}), bf16[16,32,128]{2,1,0:T(8,128)(2,1)S(1)}, u32[]{:S(2)}, u32[]{:S(2)}) async-start(bf16[16,32,128]{2,1,0:T(8,128)(2,1)} %fusion.30), calls=%async_computation.6 | async-start | bytes 262144 | tf_op jit(solution)/shard_map/all_to_all | solution.py:178
  340.5 18.9 %collective-permute-done.4 = bf16[2,16,128,128]{3,2,1,0:T(8,128)(2,1)} collective-permute-done((bf16[2,16,128,128]{3,2,1,0:T(8,128)(2,1)}, bf16[2,16,128,128]{3,2,1,0:T(8,128)(2,1)}, u32[]{:S(2)}, u32[]{:S(2)}) %collective-permute-start.4) | collective-permute-done | bytes 1048608 | tf_op jit(solution)/shard_map/ppermute | solution.py:16
  363.2 11.0 %all-to-all-start.9 = ((bf16[16,32,128]{2,1,0:T(8,128)(2,1)}), bf16[16,32,128]{2,1,0:T(8,128)(2,1)S(1)}, u32[]{:S(2)}, u32[]{:S(2)}) async-start(bf16[16,32,128]{2,1,0:T(8,128)(2,1)} %get-tuple-element.24), calls=%async_computation.9 | async-start | bytes 262144 | tf_op jit(solution)/shard_map/all_to_all | solution.py:181
  375.5 12.2 %all-to-all-done.9 = bf16[16,32,128]{2,1,0:T(8,128)(2,1)S(1)} async-done(((bf16[16,32,128]{2,1,0:T(8,128)(2,1)}), bf16[16,32,128]{2,1,0:T(8,128)(2,1)S(1)}, u32[]{:S(2)}, u32[]{:S(2)}) %all-to-all-start.9) | async-done | bytes 131104 | tf_op jit(solution)/shard_map/all_to_all | solution.py:181
  392.4 12.5 %all-to-all-done.10 = bf16[16,32,128]{2,1,0:T(8,128)(2,1)S(1)} async-done(((bf16[16,32,128]{2,1,0:T(8,128)(2,1)}), bf16[16,32,128]{2,1,0:T(8,128)(2,1)S(1)}, u32[]{:S(2)}, u32[]{:S(2)}) %all-to-all-start.10) | async-done | bytes 131104 | tf_op jit(solution)/shard_map/all_to_all | solution.py:184
  404.9 3.6 all-to-all-start.11
  409.1 15.6 %all-to-all-done.11 = bf16[16,96,128]{2,1,0:T(8,128)(2,1)S(1)} async-done(((bf16[16,96,128]{2,1,0:T(8,128)(2,1)}), bf16[16,96,128]{2,1,0:T(8,128)(2,1)S(1)}, u32[]{:S(2)}, u32[]{:S(2)}) %all-to-all-start.11) | async-done | bytes 393248 | tf_op jit(solution)/shard_map/all_to_all | solution.py:187
  424.7 3.6 all-to-all-start.12
  429.6 15.1 %all-to-all-done.12 = bf16[16,96,128]{2,1,0:T(8,128)(2,1)S(1)} async-done(((bf16[16,96,128]{2,1,0:T(8,128)(2,1)}), bf16[16,96,128]{2,1,0:T(8,128)(2,1)S(1)}, u32[]{:S(2)}, u32[]{:S(2)}) %all-to-all-start.12) | async-done | bytes 393248 | tf_op jit(solution)/shard_map/all_to_all | solution.py:190
  444.7 3.6 all-to-all-start.13
  449.8 14.7 %all-to-all-done.13 = bf16[16,96,128]{2,1,0:T(8,128)(2,1)S(1)} async-done(((bf16[16,96,128]{2,1,0:T(8,128)(2,1)}), bf16[16,96,128]{2,1,0:T(8,128)(2,1)S(1)}, u32[]{:S(2)}, u32[]{:S(2)}) %all-to-all-start.13) | async-done | bytes 393248 | tf_op jit(solution)/shard_map/all_to_all | solution.py:193
  (172 shorter events, 112.0 us)
Async XLA Ops:
  0.6 199.5 %copy-start = (s32[16,32]{1,0:T(8,128)S(1)}, s32[16,32]{1,0:T(8,128)}, u32[]{:S(2)}) copy-start(s32[16,32]{1,0:T(8,128)} %param.22) | copy-start | bytes 6148
  0.6 31.4 %copy-start.12 = (bf16[1,32,2048]{2,1,0:T(8,128)(2,1)S(1)}, bf16[1,32,2048]{2,1,0:T(8,128)(2,1)}, u32[]{:S(2)}) copy-start(bf16[1,32,2048]{2,1,0:T(8,128)(2,1)} %param.16) | copy-start | bytes 393220
  16.0 41.8 %copy-start.13 = (bf16[1,32,2048]{2,1,0:T(8,128)(2,1)S(1)}, bf16[1,32,2048]{2,1,0:T(8,128)(2,1)}, u32[]{:S(2)}) copy-start(bf16[1,32,2048]{2,1,0:T(8,128)(2,1)} %param.14) | copy-start | bytes 393220
  16.0 29.7 %all-to-all-start = ((bf16[16,2,2048]{2,1,0:T(2,128)(2,1)}), bf16[16,2,2048]{2,1,0:T(2,128)(2,1)S(1)}, u32[]{:S(2)}, u32[]{:S(2)}) async-start(bf16[16,2,2048]{2,1,0:T(2,128)(2,1)} %reshape.304), calls=%async_computation | async-start | bytes 262144 | tf_op jit(solution)/shard_map/all_to_all | solution.py:52
  45.6 38.2 %copy-start.14 = (bf16[1,32,2048]{2,1,0:T(8,128)(2,1)S(1)}, bf16[1,32,2048]{2,1,0:T(8,128)(2,1)}, u32[]{:S(2)}) copy-start(bf16[1,32,2048]{2,1,0:T(8,128)(2,1)} %param.17) | copy-start | bytes 393220
  45.6 25.8 %all-to-all-start.1 = ((bf16[16,2,2048]{2,1,0:T(2,128)(2,1)}), bf16[16,2,2048]{2,1,0:T(2,128)(2,1)S(1)}, u32[]{:S(2)}, u32[]{:S(2)}) async-start(bf16[16,2,2048]{2,1,0:T(2,128)(2,1)} %reshape.302), calls=%async_computation.1 | async-start | bytes 262144 | tf_op jit(solution)/shard_map/all_to_all | solution.py:53
  71.3 38.6 %copy-start.6 = (bf16[1,96,2048]{2,1,0:T(8,128)(2,1)S(1)}, bf16[1,96,2048]{2,1,0:T(8,128)(2,1)}, u32[]{:S(2)}) copy-start(bf16[1,96,2048]{2,1,0:T(8,128)(2,1)} %param.19) | copy-start | bytes 1179652
  71.4 26.0 %all-to-all-start.4 = ((bf16[16,2,2048]{2,1,0:T(2,128)(2,1)}), bf16[16,2,2048]{2,1,0:T(2,128)(2,1)S(1)}, u32[]{:S(2)}, u32[]{:S(2)}) async-start(bf16[16,2,2048]{2,1,0:T(2,128)(2,1)} %reshape.308), calls=%async_computation.4 | async-start | bytes 262144 | tf_op jit(solution)/shard_map/all_to_all | solution.py:51
  97.4 26.5 %all-to-all-start.5 = ((bf16[16,2,2048]{2,1,0:T(2,128)(2,1)}), bf16[16,2,2048]{2,1,0:T(2,128)(2,1)S(1)}, u32[]{:S(2)}, u32[]{:S(2)}) async-start(bf16[16,2,2048]{2,1,0:T(2,128)(2,1)} %reshape.306), calls=%async_computation.5 | async-start | bytes 262144 | tf_op jit(solution)/shard_map/all_to_all | solution.py:54
  110.7 26.2 %copy-start.7 = (bf16[1,96,2048]{2,1,0:T(8,128)(2,1)S(1)}, bf16[1,96,2048]{2,1,0:T(8,128)(2,1)}, u32[]{:S(2)}) copy-start(bf16[1,96,2048]{2,1,0:T(8,128)(2,1)} %param.20) | copy-start | bytes 1179652
  124.5 29.0 %all-to-all-start.2 = ((bf16[16,2,6144]{2,1,0:T(2,128)(2,1)}), bf16[16,2,6144]{2,1,0:T(2,128)(2,1)S(1)}, u32[]{:S(2)}, u32[]{:S(2)}) async-start(bf16[16,2,6144]{2,1,0:T(2,128)(2,1)} %reshape.300), calls=%async_computation.2 | async-start | bytes 786432 | tf_op jit(solution)/shard_map/all_to_all | solution.py:56
  137.6 25.5 %copy-start.8 = (bf16[1,96,2048]{2,1,0:T(8,128)(2,1)S(1)}, bf16[1,96,2048]{2,1,0:T(8,128)(2,1)}, u32[]{:S(2)}) copy-start(bf16[1,96,2048]{2,1,0:T(8,128)(2,1)} %param.21) | copy-start | bytes 1179652
  153.5 26.1 %all-to-all-start.3 = ((bf16[16,2,6144]{2,1,0:T(2,128)(2,1)}), bf16[16,2,6144]{2,1,0:T(2,128)(2,1)S(1)}, u32[]{:S(2)}, u32[]{:S(2)}) async-start(bf16[16,2,6144]{2,1,0:T(2,128)(2,1)} %reshape.298), calls=%async_computation.3 | async-start | bytes 786432 | tf_op jit(solution)/shard_map/all_to_all | solution.py:57
  179.6 37.3 %all-to-all-start.8 = ((bf16[16,2,6144]{2,1,0:T(2,128)(2,1)}), bf16[16,2,6144]{2,1,0:T(2,128)(2,1)S(1)}, u32[]{:S(2)}, u32[]{:S(2)}) async-start(bf16[16,2,6144]{2,1,0:T(2,128)(2,1)} %reshape.310), calls=%async_computation.8 | async-start | bytes 786432 | tf_op jit(solution)/shard_map/all_to_all | solution.py:58
  196.6 53.5 %collective-permute-start = (bf16[2,16,128,128]{3,2,1,0:T(8,128)(2,1)}, bf16[2,16,128,128]{3,2,1,0:T(8,128)(2,1)}, u32[]{:S(2)}, u32[]{:S(2)}) collective-permute-start(bf16[2,16,128,128]{3,2,1,0:T(8,128)(2,1)} %maximum_maximum_fusion), channel_id=1, source_target_pairs={{0,2},{1,3},{2,4},{3,5},{4,6},{5,7},{6,8},{7,9},{8,10},{9,11},{10,... | collective-permute-start | bytes 3145736 | tf_op jit(solution)/shard_map/ppermute | solution.py:16
  214.6 24.8 %copy-start.5 = (bf16[16,2,2048]{2,1,0:T(2,128)(2,1)S(1)}, bf16[16,2,2048]{2,1,0:T(2,128)(2,1)}, u32[]{:S(2)}) copy-start(bf16[16,2,2048]{2,1,0:T(2,128)(2,1)} %copy-done.4) | copy-start | bytes 393220
  215.0 36.3 %collective-permute-start.1 = (bf16[2,16,128,128]{3,2,1,0:T(8,128)(2,1)}, bf16[2,16,128,128]{3,2,1,0:T(8,128)(2,1)}, u32[]{:S(2)}, u32[]{:S(2)}) collective-permute-start(bf16[2,16,128,128]{3,2,1,0:T(8,128)(2,1)} %maximum_maximum_fusion), channel_id=1, source_target_pairs={{0,1},{1,2},{2,3},{3,4},{4,5},{5,6},{6,7},{7,8},{8,9},{9,10},{10,1... | collective-permute-start | bytes 3145736 | tf_op jit(solution)/shard_map/ppermute | solution.py:16
  216.9 31.4 %all-to-all-start.7 = ((bf16[16,2,6144]{2,1,0:T(2,128)(2,1)}), bf16[16,2,6144]{2,1,0:T(2,128)(2,1)S(1)}, u32[]{:S(2)}, u32[]{:S(2)}) async-start(bf16[16,2,6144]{2,1,0:T(2,128)(2,1)} %reshape.312), calls=%async_computation.7 | async-start | bytes 786432 | tf_op jit(solution)/shard_map/all_to_all | solution.py:55
  229.0 25.8 %collective-permute-start.2 = (bf16[2,16,128,128]{3,2,1,0:T(8,128)(2,1)}, bf16[2,16,128,128]{3,2,1,0:T(8,128)(2,1)}, u32[]{:S(2)}, u32[]{:S(2)}) collective-permute-start(bf16[2,16,128,128]{3,2,1,0:T(8,128)(2,1)} %maximum_maximum_fusion), channel_id=1, source_target_pairs={{1,0},{2,1},{3,2},{4,3},{5,4},{6,5},{7,6},{8,7},{9,8},{10,9},{11,1... | collective-permute-start | bytes 3145736 | tf_op jit(solution)/shard_map/ppermute | solution.py:16
  232.5 46.0 %collective-permute-start.3 = (bf16[2,16,128,128]{3,2,1,0:T(8,128)(2,1)}, bf16[2,16,128,128]{3,2,1,0:T(8,128)(2,1)}, u32[]{:S(2)}, u32[]{:S(2)}) collective-permute-start(bf16[2,16,128,128]{3,2,1,0:T(8,128)(2,1)} %maximum_maximum_fusion), channel_id=1, source_target_pairs={{2,0},{3,1},{4,2},{5,3},{6,4},{7,5},{8,6},{9,7},{10,8},{11,9},{12,... | collective-permute-start | bytes 3145736 | tf_op jit(solution)/shard_map/ppermute | solution.py:16
  252.7 28.9 %copy-start.16 = (pred[16,480]{1,0:T(8,128)(4,1)S(1)}, pred[16,480]{1,0:T(8,128)(4,1)}, u32[]{:S(2)}) copy-start(pred[16,480]{1,0:T(8,128)(4,1)} %concatenate.30) | copy-start | bytes 23044
  310.9 28.4 %collective-permute-start.7 = (bf16[2,16,128,128]{3,2,1,0:T(8,128)(2,1)}, bf16[2,16,128,128]{3,2,1,0:T(8,128)(2,1)}, u32[]{:S(2)}, u32[]{:S(2)}) collective-permute-start(bf16[2,16,128,128]{3,2,1,0:T(8,128)(2,1)} %fusion.33), channel_id=1, source_target_pairs={{0,2},{1,3},{2,4},{3,5},{4,6},{5,7},{6,8},{7,9},{8,10},{9,11},{10,... | collective-permute-start | bytes 3145736 | tf_op jit(solution)/shard_map/ppermute | solution.py:16
  312.9 26.4 %collective-permute-start.6 = (bf16[2,16,128,128]{3,2,1,0:T(8,128)(2,1)S(1)}, bf16[2,16,128,128]{3,2,1,0:T(8,128)(2,1)}, u32[]{:S(2)}, u32[]{:S(2)}) collective-permute-start(bf16[2,16,128,128]{3,2,1,0:T(8,128)(2,1)S(1)} %pad_maximum_fusion.3), channel_id=1, source_target_pairs={{0,1},{1,2},{2,3},{3,4},{4,5},{5,6},{6,7},{7,8},{8,9},{9,10},{10,1... | collective-permute-start | bytes 3145736 | tf_op jit(solution)/shard_map/ppermute | solution.py:16
  316.0 24.6 %collective-permute-start.5 = (bf16[2,16,128,128]{3,2,1,0:T(8,128)(2,1)}, bf16[2,16,128,128]{3,2,1,0:T(8,128)(2,1)}, u32[]{:S(2)}, u32[]{:S(2)}) collective-permute-start(bf16[2,16,128,128]{3,2,1,0:T(8,128)(2,1)} %pad_maximum_fusion.2), channel_id=1, source_target_pairs={{1,0},{2,1},{3,2},{4,3},{5,4},{6,5},{7,6},{8,7},{9,8},{10,9},{11,1... | collective-permute-start | bytes 3145736 | tf_op jit(solution)/shard_map/ppermute | solution.py:16
  320.8 38.6 %collective-permute-start.4 = (bf16[2,16,128,128]{3,2,1,0:T(8,128)(2,1)}, bf16[2,16,128,128]{3,2,1,0:T(8,128)(2,1)}, u32[]{:S(2)}, u32[]{:S(2)}) collective-permute-start(bf16[2,16,128,128]{3,2,1,0:T(8,128)(2,1)} %pad_maximum_fusion.1), channel_id=1, source_target_pairs={{2,0},{3,1},{4,2},{5,3},{6,4},{7,5},{8,6},{9,7},{10,8},{11,9},{12,... | collective-permute-start | bytes 3145736 | tf_op jit(solution)/shard_map/ppermute | solution.py:16
  325.9 37.2 %all-to-all-start.6 = ((bf16[16,32,128]{2,1,0:T(8,128)(2,1)}), bf16[16,32,128]{2,1,0:T(8,128)(2,1)S(1)}, u32[]{:S(2)}, u32[]{:S(2)}) async-start(bf16[16,32,128]{2,1,0:T(8,128)(2,1)} %fusion.30), calls=%async_computation.6 | async-start | bytes 262144 | tf_op jit(solution)/shard_map/all_to_all | solution.py:178
  363.2 24.5 %all-to-all-start.9 = ((bf16[16,32,128]{2,1,0:T(8,128)(2,1)}), bf16[16,32,128]{2,1,0:T(8,128)(2,1)S(1)}, u32[]{:S(2)}, u32[]{:S(2)}) async-start(bf16[16,32,128]{2,1,0:T(8,128)(2,1)} %get-tuple-element.24), calls=%async_computation.9 | async-start | bytes 262144 | tf_op jit(solution)/shard_map/all_to_all | solution.py:181
  387.7 17.2 %all-to-all-start.10 = ((bf16[16,32,128]{2,1,0:T(8,128)(2,1)}), bf16[16,32,128]{2,1,0:T(8,128)(2,1)S(1)}, u32[]{:S(2)}, u32[]{:S(2)}) async-start(bf16[16,32,128]{2,1,0:T(8,128)(2,1)} %get-tuple-element.23), calls=%async_computation.10 | async-start | bytes 262144 | tf_op jit(solution)/shard_map/all_to_all | solution.py:184
  404.9 19.8 %all-to-all-start.11 = ((bf16[16,96,128]{2,1,0:T(8,128)(2,1)}), bf16[16,96,128]{2,1,0:T(8,128)(2,1)S(1)}, u32[]{:S(2)}, u32[]{:S(2)}) async-start(bf16[16,96,128]{2,1,0:T(8,128)(2,1)} %get-tuple-element.27), calls=%async_computation.11 | async-start | bytes 786432 | tf_op jit(solution)/shard_map/all_to_all | solution.py:187
  424.7 20.0 %all-to-all-start.12 = ((bf16[16,96,128]{2,1,0:T(8,128)(2,1)}), bf16[16,96,128]{2,1,0:T(8,128)(2,1)S(1)}, u32[]{:S(2)}, u32[]{:S(2)}) async-start(bf16[16,96,128]{2,1,0:T(8,128)(2,1)} %get-tuple-element.26), calls=%async_computation.12 | async-start | bytes 786432 | tf_op jit(solution)/shard_map/all_to_all | solution.py:190
  428.2 37.0 %copy-start.1 = (s32[16,32]{1,0:T(8,128)S(1)}, s32[16,32]{1,0:T(8,128)}, u32[]{:S(2)}) copy-start(s32[16,32]{1,0:T(8,128)} %param.22) | copy-start | bytes 6148
  444.7 19.8 %all-to-all-start.13 = ((bf16[16,96,128]{2,1,0:T(8,128)(2,1)}), bf16[16,96,128]{2,1,0:T(8,128)(2,1)S(1)}, u32[]{:S(2)}, u32[]{:S(2)}) async-start(bf16[16,96,128]{2,1,0:T(8,128)(2,1)} %get-tuple-element.25), calls=%async_computation.13 | async-start | bytes 786432 | tf_op jit(solution)/shard_map/all_to_all | solution.py:193
  (13 other events, 52.6 us)
where the time goes:
time: 472 us; the launch traced here: 465 us
  starting transfers between devices  159 us (34%)
  waiting for transfers between devices  123 us (26%)
  other arithmetic  106 us (22%)
  local copies, waits for them, and re-layouts  56.1 us (12%)
  matrix products  20 us (4%)
    unnamed x10, other arithmetic  93.3 us
    ppermute x8, waiting for transfers between devices, from_behind(): return lax.ppermute(x, axis, pairs)  44.7 us
    unnamed x81, local copies, waits for them, and re-layouts  37.1 us
    ppermute x8, starting transfers between devices, from_behind(): return lax.ppermute(x, axis, pairs)  23.2 us
    all_to_all x1, starting transfers between devices, shards(): lax.all_to_all(vid_k, 'frame', split_axis=2, concat_axis=0, tiled=True)  16.1 us
    all_to_all x1, waiting for transfers between devices, shards(): lax.all_to_all(grad_aq.astype(jnp.bfloat16), 'frame', split_axis=0, conca...  15.6 us
    all_to_all x1, waiting for transfers between devices, shards(): lax.all_to_all(grad_ak.astype(jnp.bfloat16), 'frame', split_axis=0, conca...  15.1 us
    all_to_all x1, waiting for transfers between devices, shards(): lax.all_to_all(grad_av.astype(jnp.bfloat16), 'frame', split_axis=0, conca...  14.7 us
  transfers between devices with their start and end apart: 22, of which 14 were waited for; matrix products, arithmetic and copies ran while one was open for 29% of the time, Pallas kernels for 0%

commit v1 on v0

v1 whole, which is shorter than its diff:
```python
import functools

import jax
import jax.numpy as jnp
from jax import lax
from jax.experimental import pallas as pl
from jax.experimental.pallas import tpu as pltpu
from jax.sharding import PartitionSpec as P

HD = 128
BAND = 2
NEG_BIG = -1e30
FACTOR = HD ** (-0.5)
HEADS_PER_STEP = 2
INTERPRET = False


def attend(queries, keys, values, grads, mask):
    scores = (
        lax.dot_general(
            queries, keys, (((1,), (1,)), ((), ())), preferred_element_type=jnp.float32
        )
        * FACTOR
    )
    scores = jnp.where(mask, scores, NEG_BIG)
    largest = jnp.max(scores, axis=-1, keepdims=True)
    exponent = jnp.exp(scores - largest)
    weights = exponent * (1.0 / jnp.sum(exponent, axis=-1, keepdims=True))
    half = weights.astype(jnp.bfloat16)
    grad_weights = lax.dot_general(
        grads, values, (((1,), (1,)), ((), ())), preferred_element_type=jnp.float32
    )
    delta = jnp.sum(half.astype(jnp.float32) * grad_weights, axis=-1, keepdims=True)
    grad_scores = (weights * (grad_weights - delta)).astype(jnp.bfloat16)
    grad_query = (
        lax.dot_general(
            grad_scores, keys, (((1,), (0,)), ((), ())), preferred_element_type=jnp.float32
        )
        * FACTOR
    )
    key_terms = (
        lax.dot_general(
            grad_scores, queries, (((0,), (0,)), ((), ())), preferred_element_type=jnp.float32
        )
        * FACTOR
    )
    value_terms = lax.dot_general(
        half, grads, (((0,), (0,)), ((), ())), preferred_element_type=jnp.float32
    )
    return grad_query, key_terms, value_terms


def video_kernel(group, mask_ref, q_ref, g_ref, before, here, after, dq_ref, tb, th, ta):
    rows = q_ref.shape[0]
    part = before.shape[0] // 2
    late = (lax.broadcasted_iota(jnp.int32, (rows, 1), 0) // group) % 2
    mask = jnp.where(late == 0, mask_ref[0:1, :], mask_ref[1:2, :]) > 0
    for head in range(q_ref.shape[1] // HD):
        cols = slice(head * HD, (head + 1) * HD)
        keys = jnp.concatenate([ref[:part, cols] for ref in (before, here, after)], axis=0)
        values = jnp.concatenate([ref[part:, cols] for ref in (before, here, after)], axis=0)
        dq, kt, vt = attend(q_ref[:, cols], keys, values, g_ref[:, cols], mask)
        dq_ref[:, cols] = dq.astype(jnp.bfloat16)
        for place, out in enumerate((tb, th, ta)):
            span = slice(place * part, (place + 1) * part)
            out[:part, cols] = kt[span].astype(jnp.bfloat16)
            out[part:, cols] = vt[span].astype(jnp.bfloat16)


def audio_kernel(
    info, mask_ref, q_mine, g_mine, q_other, g_other, before, here, after, dq_ref, tb, th, ta
):
    rows = q_mine.shape[0]
    part = before.shape[0] // 2
    keys_total = 3 * part
    slot = lax.broadcasted_iota(jnp.int32, (rows, 1), 0)
    live_mine = slot < info[1]
    live_other = slot < info[2]
    mask = jnp.concatenate(
        [
            jnp.broadcast_to(mask_ref[0:1, :], (rows, keys_total)),
            jnp.broadcast_to(mask_ref[1:2, :], (rows, keys_total)),
        ],
        axis=0,
    )
    mask = mask > 0
    for head in range(q_mine.shape[1] // HD):
        cols = slice(head * HD, (head + 1) * HD)
        queries = jnp.concatenate([q_mine[:, cols], q_other[:, cols]], axis=0)
        zero = jnp.zeros((), jnp.bfloat16)
        grads = jnp.concatenate(
            [
                jnp.where(live_mine, g_mine[:, cols], zero),
                jnp.where(live_other, g_other[:, cols], zero),
            ],
            axis=0,
        )
        keys = jnp.concatenate([ref[:part, cols] for ref in (before, here, after)], axis=0)
        values = jnp.concatenate([ref[part:, cols] for ref in (before, here, after)], axis=0)
        dq, kt, vt = attend(queries, keys, values, grads, mask)
        dq_ref[:, cols] = dq.astype(jnp.bfloat16)
        for place, out in enumerate((tb, th, ta)):
            span = slice(place * part, (place + 1) * part)
            out[:part, cols] = kt[span].astype(jnp.bfloat16)
            out[part:, cols] = vt[span].astype(jnp.bfloat16)


def cost(rows, keys, width):
    heads = width // HD
    return pl.CostEstimate(
        flops=10 * rows * keys * HD * heads,
        bytes_accessed=2 * width * (4 * rows + 4 * keys),
        transcendentals=rows * keys * heads,
    )


def video_side(mask, video, before, here, after, group):
    width = video.shape[1]
    rows = video.shape[0] // 4
    wide = min(HEADS_PER_STEP * HD, width)
    window = before.shape[0]
    column = lambda h: (0, h)
    kv = pl.BlockSpec((window, wide), column)
    bf = jnp.bfloat16
    return pl.pallas_call(
        functools.partial(video_kernel, group),
        grid=(width // wide,),
        in_specs=[
            pl.BlockSpec(mask.shape, lambda h: (0, 0)),
            pl.BlockSpec((rows, wide), column),
            pl.BlockSpec((rows, wide), lambda h: (3, h)),
            kv,
            kv,
            kv,
        ],
        out_specs=[pl.BlockSpec((rows, wide), column), kv, kv, kv],
        out_shape=[jax.ShapeDtypeStruct((rows, width), bf)]
        + [jax.ShapeDtypeStruct((window, width), bf)] * 3,
        cost_estimate=cost(rows, 3 * window // 2, width),
        name="video_side",
        interpret=INTERPRET,
    )(mask, video, video, before, here, after)


def audio_side(info, mask, aud_q, aud_g, theirs, before, here, after):
    width = theirs.shape[1]
    rows = aud_q.shape[0]
    wide = min(HEADS_PER_STEP * HD, width)
    steps = width // wide
    window = before.shape[0]
    kv = pl.BlockSpec((window, wide), lambda h, info: (0, h))
    mine = pl.BlockSpec((rows, wide), lambda h, info: (0, info[0] * steps + h))
    bf = jnp.bfloat16
    return pl.pallas_call(
        audio_kernel,
        grid_spec=pltpu.PrefetchScalarGridSpec(
            num_scalar_prefetch=1,
            grid=(steps,),
            in_specs=[
                pl.BlockSpec(mask.shape, lambda h, info: (0, 0)),
                mine,
                mine,
                pl.BlockSpec((rows, wide), lambda h, info: (0, h)),
                pl.BlockSpec((rows, wide), lambda h, info: (3, h)),
                kv,
                kv,
                kv,
            ],
            out_specs=[pl.BlockSpec((2 * rows, wide), lambda h, info: (0, h)), kv, kv, kv],
        ),
        out_shape=[jax.ShapeDtypeStruct((2 * rows, width), bf)]
        + [jax.ShapeDtypeStruct((window, width), bf)] * 3,
        cost_estimate=cost(2 * rows, 3 * window // 2, width),
        name="audio_side",
        interpret=INTERPRET,
    )(info, mask, aud_q, aud_g, theirs, theirs, before, here, after)


def shards(vid_q, vid_k, vid_v, vid_dout, aud_q, aud_k, aud_v, aud_dout, aud_len, match):
    frames = lax.axis_size("frame")
    count = lax.axis_size("seq")
    group_here = lax.axis_index("frame")
    block_here = lax.axis_index("seq")
    core = block_here % 2
    base = block_here - core
    video_rows, width = vid_q.shape[1], vid_q.shape[2]
    audio_rows = aud_q.shape[1]
    half = width // 2
    group = 4 * video_rows // frames
    runs = frames // 4
    spreads = frames // runs
    slim = half // spreads
    f32, bf = jnp.float32, jnp.bfloat16

    pairs = [
        [f * count + 2 * c + k for f in range(frames) for k in range(2)]
        for c in range(count // 2)
    ]

    def pair_exchange(x):
        return lax.all_to_all(
            x, ("frame", "seq"), split_axis=0, concat_axis=0, tiled=True, axis_index_groups=pairs
        )

    def exchange(x):
        return lax.all_to_all(x, "frame", split_axis=0, concat_axis=0, tiled=True)

    def shift(x, by):
        return lax.ppermute(
            x, "seq", [(i, i + by) for i in range(count) if 0 <= i + by < count]
        )

    def swap(x):
        return lax.ppermute(x, "seq", [(i, i ^ 1) for i in range(count)])

    order = jnp.arange(frames, dtype=jnp.int32)
    inverse = jnp.sum(
        jnp.where(match[None, :] == order[:, None], order[None, :], 0), axis=1
    ).astype(jnp.int32)

    packed = jnp.concatenate([vid_q[0], vid_k[0], vid_v[0], vid_dout[0]], axis=0)
    packed = packed.reshape(frames, group, 2, half).transpose(0, 2, 1, 3)
    spread = pair_exchange(packed.reshape(2 * frames, group, half))
    spread = jnp.take(spread.reshape(frames, 2 * group, half), inverse, axis=0, mode="clip")
    video = exchange(spread).reshape(frames * 2 * group, half)

    def halves(x):
        low, high = x[0, :, :half], x[0, :, half:]
        return jnp.where(core == 0, low, high), jnp.where(core == 0, high, low)

    own_k, send_k = halves(aud_k)
    own_v, send_v = halves(aud_v)
    send_q = halves(aud_q)[1]
    send_g = halves(aud_dout)[1]
    theirs = swap(jnp.concatenate([send_q, send_k, send_v, send_g], axis=0))
    audio_here = jnp.concatenate(
        [
            own_k,
            theirs[audio_rows : 2 * audio_rows],
            own_v,
            theirs[2 * audio_rows : 3 * audio_rows],
        ],
        axis=0,
    )
    audio_before = shift(audio_here, 2)
    audio_after = shift(audio_here, -2)

    lengths = lax.dynamic_index_in_dim(aud_len, group_here, 0, keepdims=False)
    audio_offsets = jnp.stack(
        [-2 + core, -1 - core, core, 1 - core, 2 + core, 3 - core]
    )
    audio_times = base + audio_offsets
    audio_live = jnp.where(
        (audio_times >= 0) & (audio_times < count),
        jnp.take(lengths, audio_times, mode="clip"),
        0,
    )
    slots = jnp.arange(audio_rows, dtype=jnp.int32)
    live = slots[None, :] < audio_live[:, None]
    late = jnp.arange(2, dtype=jnp.int32)
    near = jnp.abs(late[:, None] - audio_offsets[None, :]) <= BAND
    video_mask = (near[:, :, None] & live[None]).reshape(2, 6 * audio_rows).astype(jnp.int32)

    column = jnp.arange(6 * video_rows, dtype=jnp.int32)
    video_offsets = 2 * (column // (2 * video_rows)) - 2 + (column // group) % 2
    video_times = base + video_offsets
    own_offsets = jnp.stack([core, 1 - core])
    audio_mask = (
        (jnp.abs(own_offsets[:, None] - video_offsets[None, :]) <= BAND)
        & (video_times >= 0)[None]
        & (video_times < count)[None]
    ).astype(jnp.int32)
    info = jnp.stack([core, audio_live[2], audio_live[3]]).astype(jnp.int32)

    block = 2 * video_rows
    video_here = video[block : 3 * block]
    video_before = shift(video_here, 2)
    video_after = shift(video_here, -2)
    grad_vq, audio_tb, audio_th, audio_ta = video_side(
        video_mask, video, audio_before, audio_here, audio_after, group
    )
    grad_aq, video_tb, video_th, video_ta = audio_side(
        info, audio_mask, aud_q[0], aud_dout[0], theirs, video_before, video_here, video_after
    )

    grad_vkv = (
        video_th.astype(f32)
        + shift(video_tb, -2).astype(f32)
        + shift(video_ta, 2).astype(f32)
    ).astype(bf)
    grads = jnp.concatenate([grad_vq, grad_vkv], axis=0)
    grads = grads.reshape(3, runs, 2, group, spreads, slim).transpose(1, 4, 2, 0, 3, 5)
    grads = exchange(grads.reshape(frames, 6 * group, slim))
    grads = jnp.take(grads, match, axis=0, mode="clip")
    grads = pair_exchange(grads.reshape(2 * frames, 3 * group, slim))
    grads = grads.reshape(runs, spreads, 2, 3, group, slim).transpose(3, 0, 4, 2, 1, 5)
    grads = grads.reshape(3, video_rows, width)

    grad_akv = (
        audio_th.astype(f32)
        + shift(audio_tb, -2).astype(f32)
        + shift(audio_ta, 2).astype(f32)
    ).astype(bf)
    mine = (
        grad_aq[:audio_rows],
        grad_akv[:audio_rows],
        grad_akv[2 * audio_rows : 3 * audio_rows],
    )
    back = swap(
        jnp.concatenate(
            [
                grad_aq[audio_rows:],
                grad_akv[audio_rows : 2 * audio_rows],
                grad_akv[3 * audio_rows :],
            ],
            axis=0,
        )
    )

    def whole(own, other):
        return jnp.where(
            core == 0,
            jnp.concatenate([own, other], axis=1),
            jnp.concatenate([other, own], axis=1),
        )[None]

    outs = [
        whole(mine[j], back[j * audio_rows : (j + 1) * audio_rows]) for j in range(3)
    ]
    return (grads[0][None], grads[1][None], grads[2][None], outs[0], outs[1], outs[2])


def solution(mesh):
    tokens = P("frame", "seq", None)
    return jax.shard_map(
        shards,
        mesh=mesh,
        in_specs=(tokens,) * 8 + (P(), P()),
        out_specs=(tokens,) * 6,
        check_vma=False,
    )
```

time: 472 us -> 177 us (0.38); the launches traced: 465 us -> 176 us
  other arithmetic: 106 us -> 7.62 us
  starting transfers between devices: 159 us -> 64.8 us
  local copies, waits for them, and re-layouts: 56.1 us -> 10.2 us
  waiting for transfers between devices: 123 us -> 77.2 us
  matrix products: 20 us -> 0 us
  Pallas kernels: 0 us -> 14.7 us
    all_to_all x14 -> x4, starting transfers between devices: 136 us -> 35.6 us  [the longest x2 20.1 us: pair_exchange(): lax.all_to_all(x, ('frame', 'seq'), split_axis=0, concat_axis=0, tiled=Tr...]
    unnamed x10 -> x0, other arithmetic: 93.3 us -> none
    unnamed x81 -> x36, local copies, waits for them, and re-layouts: 37.1 us -> 1.77 us
    ppermute x8 -> x10, waiting for transfers between devices: 44.7 us -> 14.6 us  [the longest x8 14.6 us: shift(): lax.ppermute(x, 'seq', [(i, i + by) for i in range(count) if 0 <= i + by...]
    dot_general x11 -> x0, matrix products: 17.1 us -> none  [the longest x2 4.74 us: query_side(): jnp.einsum('fhqk,fhkd->fhqd', weights_half, val_rows, preferred_element_t...]
    all_to_all x14 -> x4, waiting for transfers between devices: 77.9 us -> 62.6 us  [the longest x2 34 us: pair_exchange(): lax.all_to_all(x, ('frame', 'seq'), split_axis=0, concat_axis=0, tiled=Tr...]
    pallas_call x0 -> x2, Pallas kernels: none -> 14.7 us  [the longest x1 7.47 us: audio_side(): pl.pallas_call(audio_kernel, grid_spec=pltpu.PrefetchScalarGridSpec(num_s...]
    all_to_all x14 -> x0, local copies, waits for them, and re-layouts: 8.57 us -> none  [the longest x1 1.64 us: shards(): lax.all_to_all(vid_dout, 'frame', split_axis=2, concat_axis=0, tiled=True)]
  transfers between devices with their start and end apart: 22 -> 14, of which waited for: 14 -> 8; matrix products, arithmetic and copies ran while one was open for 29% -> 6% of each run, Pallas kernels for 0% -> 8%
where the time goes in v1:
time: 177 us; the launch traced here: 176 us
  waiting for transfers between devices  77.2 us (44%)
  starting transfers between devices  64.8 us (37%)
  Pallas kernels  14.7 us (8%)
  local copies, waits for them, and re-layouts  10.2 us (6%)
  other arithmetic  7.62 us (4%)
    all_to_all x2, waiting for transfers between devices, pair_exchange(): lax.all_to_all(x, ('frame', 'seq'), split_axis=0, concat_axis=0, tiled=Tr...  34 us
    all_to_all x2, waiting for transfers between devices, exchange(): return lax.all_to_all(x, 'frame', split_axis=0, concat_axis=0, tiled=True)  28.6 us
    ppermute x8, starting transfers between devices, shift(): lax.ppermute(x, 'seq', [(i, i + by) for i in range(count) if 0 <= i + by...  25.2 us
    all_to_all x2, starting transfers between devices, pair_exchange(): lax.all_to_all(x, ('frame', 'seq'), split_axis=0, concat_axis=0, tiled=Tr...  20.1 us
    all_to_all x2, starting transfers between devices, exchange(): return lax.all_to_all(x, 'frame', split_axis=0, concat_axis=0, tiled=True)  15.5 us
    ppermute x8, waiting for transfers between devices, shift(): lax.ppermute(x, 'seq', [(i, i + by) for i in range(count) if 0 <= i + by...  14.6 us
    pallas_call x1, Pallas kernels, audio_side(): pl.pallas_call(audio_kernel, grid_spec=pltpu.PrefetchScalarGridSpec(num_s...  7.47 us
    pallas_call x1, Pallas kernels, video_side(): pl.pallas_call(functools.partial(video_kernel, group), grid=(width // wid...  7.27 us
  transfers between devices with their start and end apart: 14, of which 8 were waited for; matrix products, arithmetic and copies ran while one was open for 6% of the time, Pallas kernels for 8%

profile of v1, /device:TPU:6, one launch (start us, length us, event | category | flops | bytes accessed | tf_op | source)
XLA Modules:
  0.0 175.7 jit_solution(14695424492313696583)
XLA Ops:
  0.7 1.3 select_bitcast_fusion
  2.3 2.1 %collective-permute-start = (bf16[384,1024]{1,0:T(8,128)(2,1)S(1)}, bf16[384,1024]{1,0:T(8,128)(2,1)S(1)}, u32[]{:S(2)}, u32[]{:S(2)}) collective-permute-start(bf16[384,1024]{1,0:T(8,128)(2,1)S(1)} %pad_maximum_fusion), channel_id=1, source_target_pairs={{0,1},{1,0},{2,3},{3,2},{4,5},{5,4},{6,7},{7,6},{8,9},{9,8},{10,11... | collective-permute-start | bytes 2359304 | tf_op jit(solution)/shard_map/ppermute | solution.py:214
  5.2 16.2 %all-to-all-start = ((bf16[32,8,1024]{2,1,0:T(8,128)(2,1)}), bf16[32,8,1024]{2,1,0:T(8,128)(2,1)S(1)}, u32[]{:S(2)}, u32[]{:S(2)}) async-start(bf16[32,8,1024]{2,1,0:T(8,128)(2,1)} %bitcast.20), calls=%async_computation | async-start | bytes 1048576 | tf_op jit(solution)/shard_map/all_to_all | solution.py:201
  22.7 18.8 %all-to-all-done = bf16[32,8,1024]{2,1,0:T(8,128)(2,1)S(1)} async-done(((bf16[32,8,1024]{2,1,0:T(8,128)(2,1)}), bf16[32,8,1024]{2,1,0:T(8,128)(2,1)S(1)}, u32[]{:S(2)}, u32[]{:S(2)}) %all-to-all-start) | async-done | bytes 524320 | tf_op jit(solution)/shard_map/all_to_all | solution.py:201
  41.5 1.4 gather_fusion.1
  42.9 4.6 %all-to-all-start.1 = ((bf16[16,16,1024]{2,1,0:T(8,128)(2,1)}), bf16[16,16,1024]{2,1,0:T(8,128)(2,1)S(1)}, u32[]{:S(2)}, u32[]{:S(2)}) async-start(bf16[16,16,1024]{2,1,0:T(8,128)(2,1)} %gather_fusion.1), calls=%async_computation.1 | async-start | bytes 1048576 | tf_op jit(solution)/shard_map/all_to_all | solution.py:206
  47.6 3.3 %collective-permute-start.1 = (bf16[384,1024]{1,0:T(8,128)(2,1)S(1)}, bf16[384,1024]{1,0:T(8,128)(2,1)S(1)}, u32[]{:S(2)}, u32[]{:S(2)}) collective-permute-start(bf16[384,1024]{1,0:T(8,128)(2,1)S(1)} %pad_maximum_fusion.1.here), channel_id=1, source_target_pairs={{0,2},{1,3},{2,4},{3,5},{4,6},{5,7},{6,8},{7,9},{8,10},{9,11},{10,... | collective-permute-start | bytes 2359304 | tf_op jit(solution)/shard_map/ppermute | solution.py:209
  50.9 2.5 %collective-permute-start.2 = (bf16[384,1024]{1,0:T(8,128)(2,1)S(1)}, bf16[384,1024]{1,0:T(8,128)(2,1)S(1)}, u32[]{:S(2)}, u32[]{:S(2)}) collective-permute-start(bf16[384,1024]{1,0:T(8,128)(2,1)S(1)} %pad_maximum_fusion.1.here), channel_id=1, source_target_pairs={{2,0},{3,1},{4,2},{5,3},{6,4},{7,5},{8,6},{9,7},{10,8},{11,9},{12,... | collective-permute-start | bytes 2359304 | tf_op jit(solution)/shard_map/ppermute | solution.py:209
  54.3 15.0 %all-to-all-done.1 = bf16[16,16,1024]{2,1,0:T(8,128)(2,1)S(1)} async-done(((bf16[16,16,1024]{2,1,0:T(8,128)(2,1)}), bf16[16,16,1024]{2,1,0:T(8,128)(2,1)S(1)}, u32[]{:S(2)}, u32[]{:S(2)}) %all-to-all-start.1) | async-done | bytes 524320 | tf_op jit(solution)/shard_map/all_to_all | solution.py:206
  69.4 3.3 %collective-permute-start.3 = (bf16[128,1024]{1,0:T(8,128)(2,1)S(1)}, bf16[128,1024]{1,0:T(8,128)(2,1)S(1)}, u32[]{:S(2)}, u32[]{:S(2)}) collective-permute-start(bf16[128,1024]{1,0:T(8,128)(2,1)S(1)} %bitcast.69), channel_id=1, source_target_pairs={{0,2},{1,3},{2,4},{3,5},{4,6},{5,7},{6,8},{7,9},{8,10},{9,11},{10,... | collective-permute-start | bytes 786440 | tf_op jit(solution)/shard_map/ppermute | solution.py:209
  72.7 2.5 %collective-permute-start.4 = (bf16[128,1024]{1,0:T(8,128)(2,1)S(1)}, bf16[128,1024]{1,0:T(8,128)(2,1)}, u32[]{:S(2)}, u32[]{:S(2)}) collective-permute-start(bf16[128,1024]{1,0:T(8,128)(2,1)S(1)} %bitcast.70), channel_id=1, source_target_pairs={{2,0},{3,1},{4,2},{5,3},{6,4},{7,5},{8,6},{9,7},{10,8},{11,9},{12,... | collective-permute-start | bytes 786440 | tf_op jit(solution)/shard_map/ppermute | solution.py:209
  75.2 3.8 %collective-permute-done.1.before = bf16[384,1024]{1,0:T(8,128)(2,1)S(1)} collective-permute-done((bf16[384,1024]{1,0:T(8,128)(2,1)S(1)}, bf16[384,1024]{1,0:T(8,128)(2,1)S(1)}, u32[]{:S(2)}, u32[]{:S(2)}) %collective-permute-start.1) | collective-permute-done | bytes 786464 | tf_op jit(solution)/shard_map/ppermute | solution.py:209
  79.1 3.2 %collective-permute-done.2.after = bf16[384,1024]{1,0:T(8,128)(2,1)S(1)} collective-permute-done((bf16[384,1024]{1,0:T(8,128)(2,1)S(1)}, bf16[384,1024]{1,0:T(8,128)(2,1)S(1)}, u32[]{:S(2)}, u32[]{:S(2)}) %collective-permute-start.2) | collective-permute-done | bytes 786464 | tf_op jit(solution)/shard_map/ppermute | solution.py:209
  82.3 0.9 copy-done.8
  83.2 7.3 %video_side.1 = (bf16[64,1024]{1,0:T(8,128)(2,1)}, bf16[384,1024]{1,0:T(8,128)(2,1)}, bf16[384,1024]{1,0:T(8,128)(2,1)}, bf16[384,1024]{1,0:T(8,128)(2,1)}) custom-call(s32[2,576]{1,0:T(2,128)} %and_convert_fusion.mask_ref, bf16[256,1024]{1,0:T(8,128)(2,1)} %bitcast.62, bf16[256,1024]{1,0:T(8,128)(2,1)} %bitcast.63, bf16[384,1024]{1,0:T(8,128)(2,1)} %copy-done.7, ...), custom_call_target="tpu_custom_call" | custom-call | flops 377487360 | bytes 5242880 | tf_op jit(solution)/shard_map/video_side/pallas_call | solution.py:125
  90.5 3.5 %collective-permute-start.8 = (bf16[384,1024]{1,0:T(8,128)(2,1)}, bf16[384,1024]{1,0:T(8,128)(2,1)S(1)}, u32[]{:S(2)}, u32[]{:S(2)}) collective-permute-start(bf16[384,1024]{1,0:T(8,128)(2,1)} %get-tuple-element.21), channel_id=1, source_target_pairs={{0,2},{1,3},{2,4},{3,5},{4,6},{5,7},{6,8},{7,9},{8,10},{9,11},{10,... | collective-permute-start | bytes 2359304 | tf_op jit(solution)/shard_map/ppermute | solution.py:209
  94.0 2.3 %collective-permute-start.7 = (bf16[384,1024]{1,0:T(8,128)(2,1)}, bf16[384,1024]{1,0:T(8,128)(2,1)S(1)}, u32[]{:S(2)}, u32[]{:S(2)}) collective-permute-start(bf16[384,1024]{1,0:T(8,128)(2,1)} %get-tuple-element.20), channel_id=1, source_target_pairs={{2,0},{3,1},{4,2},{5,3},{6,4},{7,5},{8,6},{9,7},{10,8},{11,9},{12,... | collective-permute-start | bytes 2359304 | tf_op jit(solution)/shard_map/ppermute | solution.py:209
  98.4 7.5 %audio_side.1 = (bf16[192,1024]{1,0:T(8,128)(2,1)}, bf16[128,1024]{1,0:T(8,128)(2,1)}, bf16[128,1024]{1,0:T(8,128)(2,1)}, bf16[128,1024]{1,0:T(8,128)(2,1)}) custom-call(s32[3]{0:T(128)} %pad_add_fusion.info, s32[2,192]{1,0:T(2,128)} %and_convert_fusion.1.mask_ref, bf16[96,2048]{1,0:T(8,128)(2,1)} %bitcast.65, bf16[96,2048]{1,0:T(8,128)(2,1)} %bitcast.66, ...), custom_call_target="tpu_custom_call" | custom-call | flops 377487360 | bytes 3145728 | tf_op jit(solution)/shard_map/audio_side/pallas_call | solution.py:154
  105.9 5.8 %collective-permute-start.6 = (bf16[128,1024]{1,0:T(8,128)(2,1)}, bf16[128,1024]{1,0:T(8,128)(2,1)S(1)}, u32[]{:S(2)}, u32[]{:S(2)}) collective-permute-start(bf16[128,1024]{1,0:T(8,128)(2,1)} %get-tuple-element.17), channel_id=1, source_target_pairs={{0,2},{1,3},{2,4},{3,5},{4,6},{5,7},{6,8},{7,9},{8,10},{9,11},{10,... | collective-permute-start | bytes 786440 | tf_op jit(solution)/shard_map/ppermute | solution.py:209
  111.7 1.9 %collective-permute-start.5 = (bf16[128,1024]{1,0:T(8,128)(2,1)}, bf16[128,1024]{1,0:T(8,128)(2,1)S(1)}, u32[]{:S(2)}, u32[]{:S(2)}) collective-permute-start(bf16[128,1024]{1,0:T(8,128)(2,1)} %get-tuple-element.16), channel_id=1, source_target_pairs={{2,0},{3,1},{4,2},{5,3},{6,4},{7,5},{8,6},{9,7},{10,8},{11,9},{12,... | collective-permute-start | bytes 786440 | tf_op jit(solution)/shard_map/ppermute | solution.py:209
  113.6 1.1 slice_bitcast_fusion.5
  114.7 2.6 %collective-permute-done.6 = bf16[128,1024]{1,0:T(8,128)(2,1)S(1)} collective-permute-done((bf16[128,1024]{1,0:T(8,128)(2,1)}, bf16[128,1024]{1,0:T(8,128)(2,1)S(1)}, u32[]{:S(2)}, u32[]{:S(2)}) %collective-permute-start.6) | collective-permute-done | bytes 262176 | tf_op jit(solution)/shard_map/ppermute | solution.py:209
  117.3 5.0 %collective-permute-done.5 = bf16[128,1024]{1,0:T(8,128)(2,1)S(1)} collective-permute-done((bf16[128,1024]{1,0:T(8,128)(2,1)}, bf16[128,1024]{1,0:T(8,128)(2,1)S(1)}, u32[]{:S(2)}, u32[]{:S(2)}) %collective-permute-start.5) | collective-permute-done | bytes 262176 | tf_op jit(solution)/shard_map/ppermute | solution.py:209
  123.2 10.9 %all-to-all-start.2 = ((bf16[16,48,256]{2,1,0:T(8,128)(2,1)}), bf16[16,48,256]{2,1,0:T(8,128)(2,1)S(1)}, u32[]{:S(2)}, u32[]{:S(2)}) async-start(bf16[16,48,256]{2,1,0:T(8,128)(2,1)} %bitcast.34), calls=%async_computation.2 | async-start | bytes 786432 | tf_op jit(solution)/shard_map/all_to_all | solution.py:206
  134.7 1.9 %collective-permute-start.9 = (bf16[288,1024]{1,0:T(8,128)(2,1)S(1)}, bf16[288,1024]{1,0:T(8,128)(2,1)S(1)}, u32[]{:S(2)}, u32[]{:S(2)}) collective-permute-start(bf16[288,1024]{1,0:T(8,128)(2,1)S(1)} %pad_maximum_fusion.2), channel_id=1, source_target_pairs={{0,1},{1,0},{2,3},{3,2},{4,5},{5,4},{6,7},{7,6},{8,9},{9,8},{10,11... | collective-permute-start | bytes 1769480 | tf_op jit(solution)/shard_map/ppermute | solution.py:214
  136.7 13.6 %all-to-all-done.2 = bf16[16,48,256]{2,1,0:T(8,128)(2,1)S(1)} async-done(((bf16[16,48,256]{2,1,0:T(8,128)(2,1)}), bf16[16,48,256]{2,1,0:T(8,128)(2,1)S(1)}, u32[]{:S(2)}, u32[]{:S(2)}) %all-to-all-start.2) | async-done | bytes 393248 | tf_op jit(solution)/shard_map/all_to_all | solution.py:206
  150.2 1.3 gather_fusion.2
  151.6 3.9 %all-to-all-start.3 = ((bf16[32,24,256]{2,1,0:T(8,128)(2,1)}), bf16[32,24,256]{2,1,0:T(8,128)(2,1)S(1)}, u32[]{:S(2)}, u32[]{:S(2)}) async-start(bf16[32,24,256]{2,1,0:T(8,128)(2,1)} %bitcast.35), calls=%async_computation.3 | async-start | bytes 786432 | tf_op jit(solution)/shard_map/all_to_all | solution.py:201
  155.5 0.8 maximum_select_fusion
  156.4 0.8 maximum_select_fusion.1
  157.2 0.8 maximum_select_fusion.2
  158.1 15.2 %all-to-all-done.3 = bf16[32,24,256]{2,1,0:T(8,128)(2,1)S(1)} async-done(((bf16[32,24,256]{2,1,0:T(8,128)(2,1)}), bf16[32,24,256]{2,1,0:T(8,128)(2,1)S(1)}, u32[]{:S(2)}, u32[]{:S(2)}) %all-to-all-start.3) | async-done | bytes 393248 | tf_op jit(solution)/shard_map/all_to_all | solution.py:201
  (86 shorter events, 9.3 us)
Async XLA Ops:
  0.6 21.2 %copy-start = (s32[16,32]{1,0:T(8,128)S(1)}, s32[16,32]{1,0:T(8,128)}, u32[]{:S(2)}) copy-start(s32[16,32]{1,0:T(8,128)} %param.18) | copy-start | bytes 6148
  0.6 1.4 copy-start.4
  0.7 1.4 copy-start.9
  2.2 2.2 %copy-start.13 = (bf16[1,32,2048]{2,1,0:T(8,128)(2,1)S(1)}, bf16[1,32,2048]{2,1,0:T(8,128)(2,1)}, u32[]{:S(2)}) copy-start(bf16[1,32,2048]{2,1,0:T(8,128)(2,1)} %param.13) | copy-start | bytes 393220
  2.2 2.2 %copy-start.14 = (bf16[1,32,2048]{2,1,0:T(8,128)(2,1)S(1)}, bf16[1,32,2048]{2,1,0:T(8,128)(2,1)}, u32[]{:S(2)}) copy-start(bf16[1,32,2048]{2,1,0:T(8,128)(2,1)} %param.12) | copy-start | bytes 393220
  2.2 2.2 %copy-start.15 = (bf16[1,32,2048]{2,1,0:T(8,128)(2,1)S(1)}, bf16[1,32,2048]{2,1,0:T(8,128)(2,1)}, u32[]{:S(2)}) copy-start(bf16[1,32,2048]{2,1,0:T(8,128)(2,1)} %param.11) | copy-start | bytes 393220
  2.2 2.2 %copy-start.16 = (bf16[1,32,2048]{2,1,0:T(8,128)(2,1)S(1)}, bf16[1,32,2048]{2,1,0:T(8,128)(2,1)}, u32[]{:S(2)}) copy-start(bf16[1,32,2048]{2,1,0:T(8,128)(2,1)} %param.10) | copy-start | bytes 393220
  2.3 20.4 %collective-permute-start = (bf16[384,1024]{1,0:T(8,128)(2,1)S(1)}, bf16[384,1024]{1,0:T(8,128)(2,1)S(1)}, u32[]{:S(2)}, u32[]{:S(2)}) collective-permute-start(bf16[384,1024]{1,0:T(8,128)(2,1)S(1)} %pad_maximum_fusion), channel_id=1, source_target_pairs={{0,1},{1,0},{2,3},{3,2},{4,5},{5,4},{6,7},{7,6},{8,9},{9,8},{10,11... | collective-permute-start | bytes 2359304 | tf_op jit(solution)/shard_map/ppermute | solution.py:214
  5.2 17.3 %copy-start.17 = (s32[16]{0:T(128)S(1)}, s32[16]{0:T(128)}, u32[]{:S(2)}) copy-start(s32[16]{0:T(128)} %param.19) | copy-start | bytes 196
  5.2 36.3 %all-to-all-start = ((bf16[32,8,1024]{2,1,0:T(8,128)(2,1)}), bf16[32,8,1024]{2,1,0:T(8,128)(2,1)S(1)}, u32[]{:S(2)}, u32[]{:S(2)}) async-start(bf16[32,8,1024]{2,1,0:T(8,128)(2,1)} %bitcast.20), calls=%async_computation | async-start | bytes 1048576 | tf_op jit(solution)/shard_map/all_to_all | solution.py:201
  22.7 20.2 %copy-start.2 = (bf16[384,1024]{1,0:T(8,128)(2,1)}, bf16[384,1024]{1,0:T(8,128)(2,1)S(1)}, u32[]{:S(2)}) copy-start(bf16[384,1024]{1,0:T(8,128)(2,1)S(1)} %collective-permute-done.q_other.g_other) | copy-start | bytes 2359300
  42.9 26.4 %all-to-all-start.1 = ((bf16[16,16,1024]{2,1,0:T(8,128)(2,1)}), bf16[16,16,1024]{2,1,0:T(8,128)(2,1)S(1)}, u32[]{:S(2)}, u32[]{:S(2)}) async-start(bf16[16,16,1024]{2,1,0:T(8,128)(2,1)} %gather_fusion.1), calls=%async_computation.1 | async-start | bytes 1048576 | tf_op jit(solution)/shard_map/all_to_all | solution.py:206
  47.6 34.7 %copy-start.3 = (bf16[384,1024]{1,0:T(8,128)(2,1)}, bf16[384,1024]{1,0:T(8,128)(2,1)S(1)}, u32[]{:S(2)}) copy-start(bf16[384,1024]{1,0:T(8,128)(2,1)S(1)} %pad_maximum_fusion.1.here) | copy-start | bytes 2359300
  47.6 31.5 %collective-permute-start.1 = (bf16[384,1024]{1,0:T(8,128)(2,1)S(1)}, bf16[384,1024]{1,0:T(8,128)(2,1)S(1)}, u32[]{:S(2)}, u32[]{:S(2)}) collective-permute-start(bf16[384,1024]{1,0:T(8,128)(2,1)S(1)} %pad_maximum_fusion.1.here), channel_id=1, source_target_pairs={{0,2},{1,3},{2,4},{3,5},{4,6},{5,7},{6,8},{7,9},{8,10},{9,11},{10,... | collective-permute-start | bytes 2359304 | tf_op jit(solution)/shard_map/ppermute | solution.py:209
  50.9 31.4 %collective-permute-start.2 = (bf16[384,1024]{1,0:T(8,128)(2,1)S(1)}, bf16[384,1024]{1,0:T(8,128)(2,1)S(1)}, u32[]{:S(2)}, u32[]{:S(2)}) collective-permute-start(bf16[384,1024]{1,0:T(8,128)(2,1)S(1)} %pad_maximum_fusion.1.here), channel_id=1, source_target_pairs={{2,0},{3,1},{4,2},{5,3},{6,4},{7,5},{8,6},{9,7},{10,8},{11,9},{12,... | collective-permute-start | bytes 2359304 | tf_op jit(solution)/shard_map/ppermute | solution.py:209
  69.3 13.0 %copy-start.1 = (bf16[16,16,1024]{2,1,0:T(8,128)(2,1)}, bf16[16,16,1024]{2,1,0:T(8,128)(2,1)S(1)}, u32[]{:S(2)}) copy-start(bf16[16,16,1024]{2,1,0:T(8,128)(2,1)S(1)} %all-to-all-done.1) | copy-start | bytes 1572868
  69.4 21.1 %copy-start.5 = (bf16[8,16,1024]{2,1,0:T(8,128)(2,1)}, bf16[8,16,1024]{2,1,0:T(8,128)(2,1)S(1)}, u32[]{:S(2)}) copy-start(bf16[8,16,1024]{2,1,0:T(8,128)(2,1)S(1)} %slice.122) | copy-start | bytes 786436
  69.4 28.4 %collective-permute-start.3 = (bf16[128,1024]{1,0:T(8,128)(2,1)S(1)}, bf16[128,1024]{1,0:T(8,128)(2,1)S(1)}, u32[]{:S(2)}, u32[]{:S(2)}) collective-permute-start(bf16[128,1024]{1,0:T(8,128)(2,1)S(1)} %bitcast.69), channel_id=1, source_target_pairs={{0,2},{1,3},{2,4},{3,5},{4,6},{5,7},{6,8},{7,9},{8,10},{9,11},{10,... | collective-permute-start | bytes 786440 | tf_op jit(solution)/shard_map/ppermute | solution.py:209
  72.7 25.0 %collective-permute-start.4 = (bf16[128,1024]{1,0:T(8,128)(2,1)S(1)}, bf16[128,1024]{1,0:T(8,128)(2,1)}, u32[]{:S(2)}, u32[]{:S(2)}) collective-permute-start(bf16[128,1024]{1,0:T(8,128)(2,1)S(1)} %bitcast.70), channel_id=1, source_target_pairs={{2,0},{3,1},{4,2},{5,3},{6,4},{7,5},{8,6},{9,7},{10,8},{11,9},{12,... | collective-permute-start | bytes 786440 | tf_op jit(solution)/shard_map/ppermute | solution.py:209
  79.1 3.3 %copy-start.7 = (bf16[384,1024]{1,0:T(8,128)(2,1)}, bf16[384,1024]{1,0:T(8,128)(2,1)S(1)}, u32[]{:S(2)}) copy-start(bf16[384,1024]{1,0:T(8,128)(2,1)S(1)} %collective-permute-done.1.before) | copy-start | bytes 2359300
  82.3 0.9 copy-start.8
  90.5 43.7 %collective-permute-start.8 = (bf16[384,1024]{1,0:T(8,128)(2,1)}, bf16[384,1024]{1,0:T(8,128)(2,1)S(1)}, u32[]{:S(2)}, u32[]{:S(2)}) collective-permute-start(bf16[384,1024]{1,0:T(8,128)(2,1)} %get-tuple-element.21), channel_id=1, source_target_pairs={{0,2},{1,3},{2,4},{3,5},{4,6},{5,7},{6,8},{7,9},{8,10},{9,11},{10,... | collective-permute-start | bytes 2359304 | tf_op jit(solution)/shard_map/ppermute | solution.py:209
  94.0 40.1 %collective-permute-start.7 = (bf16[384,1024]{1,0:T(8,128)(2,1)}, bf16[384,1024]{1,0:T(8,128)(2,1)S(1)}, u32[]{:S(2)}, u32[]{:S(2)}) collective-permute-start(bf16[384,1024]{1,0:T(8,128)(2,1)} %get-tuple-element.20), channel_id=1, source_target_pairs={{2,0},{3,1},{4,2},{5,3},{6,4},{7,5},{8,6},{9,7},{10,8},{11,9},{12,... | collective-permute-start | bytes 2359304 | tf_op jit(solution)/shard_map/ppermute | solution.py:209
  97.7 0.7 copy-start.10
  105.9 16.4 %copy-start.11 = (bf16[128,1024]{1,0:T(8,128)(2,1)S(1)}, bf16[128,1024]{1,0:T(8,128)(2,1)}, u32[]{:S(2)}) copy-start(bf16[128,1024]{1,0:T(8,128)(2,1)} %get-tuple-element.15) | copy-start | bytes 786436
  105.9 11.4 %collective-permute-start.6 = (bf16[128,1024]{1,0:T(8,128)(2,1)}, bf16[128,1024]{1,0:T(8,128)(2,1)S(1)}, u32[]{:S(2)}, u32[]{:S(2)}) collective-permute-start(bf16[128,1024]{1,0:T(8,128)(2,1)} %get-tuple-element.17), channel_id=1, source_target_pairs={{0,2},{1,3},{2,4},{3,5},{4,6},{5,7},{6,8},{7,9},{8,10},{9,11},{10,... | collective-permute-start | bytes 786440 | tf_op jit(solution)/shard_map/ppermute | solution.py:209
  111.7 10.6 %collective-permute-start.5 = (bf16[128,1024]{1,0:T(8,128)(2,1)}, bf16[128,1024]{1,0:T(8,128)(2,1)S(1)}, u32[]{:S(2)}, u32[]{:S(2)}) collective-permute-start(bf16[128,1024]{1,0:T(8,128)(2,1)} %get-tuple-element.16), channel_id=1, source_target_pairs={{2,0},{3,1},{4,2},{5,3},{6,4},{7,5},{8,6},{9,7},{10,8},{11,9},{12,... | collective-permute-start | bytes 786440 | tf_op jit(solution)/shard_map/ppermute | solution.py:209
  113.6 8.8 %copy-start.12 = (bf16[64,1024]{1,0:T(8,128)(2,1)S(1)}, bf16[64,1024]{1,0:T(8,128)(2,1)}, u32[]{:S(2)}) copy-start(bf16[64,1024]{1,0:T(8,128)(2,1)} %get-tuple-element.14) | copy-start | bytes 393220
  122.4 11.7 %copy-start.6 = (bf16[384,1024]{1,0:T(8,128)(2,1)S(1)}, bf16[384,1024]{1,0:T(8,128)(2,1)}, u32[]{:S(2)}) copy-start(bf16[384,1024]{1,0:T(8,128)(2,1)} %get-tuple-element.19) | copy-start | bytes 2359300
  123.2 27.0 %all-to-all-start.2 = ((bf16[16,48,256]{2,1,0:T(8,128)(2,1)}), bf16[16,48,256]{2,1,0:T(8,128)(2,1)S(1)}, u32[]{:S(2)}, u32[]{:S(2)}) async-start(bf16[16,48,256]{2,1,0:T(8,128)(2,1)} %bitcast.34), calls=%async_computation.2 | async-start | bytes 786432 | tf_op jit(solution)/shard_map/all_to_all | solution.py:206
  134.7 20.7 %collective-permute-start.9 = (bf16[288,1024]{1,0:T(8,128)(2,1)S(1)}, bf16[288,1024]{1,0:T(8,128)(2,1)S(1)}, u32[]{:S(2)}, u32[]{:S(2)}) collective-permute-start(bf16[288,1024]{1,0:T(8,128)(2,1)S(1)} %pad_maximum_fusion.2), channel_id=1, source_target_pairs={{0,1},{1,0},{2,3},{3,2},{4,5},{5,4},{6,7},{7,6},{8,9},{9,8},{10,11... | collective-permute-start | bytes 1769480 | tf_op jit(solution)/shard_map/ppermute | solution.py:214
  151.6 21.7 %all-to-all-start.3 = ((bf16[32,24,256]{2,1,0:T(8,128)(2,1)}), bf16[32,24,256]{2,1,0:T(8,128)(2,1)S(1)}, u32[]{:S(2)}, u32[]{:S(2)}) async-start(bf16[32,24,256]{2,1,0:T(8,128)(2,1)} %bitcast.35), calls=%async_computation.3 | async-start | bytes 786432 | tf_op jit(solution)/shard_map/all_to_all | solution.py:201

commit v2 on v1

v2 whole, which is shorter than its diff:
```python
import functools

import jax
import jax.numpy as jnp
from jax import lax
from jax.experimental import pallas as pl
from jax.experimental.pallas import tpu as pltpu
from jax.sharding import PartitionSpec as P


HD = 128
BAND = 2
NEG_BIG = -1e30
FACTOR = HD ** (-0.5)
HEADS_PER_STEP = 2
INTERPRET = False


def attend(queries, keys, values, grads, bias):
    scores = (
        lax.dot_general(
            queries, keys, (((1,), (1,)), ((), ())), preferred_element_type=jnp.float32
        )
        * FACTOR
    )
    scores = scores + bias
    largest = jnp.max(scores, axis=-1, keepdims=True)
    exponent = jnp.exp(scores - largest)
    weights = exponent * (1.0 / jnp.sum(exponent, axis=-1, keepdims=True))
    half = weights.astype(jnp.bfloat16)
    grad_weights = lax.dot_general(
        grads, values, (((1,), (1,)), ((), ())), preferred_element_type=jnp.float32
    )
    delta = jnp.sum(half.astype(jnp.float32) * grad_weights, axis=-1, keepdims=True)
    grad_scores = (weights * (grad_weights - delta)).astype(jnp.bfloat16)
    grad_query = (
        lax.dot_general(
            grad_scores, keys, (((1,), (0,)), ((), ())), preferred_element_type=jnp.float32
        )
        * FACTOR
    )
    key_terms = (
        lax.dot_general(
            grad_scores, queries, (((0,), (0,)), ((), ())), preferred_element_type=jnp.float32
        )
        * FACTOR
    )
    value_terms = lax.dot_general(
        half, grads, (((0,), (0,)), ((), ())), preferred_element_type=jnp.float32
    )
    return grad_query, key_terms, value_terms


def video_kernel(group, count, lens, queries, grads, before, here, after, dq_ref, tb, th, ta, bias):
    part = before.shape[0] // 2

    @pl.when(pl.program_id(0) == 0)
    def _():
        video_bias(group, count, lens, part, bias)

    def one(head):
        cols = slice(head * HD, (head + 1) * HD)
        keys = jnp.concatenate([ref[:part, cols] for ref in (before, here, after)], axis=0)
        values = jnp.concatenate([ref[part:, cols] for ref in (before, here, after)], axis=0)
        dq, kt, vt = attend(queries[:, cols], keys, values, grads[:, cols], bias[...])
        dq_ref[:, cols] = dq.astype(jnp.bfloat16)
        for place, out in enumerate((tb, th, ta)):
            span = slice(place * part, (place + 1) * part)
            out[:part, cols] = kt[span].astype(jnp.bfloat16)
            out[part:, cols] = vt[span].astype(jnp.bfloat16)

    for head in range(dq_ref.shape[1] // HD):
        one(head)


def video_bias(group, count, lens, part, bias):
    rows, slots = bias.shape[0], part // 2
    frame = lax.axis_index("frame")
    block = lax.axis_index("seq")
    core = lax.rem(block, 2)
    base = block - core
    column = lax.broadcasted_iota(jnp.int32, (1, 3 * part), 1)
    early_row = jnp.full((1, 3 * part), NEG_BIG, jnp.float32)
    late_row = early_row
    for place in range(6):
        offset = 2 * (place // 2) - 2 + (core if place % 2 == 0 else 1 - core)
        time = base + offset
        known = (time >= 0) & (time < count)
        live = lens[frame, jnp.clip(time, 0, count - 1)]
        live = jnp.where(known, live, 0)
        early = jnp.where(jnp.abs(offset) <= BAND, live, 0)
        late = jnp.where(jnp.abs(offset - 1) <= BAND, live, 0)
        first = column >= place * slots
        early_row = jnp.where(first & (column < place * slots + early), 0.0, early_row)
        late_row = jnp.where(first & (column < place * slots + late), 0.0, late_row)
    is_late = (lax.broadcasted_iota(jnp.int32, (rows, 1), 0) // group) % 2
    bias[...] = jnp.where(is_late == 0, early_row, late_row)


def audio_kernel(
    group, count, lens, aud_q, aud_g, their_q, their_g, before, here, after, dq_ref, tb, th, ta, bias
):
    rows, half = aud_q.shape[0], aud_q.shape[1] // 2
    wide = their_q.shape[1]
    part = before.shape[0] // 2
    frame = lax.axis_index("frame")
    block = lax.axis_index("seq")
    core = lax.rem(block, 2)
    base = block - core
    other = base + 1 - core
    column = lax.broadcasted_iota(jnp.int32, (1, 3 * part), 1)
    offset = 2 * (column // part) - 2 + (column // group) % 2
    known = (base + offset >= 0) & (base + offset < count)

    @pl.when(pl.program_id(0) == 0)
    def _():
        for j, own in enumerate((core, 1 - core)):
            seen = known & (jnp.abs(offset - own) <= BAND)
            bias[j * rows : (j + 1) * rows] = jnp.broadcast_to(
                jnp.where(seen, 0.0, NEG_BIG), (rows, 3 * part)
            )

    slot = lax.broadcasted_iota(jnp.int32, (rows, 1), 0)
    live_mine = (slot < lens[frame, block]).astype(jnp.float32)
    live_other = (slot < lens[frame, other]).astype(jnp.float32)

    def one(head):
        cols = slice(head * HD, (head + 1) * HD)
        start = core * half + pl.program_id(0) * wide + head * HD
        mine = pl.ds(pl.multiple_of(start, HD), HD)
        queries = jnp.concatenate([aud_q[:, mine], their_q[:, cols]], axis=0)
        zero = jnp.zeros((), jnp.float32)
        grads = jnp.concatenate(
            [
                jnp.where(live_mine > 0, aud_g[:, mine].astype(jnp.float32), zero),
                jnp.where(live_other > 0, their_g[:, cols].astype(jnp.float32), zero),
            ],
            axis=0,
        ).astype(jnp.bfloat16)
        keys = jnp.concatenate([ref[:part, cols] for ref in (before, here, after)], axis=0)
        values = jnp.concatenate([ref[part:, cols] for ref in (before, here, after)], axis=0)
        dq, kt, vt = attend(queries, keys, values, grads, bias[...])
        dq_ref[:, cols] = dq.astype(jnp.bfloat16)
        for place, out in enumerate((tb, th, ta)):
            span = slice(place * part, (place + 1) * part)
            out[:part, cols] = kt[span].astype(jnp.bfloat16)
            out[part:, cols] = vt[span].astype(jnp.bfloat16)

    for head in range(wide // HD):
        one(head)


def cost(rows, keys, width):
    heads_here = width // HD
    return pl.CostEstimate(
        flops=10 * rows * keys * HD * heads_here,
        bytes_accessed=2 * width * (4 * rows + 4 * keys),
        transcendentals=rows * keys * heads_here,
    )


ON_CHIP = pl.BlockSpec(memory_space=pltpu.VMEM)
GRANT = 20 * 2**20
SCALARS = pl.BlockSpec(memory_space=pltpu.SMEM)


def side(kernel, lens, operands, specs, rows, window, width):
    bf = jnp.bfloat16
    wide = min(HEADS_PER_STEP * HD, width)
    return pl.pallas_call(
        kernel,
        grid=(width // wide,),
        in_specs=[SCALARS] + specs,
        out_specs=[columns(rows, wide)] + [columns(window, wide)] * 3,
        out_shape=[jax.ShapeDtypeStruct((rows, width), bf)]
        + [jax.ShapeDtypeStruct((window, width), bf)] * 3,
        scratch_shapes=[pltpu.VMEM((rows, 3 * window // 2), jnp.float32)],
        compiler_params=pltpu.CompilerParams(vmem_limit_bytes=GRANT),
        cost_estimate=cost(rows, 3 * window // 2, width),
        interpret=INTERPRET,
    )(lens, *operands)


def columns(rows, wide, row=0):
    return pl.BlockSpec((rows, wide), lambda h: (row, h))


def assemble_kernel(runs, spreads, group, x, *outs):
    slim = x.shape[2]
    for run in range(runs):
        for spread in range(spreads):
            for core in range(2):
                piece = (run * spreads + spread) * 2 + core
                for j, out in enumerate(outs):
                    left = (core * spreads + spread) * slim
                    out[0, run * group : (run + 1) * group, left : left + slim] = x[
                        piece, j * group : (j + 1) * group, :
                    ]


def assemble(x, runs, spreads, group):
    shape = (1, runs * group, 2 * spreads * x.shape[2])
    return pl.pallas_call(
        functools.partial(assemble_kernel, runs, spreads, group),
        in_specs=[ON_CHIP],
        out_specs=[ON_CHIP] * 3,
        out_shape=[jax.ShapeDtypeStruct(shape, jnp.bfloat16)] * 3,
        compiler_params=pltpu.CompilerParams(vmem_limit_bytes=GRANT),
        name="assemble",
        interpret=INTERPRET,
    )(x)


def shards(vid_q, vid_k, vid_v, vid_dout, aud_q, aud_k, aud_v, aud_dout, aud_len, match):
    frames = lax.axis_size("frame")
    count = lax.axis_size("seq")
    block_here = lax.axis_index("seq")
    core = block_here % 2
    video_rows, width = vid_q.shape[1], vid_q.shape[2]
    audio_rows = aud_q.shape[1]
    half = width // 2
    group = 4 * video_rows // frames
    runs = frames // 4
    spreads = frames // runs
    slim = half // spreads
    f32, bf = jnp.float32, jnp.bfloat16

    pairs = [
        [f * count + 2 * c + k for f in range(frames) for k in range(2)]
        for c in range(count // 2)
    ]

    def pair_exchange(x):
        return lax.all_to_all(
            x, ("frame", "seq"), split_axis=0, concat_axis=0, tiled=True, axis_index_groups=pairs
        )

    def exchange(x):
        return lax.all_to_all(x, "frame", split_axis=0, concat_axis=0, tiled=True)

    def shift(x, by):
        return lax.ppermute(
            x, "seq", [(i, i + by) for i in range(count) if 0 <= i + by < count]
        )

    def swap(x):
        return lax.ppermute(x, "seq", [(i, i ^ 1) for i in range(count)])

    order = jnp.arange(frames, dtype=jnp.int32)
    inverse = jnp.sum(
        jnp.where(match[None, :] == order[:, None], order[None, :], 0), axis=1
    ).astype(jnp.int32)

    packed = jnp.concatenate([vid_q[0], vid_k[0], vid_v[0], vid_dout[0]], axis=0)
    packed = packed.reshape(frames, group, 2, half).transpose(0, 2, 1, 3)
    spread = pair_exchange(packed.reshape(2 * frames, group, half))
    spread = jnp.take(spread.reshape(frames, 2 * group, half), inverse, axis=0, mode="clip")
    video = exchange(spread).reshape(frames * 2 * group, half)

    def halves(x):
        low, high = x[0, :, :half], x[0, :, half:]
        return jnp.where(core == 0, low, high), jnp.where(core == 0, high, low)

    own_k, send_k = halves(aud_k)
    own_v, send_v = halves(aud_v)
    send_q = halves(aud_q)[1]
    send_g = halves(aud_dout)[1]
    sent = jnp.concatenate([send_q, send_k, send_v, send_g], axis=0)
    theirs = swap(sent)
    audio_here = jnp.concatenate(
        [
            own_k,
            theirs[audio_rows : 2 * audio_rows],
            own_v,
            theirs[2 * audio_rows : 3 * audio_rows],
        ],
        axis=0,
    )
    audio_before = shift(audio_here, 2)
    audio_after = shift(audio_here, -2)

    block = 2 * video_rows
    video_here = video[block : 3 * block]
    video_before = shift(video_here, 2)
    video_after = shift(video_here, -2)
    wide = min(HEADS_PER_STEP * HD, half)
    full = pl.BlockSpec((audio_rows, width), lambda h: (0, 0))
    grad_vq, audio_tb, audio_th, audio_ta = side(
        functools.partial(video_kernel, group, count),
        aud_len,
        (video, video, audio_before, audio_here, audio_after),
        [columns(block, wide), columns(block, wide, 3)] + [columns(4 * audio_rows, wide)] * 3,
        block,
        4 * audio_rows,
        half,
    )
    grad_aq, video_tb, video_th, video_ta = side(
        functools.partial(audio_kernel, group, count),
        aud_len,
        (aud_q[0], aud_dout[0], theirs, theirs, video_before, video_here, video_after),
        [full, full, columns(audio_rows, wide), columns(audio_rows, wide, 3)]
        + [columns(2 * block, wide)] * 3,
        2 * audio_rows,
        2 * block,
        half,
    )

    grad_vkv = (
        video_th.astype(f32)
        + shift(video_tb, -2).astype(f32)
        + shift(video_ta, 2).astype(f32)
    ).astype(bf)
    grads = jnp.concatenate([grad_vq, grad_vkv], axis=0)
    grads = grads.reshape(3, runs, 2, group, spreads, slim).transpose(1, 4, 2, 0, 3, 5)
    grads = exchange(grads.reshape(frames, 6 * group, slim))
    grads = jnp.take(grads, match, axis=0, mode="clip")
    grads = pair_exchange(grads.reshape(2 * frames, 3 * group, slim))
    grads = assemble(grads, runs, spreads, group)

    from_after, from_before = shift(audio_tb, -2), shift(audio_ta, 2)
    grad_akv = (
        audio_th.astype(f32) + from_after.astype(f32) + from_before.astype(f32)
    ).astype(bf)
    mine = (
        grad_aq[:audio_rows],
        grad_akv[:audio_rows],
        grad_akv[2 * audio_rows : 3 * audio_rows],
    )
    back = swap(
        jnp.concatenate(
            [
                grad_aq[audio_rows:],
                grad_akv[audio_rows : 2 * audio_rows],
                grad_akv[3 * audio_rows :],
            ],
            axis=0,
        )
    )

    def whole(own, other):
        return jnp.where(
            core == 0,
            jnp.concatenate([own, other], axis=1),
            jnp.concatenate([other, own], axis=1),
        )[None]

    outs = [
        whole(mine[j], back[j * audio_rows : (j + 1) * audio_rows]) for j in range(3)
    ]
    return (*grads, *outs)


def solution(mesh):
    tokens = P("frame", "seq", None)
    return jax.shard_map(
        shards,
        mesh=mesh,
        in_specs=(tokens,) * 8 + (P(), P()),
        out_specs=(tokens,) * 6,
        check_vma=False,
    )
```

time: 177 us -> 171 us (0.966)
  local copies, waits for them, and re-layouts: 10.2 us -> 4.63 us
  waiting for transfers between devices: 77.2 us -> 79.5 us
    ppermute x8, waiting for transfers between devices: 14.6 us -> 18.6 us  [shift(): lax.ppermute(x, 'seq', [(i, i + by) for i in range(count) if 0 <= i + by...]
    slice x8 -> x0, local copies, waits for them, and re-layouts: 2.5 us -> none  [the longest x3 0.83 us: shards(): grads[2][None]]
    pallas_call x2 -> x3, Pallas kernels: 14.7 us -> 14.3 us  [the longest x2 13.6 us: side(): pl.pallas_call(kernel, grid=(width // wide,), in_specs=[SCALARS] + specs,...]
  transfers between devices with their start and end apart: 14 -> 14, of which waited for: 8 -> 8; matrix products, arithmetic and copies ran while one was open for 6% -> 5% of each run, Pallas kernels for 8% -> 8%
where the time goes in v2:
time: 171 us; the launch traced here: 170 us
  waiting for transfers between devices  79.5 us (46%)
  starting transfers between devices  64.6 us (38%)
  Pallas kernels  14.3 us (8%)
  other arithmetic  6.24 us (4%)
  local copies, waits for them, and re-layouts  4.63 us (3%)
    all_to_all x2, waiting for transfers between devices, pair_exchange(): lax.all_to_all(x, ('frame', 'seq'), split_axis=0, concat_axis=0, tiled=Tr...  32.3 us
    all_to_all x2, waiting for transfers between devices, exchange(): return lax.all_to_all(x, 'frame', split_axis=0, concat_axis=0, tiled=True)  28.5 us
    ppermute x8, starting transfers between devices, shift(): lax.ppermute(x, 'seq', [(i, i + by) for i in range(count) if 0 <= i + by...  24.9 us
    all_to_all x2, starting transfers between devices, pair_exchange(): lax.all_to_all(x, ('frame', 'seq'), split_axis=0, concat_axis=0, tiled=Tr...  19.9 us
    ppermute x8, waiting for transfers between devices, shift(): lax.ppermute(x, 'seq', [(i, i + by) for i in range(count) if 0 <= i + by...  18.6 us
    all_to_all x2, starting transfers between devices, exchange(): return lax.all_to_all(x, 'frame', split_axis=0, concat_axis=0, tiled=True)  15.7 us
    pallas_call x2, Pallas kernels, side(): pl.pallas_call(kernel, grid=(width // wide,), in_specs=[SCALARS] + specs,...  13.6 us
    ppermute x2, starting transfers between devices, swap(): return lax.ppermute(x, 'seq', [(i, i ^ 1) for i in range(count)])  4.1 us
  transfers between devices with their start and end apart: 14, of which 8 were waited for; matrix products, arithmetic and copies ran while one was open for 5% of the time, Pallas kernels for 8%

profile of v2, /device:TPU:6, one launch (start us, length us, event | category | flops | bytes accessed | tf_op | source)
XLA Modules:
  0.0 170.3 jit_solution(2168027836338975300)
XLA Ops:
  0.6 1.9 %pad_maximum_fusion.3 = bf16[128,2048]{1,0:T(8,128)(2,1)} fusion(bf16[32,2048]{1,0:T(8,128)(2,1)} %bitcast.52, bf16[32,2048]{1,0:T(8,128)(2,1)} %bitcast.53, bf16[32,2048]{1,0:T(8,128)(2,1)} %bitcast.54, bf16[32,2048]{1,0:T(8,128)(2,1)} %bitcast.55), kind=kLoop, calls=%fused_computation.6 | loop fusion | flops 2097152 | bytes 1048576 | tf_op jit(solution)/shard_map/concatenate | solution.py:254
  2.6 16.1 %all-to-all-start = ((bf16[32,8,1024]{2,1,0:T(8,128)(2,1)}), bf16[32,8,1024]{2,1,0:T(8,128)(2,1)S(1)}, u32[]{:S(2)}, u32[]{:S(2)}) async-start(bf16[32,8,1024]{2,1,0:T(8,128)(2,1)} %bitcast.6), calls=%async_computation | async-start | bytes 1048576 | tf_op jit(solution)/shard_map/all_to_all | solution.py:234
  18.8 0.9 copy-done.6
  19.9 2.2 %collective-permute-start = (bf16[384,1024]{1,0:T(8,128)(2,1)S(1)}, bf16[384,1024]{1,0:T(8,128)(2,1)S(1)}, u32[]{:S(2)}, u32[]{:S(2)}) collective-permute-start(bf16[384,1024]{1,0:T(8,128)(2,1)S(1)} %pad_maximum_fusion), channel_id=1, source_target_pairs={{0,1},{1,0},{2,3},{3,2},{4,5},{5,4},{6,7},{7,6},{8,9},{9,8},{10,11... | collective-permute-start | bytes 2359304 | tf_op jit(solution)/shard_map/ppermute | solution.py:247
  22.2 16.6 %all-to-all-done = bf16[32,8,1024]{2,1,0:T(8,128)(2,1)S(1)} async-done(((bf16[32,8,1024]{2,1,0:T(8,128)(2,1)}), bf16[32,8,1024]{2,1,0:T(8,128)(2,1)S(1)}, u32[]{:S(2)}, u32[]{:S(2)}) %all-to-all-start) | async-done | bytes 524320 | tf_op jit(solution)/shard_map/all_to_all | solution.py:234
  38.8 1.4 gather_fusion
  40.2 4.6 %all-to-all-start.1 = ((bf16[16,16,1024]{2,1,0:T(8,128)(2,1)}), bf16[16,16,1024]{2,1,0:T(8,128)(2,1)S(1)}, u32[]{:S(2)}, u32[]{:S(2)}) async-start(bf16[16,16,1024]{2,1,0:T(8,128)(2,1)} %gather_fusion), calls=%async_computation.1 | async-start | bytes 1048576 | tf_op jit(solution)/shard_map/all_to_all | solution.py:239
  44.9 3.3 %collective-permute-start.1 = (bf16[384,1024]{1,0:T(8,128)(2,1)S(1)}, bf16[384,1024]{1,0:T(8,128)(2,1)}, u32[]{:S(2)}, u32[]{:S(2)}) collective-permute-start(bf16[384,1024]{1,0:T(8,128)(2,1)S(1)} %pad_maximum_fusion.1.here), channel_id=1, source_target_pairs={{0,2},{1,3},{2,4},{3,5},{4,6},{5,7},{6,8},{7,9},{8,10},{9,11},{10,... | collective-permute-start | bytes 2359304 | tf_op jit(solution)/shard_map/ppermute | solution.py:242
  48.2 2.5 %collective-permute-start.2 = (bf16[384,1024]{1,0:T(8,128)(2,1)S(1)}, bf16[384,1024]{1,0:T(8,128)(2,1)}, u32[]{:S(2)}, u32[]{:S(2)}) collective-permute-start(bf16[384,1024]{1,0:T(8,128)(2,1)S(1)} %pad_maximum_fusion.1.here), channel_id=1, source_target_pairs={{2,0},{3,1},{4,2},{5,3},{6,4},{7,5},{8,6},{9,7},{10,8},{11,9},{12,... | collective-permute-start | bytes 2359304 | tf_op jit(solution)/shard_map/ppermute | solution.py:242
  50.8 15.8 %all-to-all-done.1 = bf16[16,16,1024]{2,1,0:T(8,128)(2,1)S(1)} async-done(((bf16[16,16,1024]{2,1,0:T(8,128)(2,1)}), bf16[16,16,1024]{2,1,0:T(8,128)(2,1)S(1)}, u32[]{:S(2)}, u32[]{:S(2)}) %all-to-all-start.1) | async-done | bytes 524320 | tf_op jit(solution)/shard_map/all_to_all | solution.py:239
  66.6 3.3 %collective-permute-start.3 = (bf16[128,1024]{1,0:T(8,128)(2,1)S(1)}, bf16[128,1024]{1,0:T(8,128)(2,1)S(1)}, u32[]{:S(2)}, u32[]{:S(2)}) collective-permute-start(bf16[128,1024]{1,0:T(8,128)(2,1)S(1)} %bitcast.47), channel_id=1, source_target_pairs={{0,2},{1,3},{2,4},{3,5},{4,6},{5,7},{6,8},{7,9},{8,10},{9,11},{10,... | collective-permute-start | bytes 786440 | tf_op jit(solution)/shard_map/ppermute | solution.py:242
  70.0 2.5 %collective-permute-start.4 = (bf16[128,1024]{1,0:T(8,128)(2,1)S(1)}, bf16[128,1024]{1,0:T(8,128)(2,1)S(1)}, u32[]{:S(2)}, u32[]{:S(2)}) collective-permute-start(bf16[128,1024]{1,0:T(8,128)(2,1)S(1)} %bitcast.48), channel_id=1, source_target_pairs={{2,0},{3,1},{4,2},{5,3},{6,4},{7,5},{8,6},{9,7},{10,8},{11,9},{12,... | collective-permute-start | bytes 786440 | tf_op jit(solution)/shard_map/ppermute | solution.py:242
  72.5 3.9 %collective-permute-done.1.before = bf16[384,1024]{1,0:T(8,128)(2,1)} collective-permute-done((bf16[384,1024]{1,0:T(8,128)(2,1)S(1)}, bf16[384,1024]{1,0:T(8,128)(2,1)}, u32[]{:S(2)}, u32[]{:S(2)}) %collective-permute-start.1) | collective-permute-done | bytes 786464 | tf_op jit(solution)/shard_map/ppermute | solution.py:242
  76.4 3.3 %collective-permute-done.2.after = bf16[384,1024]{1,0:T(8,128)(2,1)} collective-permute-done((bf16[384,1024]{1,0:T(8,128)(2,1)S(1)}, bf16[384,1024]{1,0:T(8,128)(2,1)}, u32[]{:S(2)}, u32[]{:S(2)}) %collective-permute-start.2) | collective-permute-done | bytes 786464 | tf_op jit(solution)/shard_map/ppermute | solution.py:242
  79.7 7.4 %shard_map.145 = (bf16[64,1024]{1,0:T(8,128)(2,1)S(1)}, bf16[384,1024]{1,0:T(8,128)(2,1)}, bf16[384,1024]{1,0:T(8,128)(2,1)S(1)}, bf16[384,1024]{1,0:T(8,128)(2,1)}) custom-call(s32[16,32]{1,0:T(8,128)S(1)} %copy-done.4, bf16[256,1024]{1,0:T(8,128)(2,1)S(1)} %bitcast.43, bf16[256,1024]{1,0:T(8,128)(2,1)S(1)} %bitcast.44, ...), custom_call_target="tpu_custom_call" | custom-call | flops 377487360 | bytes 5242880 | tf_op jit(solution)/shard_map/pallas_call | solution.py:170
  87.1 3.3 %collective-permute-start.8 = (bf16[384,1024]{1,0:T(8,128)(2,1)}, bf16[384,1024]{1,0:T(8,128)(2,1)}, u32[]{:S(2)}, u32[]{:S(2)}) collective-permute-start(bf16[384,1024]{1,0:T(8,128)(2,1)} %get-tuple-element.27), channel_id=1, source_target_pairs={{0,2},{1,3},{2,4},{3,5},{4,6},{5,7},{6,8},{7,9},{8,10},{9,11},{10,... | collective-permute-start | bytes 2359304 | tf_op jit(solution)/shard_map/ppermute | solution.py:242
  90.4 2.5 %collective-permute-start.7 = (bf16[384,1024]{1,0:T(8,128)(2,1)}, bf16[384,1024]{1,0:T(8,128)(2,1)}, u32[]{:S(2)}, u32[]{:S(2)}) collective-permute-start(bf16[384,1024]{1,0:T(8,128)(2,1)} %get-tuple-element.26), channel_id=1, source_target_pairs={{2,0},{3,1},{4,2},{5,3},{6,4},{7,5},{8,6},{9,7},{10,8},{11,9},{12,... | collective-permute-start | bytes 2359304 | tf_op jit(solution)/shard_map/ppermute | solution.py:242
  93.0 6.1 %shard_map.146 = (bf16[192,1024]{1,0:T(8,128)(2,1)S(1)}, bf16[128,1024]{1,0:T(8,128)(2,1)S(1)}, bf16[128,1024]{1,0:T(8,128)(2,1)S(1)}, bf16[128,1024]{1,0:T(8,128)(2,1)S(1)}) custom-call(s32[16,32]{1,0:T(8,128)S(1)} %copy-done.4, bf16[96,2048]{1,0:T(8,128)(2,1)S(1)} %bitcast.45, bf16[96,2048]{1,0:T(8,128)(2,1)S(1)} %bitcast.46, ...), custom_call_target="tpu_custom_call" | custom-call | flops 377487360 | bytes 3145728 | tf_op jit(solution)/shard_map/pallas_call | solution.py:170
  99.1 5.4 %collective-permute-start.6 = (bf16[128,1024]{1,0:T(8,128)(2,1)S(1)}, bf16[128,1024]{1,0:T(8,128)(2,1)S(1)}, u32[]{:S(2)}, u32[]{:S(2)}) collective-permute-start(bf16[128,1024]{1,0:T(8,128)(2,1)S(1)} %get-tuple-element.20), channel_id=1, source_target_pairs={{0,2},{1,3},{2,4},{3,5},{4,6},{5,7},{6,8},{7,9},{8,10},{9,11},{10,... | collective-permute-start | bytes 786440 | tf_op jit(solution)/shard_map/ppermute | solution.py:242
  104.6 1.9 %collective-permute-start.5 = (bf16[128,1024]{1,0:T(8,128)(2,1)S(1)}, bf16[128,1024]{1,0:T(8,128)(2,1)S(1)}, u32[]{:S(2)}, u32[]{:S(2)}) collective-permute-start(bf16[128,1024]{1,0:T(8,128)(2,1)S(1)} %get-tuple-element.19), channel_id=1, source_target_pairs={{2,0},{3,1},{4,2},{5,3},{6,4},{7,5},{8,6},{9,7},{10,8},{11,9},{12,... | collective-permute-start | bytes 786440 | tf_op jit(solution)/shard_map/ppermute | solution.py:242
  106.5 7.4 %collective-permute-done.6 = bf16[128,1024]{1,0:T(8,128)(2,1)S(1)} collective-permute-done((bf16[128,1024]{1,0:T(8,128)(2,1)S(1)}, bf16[128,1024]{1,0:T(8,128)(2,1)S(1)}, u32[]{:S(2)}, u32[]{:S(2)}) %collective-permute-start.6) | collective-permute-done | bytes 262176 | tf_op jit(solution)/shard_map/ppermute | solution.py:242
  113.9 4.0 %collective-permute-done.5 = bf16[128,1024]{1,0:T(8,128)(2,1)S(1)} collective-permute-done((bf16[128,1024]{1,0:T(8,128)(2,1)S(1)}, bf16[128,1024]{1,0:T(8,128)(2,1)S(1)}, u32[]{:S(2)}, u32[]{:S(2)}) %collective-permute-start.5) | collective-permute-done | bytes 262176 | tf_op jit(solution)/shard_map/ppermute | solution.py:242
  118.1 0.8 copy.17
  118.9 11.1 %all-to-all-start.2 = ((bf16[16,48,256]{2,1,0:T(8,128)(2,1)}), bf16[16,48,256]{2,1,0:T(8,128)(2,1)S(1)}, u32[]{:S(2)}, u32[]{:S(2)}) async-start(bf16[16,48,256]{2,1,0:T(8,128)(2,1)} %bitcast.20), calls=%async_computation.2 | async-start | bytes 786432 | tf_op jit(solution)/shard_map/all_to_all | solution.py:239
  130.0 1.8 %add_convert_fusion = bf16[384,1024]{1,0:T(8,128)(2,1)S(1)} fusion(bf16[384,1024]{1,0:T(8,128)(2,1)} %collective-permute-done.8, bf16[384,1024]{1,0:T(8,128)(2,1)} %collective-permute-done.7, bf16[384,1024]{1,0:T(8,128)(2,1)S(1)} %copy-done.3), kind=kLoop, calls=%fused_computation.2 | loop fusion | flops 2359296 | bytes 3145728 | tf_op jit(solution)/shard_map/convert_element_type | solution.py:323
  131.9 1.9 %collective-permute-start.9 = (bf16[288,1024]{1,0:T(8,128)(2,1)S(1)}, bf16[288,1024]{1,0:T(8,128)(2,1)S(1)}, u32[]{:S(2)}, u32[]{:S(2)}) collective-permute-start(bf16[288,1024]{1,0:T(8,128)(2,1)S(1)} %pad_maximum_fusion.2), channel_id=1, source_target_pairs={{0,1},{1,0},{2,3},{3,2},{4,5},{5,4},{6,7},{7,6},{8,9},{9,8},{10,11... | collective-permute-start | bytes 1769480 | tf_op jit(solution)/shard_map/ppermute | solution.py:247
  133.9 12.7 %all-to-all-done.2 = bf16[16,48,256]{2,1,0:T(8,128)(2,1)S(1)} async-done(((bf16[16,48,256]{2,1,0:T(8,128)(2,1)}), bf16[16,48,256]{2,1,0:T(8,128)(2,1)S(1)}, u32[]{:S(2)}, u32[]{:S(2)}) %all-to-all-start.2) | async-done | bytes 393248 | tf_op jit(solution)/shard_map/all_to_all | solution.py:239
  146.5 1.3 gather_fusion.1
  147.8 3.9 %all-to-all-start.3 = ((bf16[32,24,256]{2,1,0:T(8,128)(2,1)}), bf16[32,24,256]{2,1,0:T(8,128)(2,1)S(1)}, u32[]{:S(2)}, u32[]{:S(2)}) async-start(bf16[32,24,256]{2,1,0:T(8,128)(2,1)} %bitcast.21), calls=%async_computation.3 | async-start | bytes 786432 | tf_op jit(solution)/shard_map/all_to_all | solution.py:234
  151.8 0.8 maximum_select_fusion.2
  152.6 1.2 maximum_select_fusion
  153.8 15.7 %all-to-all-done.3.x = bf16[32,24,256]{2,1,0:T(8,128)(2,1)S(1)} async-done(((bf16[32,24,256]{2,1,0:T(8,128)(2,1)}), bf16[32,24,256]{2,1,0:T(8,128)(2,1)S(1)}, u32[]{:S(2)}, u32[]{:S(2)}) %all-to-all-start.3) | async-done | bytes 393248 | tf_op jit(solution)/shard_map/all_to_all | solution.py:234
  (39 shorter events, 1.6 us)
Async XLA Ops:
  2.6 16.1 %copy-start.1 = (bf16[1,96,2048]{2,1,0:T(8,128)(2,1)S(1)}, bf16[1,96,2048]{2,1,0:T(8,128)(2,1)}, u32[]{:S(2)}) copy-start(bf16[1,96,2048]{2,1,0:T(8,128)(2,1)} %param.17) | copy-start | bytes 1179652
  2.6 16.1 %copy-start.5 = (bf16[1,96,2048]{2,1,0:T(8,128)(2,1)S(1)}, bf16[1,96,2048]{2,1,0:T(8,128)(2,1)}, u32[]{:S(2)}) copy-start(bf16[1,96,2048]{2,1,0:T(8,128)(2,1)} %param.16) | copy-start | bytes 1179652
  2.6 36.2 %all-to-all-start = ((bf16[32,8,1024]{2,1,0:T(8,128)(2,1)}), bf16[32,8,1024]{2,1,0:T(8,128)(2,1)S(1)}, u32[]{:S(2)}, u32[]{:S(2)}) async-start(bf16[32,8,1024]{2,1,0:T(8,128)(2,1)} %bitcast.6), calls=%async_computation | async-start | bytes 1048576 | tf_op jit(solution)/shard_map/all_to_all | solution.py:234
  18.6 1.0 copy-start.6
  18.7 1.1 copy-start
  19.8 2.3 %copy-start.7 = (s32[16]{0:T(128)S(1)}, s32[16]{0:T(128)}, u32[]{:S(2)}) copy-start(s32[16]{0:T(128)} %param.19) | copy-start | bytes 196
  19.9 24.9 %collective-permute-start = (bf16[384,1024]{1,0:T(8,128)(2,1)S(1)}, bf16[384,1024]{1,0:T(8,128)(2,1)S(1)}, u32[]{:S(2)}, u32[]{:S(2)}) collective-permute-start(bf16[384,1024]{1,0:T(8,128)(2,1)S(1)} %pad_maximum_fusion), channel_id=1, source_target_pairs={{0,1},{1,0},{2,3},{3,2},{4,5},{5,4},{6,7},{7,6},{8,9},{9,8},{10,11... | collective-permute-start | bytes 2359304 | tf_op jit(solution)/shard_map/ppermute | solution.py:247
  40.2 26.4 %all-to-all-start.1 = ((bf16[16,16,1024]{2,1,0:T(8,128)(2,1)}), bf16[16,16,1024]{2,1,0:T(8,128)(2,1)S(1)}, u32[]{:S(2)}, u32[]{:S(2)}) async-start(bf16[16,16,1024]{2,1,0:T(8,128)(2,1)} %gather_fusion), calls=%async_computation.1 | async-start | bytes 1048576 | tf_op jit(solution)/shard_map/all_to_all | solution.py:239
  44.8 34.8 %copy-start.4 = (s32[16,32]{1,0:T(8,128)S(1)}, s32[16,32]{1,0:T(8,128)}, u32[]{:S(2)}) copy-start(s32[16,32]{1,0:T(8,128)} %lens.3) | copy-start | bytes 6148
  44.9 31.5 %collective-permute-start.1 = (bf16[384,1024]{1,0:T(8,128)(2,1)S(1)}, bf16[384,1024]{1,0:T(8,128)(2,1)}, u32[]{:S(2)}, u32[]{:S(2)}) collective-permute-start(bf16[384,1024]{1,0:T(8,128)(2,1)S(1)} %pad_maximum_fusion.1.here), channel_id=1, source_target_pairs={{0,2},{1,3},{2,4},{3,5},{4,6},{5,7},{6,8},{7,9},{8,10},{9,11},{10,... | collective-permute-start | bytes 2359304 | tf_op jit(solution)/shard_map/ppermute | solution.py:242
  48.2 31.4 %collective-permute-start.2 = (bf16[384,1024]{1,0:T(8,128)(2,1)S(1)}, bf16[384,1024]{1,0:T(8,128)(2,1)}, u32[]{:S(2)}, u32[]{:S(2)}) collective-permute-start(bf16[384,1024]{1,0:T(8,128)(2,1)S(1)} %pad_maximum_fusion.1.here), channel_id=1, source_target_pairs={{2,0},{3,1},{4,2},{5,3},{6,4},{7,5},{8,6},{9,7},{10,8},{11,9},{12,... | collective-permute-start | bytes 2359304 | tf_op jit(solution)/shard_map/ppermute | solution.py:242
  66.6 26.3 %collective-permute-start.3 = (bf16[128,1024]{1,0:T(8,128)(2,1)S(1)}, bf16[128,1024]{1,0:T(8,128)(2,1)S(1)}, u32[]{:S(2)}, u32[]{:S(2)}) collective-permute-start(bf16[128,1024]{1,0:T(8,128)(2,1)S(1)} %bitcast.47), channel_id=1, source_target_pairs={{0,2},{1,3},{2,4},{3,5},{4,6},{5,7},{6,8},{7,9},{8,10},{9,11},{10,... | collective-permute-start | bytes 786440 | tf_op jit(solution)/shard_map/ppermute | solution.py:242
  70.0 23.0 %collective-permute-start.4 = (bf16[128,1024]{1,0:T(8,128)(2,1)S(1)}, bf16[128,1024]{1,0:T(8,128)(2,1)S(1)}, u32[]{:S(2)}, u32[]{:S(2)}) collective-permute-start(bf16[128,1024]{1,0:T(8,128)(2,1)S(1)} %bitcast.48), channel_id=1, source_target_pairs={{2,0},{3,1},{4,2},{5,3},{6,4},{7,5},{8,6},{9,7},{10,8},{11,9},{12,... | collective-permute-start | bytes 786440 | tf_op jit(solution)/shard_map/ppermute | solution.py:242
  87.1 12.0 %copy-start.2 = (bf16[384,1024]{1,0:T(8,128)(2,1)}, bf16[384,1024]{1,0:T(8,128)(2,1)S(1)}, u32[]{:S(2)}) copy-start(bf16[384,1024]{1,0:T(8,128)(2,1)S(1)} %get-tuple-element.25) | copy-start | bytes 2359300
  87.1 42.9 %collective-permute-start.8 = (bf16[384,1024]{1,0:T(8,128)(2,1)}, bf16[384,1024]{1,0:T(8,128)(2,1)}, u32[]{:S(2)}, u32[]{:S(2)}) collective-permute-start(bf16[384,1024]{1,0:T(8,128)(2,1)} %get-tuple-element.27), channel_id=1, source_target_pairs={{0,2},{1,3},{2,4},{3,5},{4,6},{5,7},{6,8},{7,9},{8,10},{9,11},{10,... | collective-permute-start | bytes 2359304 | tf_op jit(solution)/shard_map/ppermute | solution.py:242
  90.4 39.6 %collective-permute-start.7 = (bf16[384,1024]{1,0:T(8,128)(2,1)}, bf16[384,1024]{1,0:T(8,128)(2,1)}, u32[]{:S(2)}, u32[]{:S(2)}) collective-permute-start(bf16[384,1024]{1,0:T(8,128)(2,1)} %get-tuple-element.26), channel_id=1, source_target_pairs={{2,0},{3,1},{4,2},{5,3},{6,4},{7,5},{8,6},{9,7},{10,8},{11,9},{12,... | collective-permute-start | bytes 2359304 | tf_op jit(solution)/shard_map/ppermute | solution.py:242
  99.1 14.8 %collective-permute-start.6 = (bf16[128,1024]{1,0:T(8,128)(2,1)S(1)}, bf16[128,1024]{1,0:T(8,128)(2,1)S(1)}, u32[]{:S(2)}, u32[]{:S(2)}) collective-permute-start(bf16[128,1024]{1,0:T(8,128)(2,1)S(1)} %get-tuple-element.20), channel_id=1, source_target_pairs={{0,2},{1,3},{2,4},{3,5},{4,6},{5,7},{6,8},{7,9},{8,10},{9,11},{10,... | collective-permute-start | bytes 786440 | tf_op jit(solution)/shard_map/ppermute | solution.py:242
  104.6 13.4 %collective-permute-start.5 = (bf16[128,1024]{1,0:T(8,128)(2,1)S(1)}, bf16[128,1024]{1,0:T(8,128)(2,1)S(1)}, u32[]{:S(2)}, u32[]{:S(2)}) collective-permute-start(bf16[128,1024]{1,0:T(8,128)(2,1)S(1)} %get-tuple-element.19), channel_id=1, source_target_pairs={{2,0},{3,1},{4,2},{5,3},{6,4},{7,5},{8,6},{9,7},{10,8},{11,9},{12,... | collective-permute-start | bytes 786440 | tf_op jit(solution)/shard_map/ppermute | solution.py:242
  118.1 11.9 %copy-start.3 = (bf16[384,1024]{1,0:T(8,128)(2,1)S(1)}, bf16[384,1024]{1,0:T(8,128)(2,1)}, u32[]{:S(2)}) copy-start(bf16[384,1024]{1,0:T(8,128)(2,1)} %copy-done.2) | copy-start | bytes 2359300
  118.9 27.6 %all-to-all-start.2 = ((bf16[16,48,256]{2,1,0:T(8,128)(2,1)}), bf16[16,48,256]{2,1,0:T(8,128)(2,1)S(1)}, u32[]{:S(2)}, u32[]{:S(2)}) async-start(bf16[16,48,256]{2,1,0:T(8,128)(2,1)} %bitcast.20), calls=%async_computation.2 | async-start | bytes 786432 | tf_op jit(solution)/shard_map/all_to_all | solution.py:239
  131.9 19.8 %collective-permute-start.9 = (bf16[288,1024]{1,0:T(8,128)(2,1)S(1)}, bf16[288,1024]{1,0:T(8,128)(2,1)S(1)}, u32[]{:S(2)}, u32[]{:S(2)}) collective-permute-start(bf16[288,1024]{1,0:T(8,128)(2,1)S(1)} %pad_maximum_fusion.2), channel_id=1, source_target_pairs={{0,1},{1,0},{2,3},{3,2},{4,5},{5,4},{6,7},{7,6},{8,9},{9,8},{10,11... | collective-permute-start | bytes 1769480 | tf_op jit(solution)/shard_map/ppermute | solution.py:247
  147.8 21.7 %all-to-all-start.3 = ((bf16[32,24,256]{2,1,0:T(8,128)(2,1)}), bf16[32,24,256]{2,1,0:T(8,128)(2,1)S(1)}, u32[]{:S(2)}, u32[]{:S(2)}) async-start(bf16[32,24,256]{2,1,0:T(8,128)(2,1)} %bitcast.21), calls=%async_computation.3 | async-start | bytes 786432 | tf_op jit(solution)/shard_map/all_to_all | solution.py:234

commit v3 on v2

--- a/solution.py
+++ b/solution.py
@@ -318,24 +318,21 @@
     grads = assemble(grads, runs, spreads, group)
 
     from_after, from_before = shift(audio_tb, -2), shift(audio_ta, 2)
-    grad_akv = (
-        audio_th.astype(f32) + from_after.astype(f32) + from_before.astype(f32)
-    ).astype(bf)
+    grad_akv = (audio_th.astype(f32) + from_after.astype(f32) + from_before.astype(f32)).astype(bf)
     mine = (
         grad_aq[:audio_rows],
         grad_akv[:audio_rows],
         grad_akv[2 * audio_rows : 3 * audio_rows],
     )
-    back = swap(
-        jnp.concatenate(
-            [
-                grad_aq[audio_rows:],
-                grad_akv[audio_rows : 2 * audio_rows],
-                grad_akv[3 * audio_rows :],
-            ],
-            axis=0,
-        )
-    )
+    back = jnp.concatenate(
+        [
+            grad_aq[audio_rows:],
+            grad_akv[audio_rows : 2 * audio_rows],
+            grad_akv[3 * audio_rows :],
+        ],
+        axis=0,
+    )
+    back = swap(back)
 
     def whole(own, other):
         return jnp.where(

time: 171 us -> 171 us (level)
  no operation moved by 1% of the time
where the time goes in v3:
time: 171 us; the launch traced here: 170 us
  waiting for transfers between devices  79.5 us (46%)
  starting transfers between devices  64.6 us (38%)
  Pallas kernels  14.3 us (8%)
  other arithmetic  6.24 us (4%)
  local copies, waits for them, and re-layouts  4.63 us (3%)
    all_to_all x2, waiting for transfers between devices, pair_exchange(): lax.all_to_all(x, ('frame', 'seq'), split_axis=0, concat_axis=0, tiled=Tr...  32.3 us
    all_to_all x2, waiting for transfers between devices, exchange(): return lax.all_to_all(x, 'frame', split_axis=0, concat_axis=0, tiled=True)  28.5 us
    ppermute x8, starting transfers between devices, shift(): lax.ppermute(x, 'seq', [(i, i + by) for i in range(count) if 0 <= i + by...  24.9 us
    all_to_all x2, starting transfers between devices, pair_exchange(): lax.all_to_all(x, ('frame', 'seq'), split_axis=0, concat_axis=0, tiled=Tr...  19.9 us
    ppermute x8, waiting for transfers between devices, shift(): lax.ppermute(x, 'seq', [(i, i + by) for i in range(count) if 0 <= i + by...  18.6 us
    all_to_all x2, starting transfers between devices, exchange(): return lax.all_to_all(x, 'frame', split_axis=0, concat_axis=0, tiled=True)  15.7 us
    pallas_call x2, Pallas kernels, side(): pl.pallas_call(kernel, grid=(width // wide,), in_specs=[SCALARS] + specs,...  13.6 us
    ppermute x2, starting transfers between devices, swap(): return lax.ppermute(x, 'seq', [(i, i ^ 1) for i in range(count)])  4.1 us
  transfers between devices with their start and end apart: 14, of which 8 were waited for; matrix products, arithmetic and copies ran while one was open for 5% of the time, Pallas kernels for 8%

profile of v3, /device:TPU:6, one launch (start us, length us, event | category | flops | bytes accessed | tf_op | source)
XLA Modules:
  0.0 170.3 jit_solution(2168027836338975300)
XLA Ops:
  0.6 1.9 %pad_maximum_fusion.3 = bf16[128,2048]{1,0:T(8,128)(2,1)} fusion(bf16[32,2048]{1,0:T(8,128)(2,1)} %bitcast.52, bf16[32,2048]{1,0:T(8,128)(2,1)} %bitcast.53, bf16[32,2048]{1,0:T(8,128)(2,1)} %bitcast.54, bf16[32,2048]{1,0:T(8,128)(2,1)} %bitcast.55), kind=kLoop, calls=%fused_computation.6 | loop fusion | flops 2097152 | bytes 1048576 | tf_op jit(solution)/shard_map/concatenate | solution.py:254
  2.6 16.1 %all-to-all-start = ((bf16[32,8,1024]{2,1,0:T(8,128)(2,1)}), bf16[32,8,1024]{2,1,0:T(8,128)(2,1)S(1)}, u32[]{:S(2)}, u32[]{:S(2)}) async-start(bf16[32,8,1024]{2,1,0:T(8,128)(2,1)} %bitcast.6), calls=%async_computation | async-start | bytes 1048576 | tf_op jit(solution)/shard_map/all_to_all | solution.py:234
  18.8 0.9 copy-done.6
  19.9 2.2 %collective-permute-start = (bf16[384,1024]{1,0:T(8,128)(2,1)S(1)}, bf16[384,1024]{1,0:T(8,128)(2,1)S(1)}, u32[]{:S(2)}, u32[]{:S(2)}) collective-permute-start(bf16[384,1024]{1,0:T(8,128)(2,1)S(1)} %pad_maximum_fusion), channel_id=1, source_target_pairs={{0,1},{1,0},{2,3},{3,2},{4,5},{5,4},{6,7},{7,6},{8,9},{9,8},{10,11... | collective-permute-start | bytes 2359304 | tf_op jit(solution)/shard_map/ppermute | solution.py:247
  22.2 16.6 %all-to-all-done = bf16[32,8,1024]{2,1,0:T(8,128)(2,1)S(1)} async-done(((bf16[32,8,1024]{2,1,0:T(8,128)(2,1)}), bf16[32,8,1024]{2,1,0:T(8,128)(2,1)S(1)}, u32[]{:S(2)}, u32[]{:S(2)}) %all-to-all-start) | async-done | bytes 524320 | tf_op jit(solution)/shard_map/all_to_all | solution.py:234
  38.8 1.4 gather_fusion
  40.2 4.6 %all-to-all-start.1 = ((bf16[16,16,1024]{2,1,0:T(8,128)(2,1)}), bf16[16,16,1024]{2,1,0:T(8,128)(2,1)S(1)}, u32[]{:S(2)}, u32[]{:S(2)}) async-start(bf16[16,16,1024]{2,1,0:T(8,128)(2,1)} %gather_fusion), calls=%async_computation.1 | async-start | bytes 1048576 | tf_op jit(solution)/shard_map/all_to_all | solution.py:239
  44.9 3.3 %collective-permute-start.1 = (bf16[384,1024]{1,0:T(8,128)(2,1)S(1)}, bf16[384,1024]{1,0:T(8,128)(2,1)}, u32[]{:S(2)}, u32[]{:S(2)}) collective-permute-start(bf16[384,1024]{1,0:T(8,128)(2,1)S(1)} %pad_maximum_fusion.1.here), channel_id=1, source_target_pairs={{0,2},{1,3},{2,4},{3,5},{4,6},{5,7},{6,8},{7,9},{8,10},{9,11},{10,... | collective-permute-start | bytes 2359304 | tf_op jit(solution)/shard_map/ppermute | solution.py:242
  48.2 2.5 %collective-permute-start.2 = (bf16[384,1024]{1,0:T(8,128)(2,1)S(1)}, bf16[384,1024]{1,0:T(8,128)(2,1)}, u32[]{:S(2)}, u32[]{:S(2)}) collective-permute-start(bf16[384,1024]{1,0:T(8,128)(2,1)S(1)} %pad_maximum_fusion.1.here), channel_id=1, source_target_pairs={{2,0},{3,1},{4,2},{5,3},{6,4},{7,5},{8,6},{9,7},{10,8},{11,9},{12,... | collective-permute-start | bytes 2359304 | tf_op jit(solution)/shard_map/ppermute | solution.py:242
  50.8 15.8 %all-to-all-done.1 = bf16[16,16,1024]{2,1,0:T(8,128)(2,1)S(1)} async-done(((bf16[16,16,1024]{2,1,0:T(8,128)(2,1)}), bf16[16,16,1024]{2,1,0:T(8,128)(2,1)S(1)}, u32[]{:S(2)}, u32[]{:S(2)}) %all-to-all-start.1) | async-done | bytes 524320 | tf_op jit(solution)/shard_map/all_to_all | solution.py:239
  66.6 3.3 %collective-permute-start.3 = (bf16[128,1024]{1,0:T(8,128)(2,1)S(1)}, bf16[128,1024]{1,0:T(8,128)(2,1)S(1)}, u32[]{:S(2)}, u32[]{:S(2)}) collective-permute-start(bf16[128,1024]{1,0:T(8,128)(2,1)S(1)} %bitcast.47), channel_id=1, source_target_pairs={{0,2},{1,3},{2,4},{3,5},{4,6},{5,7},{6,8},{7,9},{8,10},{9,11},{10,... | collective-permute-start | bytes 786440 | tf_op jit(solution)/shard_map/ppermute | solution.py:242
  70.0 2.5 %collective-permute-start.4 = (bf16[128,1024]{1,0:T(8,128)(2,1)S(1)}, bf16[128,1024]{1,0:T(8,128)(2,1)S(1)}, u32[]{:S(2)}, u32[]{:S(2)}) collective-permute-start(bf16[128,1024]{1,0:T(8,128)(2,1)S(1)} %bitcast.48), channel_id=1, source_target_pairs={{2,0},{3,1},{4,2},{5,3},{6,4},{7,5},{8,6},{9,7},{10,8},{11,9},{12,... | collective-permute-start | bytes 786440 | tf_op jit(solution)/shard_map/ppermute | solution.py:242
  72.5 3.9 %collective-permute-done.1.before = bf16[384,1024]{1,0:T(8,128)(2,1)} collective-permute-done((bf16[384,1024]{1,0:T(8,128)(2,1)S(1)}, bf16[384,1024]{1,0:T(8,128)(2,1)}, u32[]{:S(2)}, u32[]{:S(2)}) %collective-permute-start.1) | collective-permute-done | bytes 786464 | tf_op jit(solution)/shard_map/ppermute | solution.py:242
  76.4 3.3 %collective-permute-done.2.after = bf16[384,1024]{1,0:T(8,128)(2,1)} collective-permute-done((bf16[384,1024]{1,0:T(8,128)(2,1)S(1)}, bf16[384,1024]{1,0:T(8,128)(2,1)}, u32[]{:S(2)}, u32[]{:S(2)}) %collective-permute-start.2) | collective-permute-done | bytes 786464 | tf_op jit(solution)/shard_map/ppermute | solution.py:242
  79.7 7.4 %shard_map.145 = (bf16[64,1024]{1,0:T(8,128)(2,1)S(1)}, bf16[384,1024]{1,0:T(8,128)(2,1)}, bf16[384,1024]{1,0:T(8,128)(2,1)S(1)}, bf16[384,1024]{1,0:T(8,128)(2,1)}) custom-call(s32[16,32]{1,0:T(8,128)S(1)} %copy-done.4, bf16[256,1024]{1,0:T(8,128)(2,1)S(1)} %bitcast.43, bf16[256,1024]{1,0:T(8,128)(2,1)S(1)} %bitcast.44, ...), custom_call_target="tpu_custom_call" | custom-call | flops 377487360 | bytes 5242880 | tf_op jit(solution)/shard_map/pallas_call | solution.py:170
  87.1 3.3 %collective-permute-start.8 = (bf16[384,1024]{1,0:T(8,128)(2,1)}, bf16[384,1024]{1,0:T(8,128)(2,1)}, u32[]{:S(2)}, u32[]{:S(2)}) collective-permute-start(bf16[384,1024]{1,0:T(8,128)(2,1)} %get-tuple-element.27), channel_id=1, source_target_pairs={{0,2},{1,3},{2,4},{3,5},{4,6},{5,7},{6,8},{7,9},{8,10},{9,11},{10,... | collective-permute-start | bytes 2359304 | tf_op jit(solution)/shard_map/ppermute | solution.py:242
  90.4 2.5 %collective-permute-start.7 = (bf16[384,1024]{1,0:T(8,128)(2,1)}, bf16[384,1024]{1,0:T(8,128)(2,1)}, u32[]{:S(2)}, u32[]{:S(2)}) collective-permute-start(bf16[384,1024]{1,0:T(8,128)(2,1)} %get-tuple-element.26), channel_id=1, source_target_pairs={{2,0},{3,1},{4,2},{5,3},{6,4},{7,5},{8,6},{9,7},{10,8},{11,9},{12,... | collective-permute-start | bytes 2359304 | tf_op jit(solution)/shard_map/ppermute | solution.py:242
  93.0 6.1 %shard_map.146 = (bf16[192,1024]{1,0:T(8,128)(2,1)S(1)}, bf16[128,1024]{1,0:T(8,128)(2,1)S(1)}, bf16[128,1024]{1,0:T(8,128)(2,1)S(1)}, bf16[128,1024]{1,0:T(8,128)(2,1)S(1)}) custom-call(s32[16,32]{1,0:T(8,128)S(1)} %copy-done.4, bf16[96,2048]{1,0:T(8,128)(2,1)S(1)} %bitcast.45, bf16[96,2048]{1,0:T(8,128)(2,1)S(1)} %bitcast.46, ...), custom_call_target="tpu_custom_call" | custom-call | flops 377487360 | bytes 3145728 | tf_op jit(solution)/shard_map/pallas_call | solution.py:170
  99.1 5.4 %collective-permute-start.6 = (bf16[128,1024]{1,0:T(8,128)(2,1)S(1)}, bf16[128,1024]{1,0:T(8,128)(2,1)S(1)}, u32[]{:S(2)}, u32[]{:S(2)}) collective-permute-start(bf16[128,1024]{1,0:T(8,128)(2,1)S(1)} %get-tuple-element.20), channel_id=1, source_target_pairs={{0,2},{1,3},{2,4},{3,5},{4,6},{5,7},{6,8},{7,9},{8,10},{9,11},{10,... | collective-permute-start | bytes 786440 | tf_op jit(solution)/shard_map/ppermute | solution.py:242
  104.6 1.9 %collective-permute-start.5 = (bf16[128,1024]{1,0:T(8,128)(2,1)S(1)}, bf16[128,1024]{1,0:T(8,128)(2,1)S(1)}, u32[]{:S(2)}, u32[]{:S(2)}) collective-permute-start(bf16[128,1024]{1,0:T(8,128)(2,1)S(1)} %get-tuple-element.19), channel_id=1, source_target_pairs={{2,0},{3,1},{4,2},{5,3},{6,4},{7,5},{8,6},{9,7},{10,8},{11,9},{12,... | collective-permute-start | bytes 786440 | tf_op jit(solution)/shard_map/ppermute | solution.py:242
  106.5 7.4 %collective-permute-done.6 = bf16[128,1024]{1,0:T(8,128)(2,1)S(1)} collective-permute-done((bf16[128,1024]{1,0:T(8,128)(2,1)S(1)}, bf16[128,1024]{1,0:T(8,128)(2,1)S(1)}, u32[]{:S(2)}, u32[]{:S(2)}) %collective-permute-start.6) | collective-permute-done | bytes 262176 | tf_op jit(solution)/shard_map/ppermute | solution.py:242
  113.9 4.0 %collective-permute-done.5 = bf16[128,1024]{1,0:T(8,128)(2,1)S(1)} collective-permute-done((bf16[128,1024]{1,0:T(8,128)(2,1)S(1)}, bf16[128,1024]{1,0:T(8,128)(2,1)S(1)}, u32[]{:S(2)}, u32[]{:S(2)}) %collective-permute-start.5) | collective-permute-done | bytes 262176 | tf_op jit(solution)/shard_map/ppermute | solution.py:242
  118.1 0.8 copy.17
  118.9 11.1 %all-to-all-start.2 = ((bf16[16,48,256]{2,1,0:T(8,128)(2,1)}), bf16[16,48,256]{2,1,0:T(8,128)(2,1)S(1)}, u32[]{:S(2)}, u32[]{:S(2)}) async-start(bf16[16,48,256]{2,1,0:T(8,128)(2,1)} %bitcast.20), calls=%async_computation.2 | async-start | bytes 786432 | tf_op jit(solution)/shard_map/all_to_all | solution.py:239
  130.0 1.8 %add_convert_fusion = bf16[384,1024]{1,0:T(8,128)(2,1)S(1)} fusion(bf16[384,1024]{1,0:T(8,128)(2,1)} %collective-permute-done.8, bf16[384,1024]{1,0:T(8,128)(2,1)} %collective-permute-done.7, bf16[384,1024]{1,0:T(8,128)(2,1)S(1)} %copy-done.3), kind=kLoop, calls=%fused_computation.2 | loop fusion | flops 2359296 | bytes 3145728 | tf_op jit(solution)/shard_map/convert_element_type | solution.py:321
  131.9 1.9 %collective-permute-start.9 = (bf16[288,1024]{1,0:T(8,128)(2,1)S(1)}, bf16[288,1024]{1,0:T(8,128)(2,1)S(1)}, u32[]{:S(2)}, u32[]{:S(2)}) collective-permute-start(bf16[288,1024]{1,0:T(8,128)(2,1)S(1)} %pad_maximum_fusion.2), channel_id=1, source_target_pairs={{0,1},{1,0},{2,3},{3,2},{4,5},{5,4},{6,7},{7,6},{8,9},{9,8},{10,11... | collective-permute-start | bytes 1769480 | tf_op jit(solution)/shard_map/ppermute | solution.py:247
  133.9 12.7 %all-to-all-done.2 = bf16[16,48,256]{2,1,0:T(8,128)(2,1)S(1)} async-done(((bf16[16,48,256]{2,1,0:T(8,128)(2,1)}), bf16[16,48,256]{2,1,0:T(8,128)(2,1)S(1)}, u32[]{:S(2)}, u32[]{:S(2)}) %all-to-all-start.2) | async-done | bytes 393248 | tf_op jit(solution)/shard_map/all_to_all | solution.py:239
  146.5 1.3 gather_fusion.1
  147.8 3.9 %all-to-all-start.3 = ((bf16[32,24,256]{2,1,0:T(8,128)(2,1)}), bf16[32,24,256]{2,1,0:T(8,128)(2,1)S(1)}, u32[]{:S(2)}, u32[]{:S(2)}) async-start(bf16[32,24,256]{2,1,0:T(8,128)(2,1)} %bitcast.21), calls=%async_computation.3 | async-start | bytes 786432 | tf_op jit(solution)/shard_map/all_to_all | solution.py:234
  151.8 0.8 maximum_select_fusion.2
  152.6 1.2 maximum_select_fusion
  153.8 15.7 %all-to-all-done.3.x = bf16[32,24,256]{2,1,0:T(8,128)(2,1)S(1)} async-done(((bf16[32,24,256]{2,1,0:T(8,128)(2,1)}), bf16[32,24,256]{2,1,0:T(8,128)(2,1)S(1)}, u32[]{:S(2)}, u32[]{:S(2)}) %all-to-all-start.3) | async-done | bytes 393248 | tf_op jit(solution)/shard_map/all_to_all | solution.py:234
  (39 shorter events, 1.6 us)
Async XLA Ops:
  2.6 16.1 %copy-start.1 = (bf16[1,96,2048]{2,1,0:T(8,128)(2,1)S(1)}, bf16[1,96,2048]{2,1,0:T(8,128)(2,1)}, u32[]{:S(2)}) copy-start(bf16[1,96,2048]{2,1,0:T(8,128)(2,1)} %param.17) | copy-start | bytes 1179652
  2.6 16.1 %copy-start.5 = (bf16[1,96,2048]{2,1,0:T(8,128)(2,1)S(1)}, bf16[1,96,2048]{2,1,0:T(8,128)(2,1)}, u32[]{:S(2)}) copy-start(bf16[1,96,2048]{2,1,0:T(8,128)(2,1)} %param.16) | copy-start | bytes 1179652
  2.6 36.2 %all-to-all-start = ((bf16[32,8,1024]{2,1,0:T(8,128)(2,1)}), bf16[32,8,1024]{2,1,0:T(8,128)(2,1)S(1)}, u32[]{:S(2)}, u32[]{:S(2)}) async-start(bf16[32,8,1024]{2,1,0:T(8,128)(2,1)} %bitcast.6), calls=%async_computation | async-start | bytes 1048576 | tf_op jit(solution)/shard_map/all_to_all | solution.py:234
  18.6 1.0 copy-start.6
  18.7 1.1 copy-start
  19.8 2.3 %copy-start.7 = (s32[16]{0:T(128)S(1)}, s32[16]{0:T(128)}, u32[]{:S(2)}) copy-start(s32[16]{0:T(128)} %param.19) | copy-start | bytes 196
  19.9 24.9 %collective-permute-start = (bf16[384,1024]{1,0:T(8,128)(2,1)S(1)}, bf16[384,1024]{1,0:T(8,128)(2,1)S(1)}, u32[]{:S(2)}, u32[]{:S(2)}) collective-permute-start(bf16[384,1024]{1,0:T(8,128)(2,1)S(1)} %pad_maximum_fusion), channel_id=1, source_target_pairs={{0,1},{1,0},{2,3},{3,2},{4,5},{5,4},{6,7},{7,6},{8,9},{9,8},{10,11... | collective-permute-start | bytes 2359304 | tf_op jit(solution)/shard_map/ppermute | solution.py:247
  40.2 26.4 %all-to-all-start.1 = ((bf16[16,16,1024]{2,1,0:T(8,128)(2,1)}), bf16[16,16,1024]{2,1,0:T(8,128)(2,1)S(1)}, u32[]{:S(2)}, u32[]{:S(2)}) async-start(bf16[16,16,1024]{2,1,0:T(8,128)(2,1)} %gather_fusion), calls=%async_computation.1 | async-start | bytes 1048576 | tf_op jit(solution)/shard_map/all_to_all | solution.py:239
  44.8 34.8 %copy-start.4 = (s32[16,32]{1,0:T(8,128)S(1)}, s32[16,32]{1,0:T(8,128)}, u32[]{:S(2)}) copy-start(s32[16,32]{1,0:T(8,128)} %lens.3) | copy-start | bytes 6148
  44.9 31.5 %collective-permute-start.1 = (bf16[384,1024]{1,0:T(8,128)(2,1)S(1)}, bf16[384,1024]{1,0:T(8,128)(2,1)}, u32[]{:S(2)}, u32[]{:S(2)}) collective-permute-start(bf16[384,1024]{1,0:T(8,128)(2,1)S(1)} %pad_maximum_fusion.1.here), channel_id=1, source_target_pairs={{0,2},{1,3},{2,4},{3,5},{4,6},{5,7},{6,8},{7,9},{8,10},{9,11},{10,... | collective-permute-start | bytes 2359304 | tf_op jit(solution)/shard_map/ppermute | solution.py:242
  48.2 31.4 %collective-permute-start.2 = (bf16[384,1024]{1,0:T(8,128)(2,1)S(1)}, bf16[384,1024]{1,0:T(8,128)(2,1)}, u32[]{:S(2)}, u32[]{:S(2)}) collective-permute-start(bf16[384,1024]{1,0:T(8,128)(2,1)S(1)} %pad_maximum_fusion.1.here), channel_id=1, source_target_pairs={{2,0},{3,1},{4,2},{5,3},{6,4},{7,5},{8,6},{9,7},{10,8},{11,9},{12,... | collective-permute-start | bytes 2359304 | tf_op jit(solution)/shard_map/ppermute | solution.py:242
  66.6 26.3 %collective-permute-start.3 = (bf16[128,1024]{1,0:T(8,128)(2,1)S(1)}, bf16[128,1024]{1,0:T(8,128)(2,1)S(1)}, u32[]{:S(2)}, u32[]{:S(2)}) collective-permute-start(bf16[128,1024]{1,0:T(8,128)(2,1)S(1)} %bitcast.47), channel_id=1, source_target_pairs={{0,2},{1,3},{2,4},{3,5},{4,6},{5,7},{6,8},{7,9},{8,10},{9,11},{10,... | collective-permute-start | bytes 786440 | tf_op jit(solution)/shard_map/ppermute | solution.py:242
  70.0 23.0 %collective-permute-start.4 = (bf16[128,1024]{1,0:T(8,128)(2,1)S(1)}, bf16[128,1024]{1,0:T(8,128)(2,1)S(1)}, u32[]{:S(2)}, u32[]{:S(2)}) collective-permute-start(bf16[128,1024]{1,0:T(8,128)(2,1)S(1)} %bitcast.48), channel_id=1, source_target_pairs={{2,0},{3,1},{4,2},{5,3},{6,4},{7,5},{8,6},{9,7},{10,8},{11,9},{12,... | collective-permute-start | bytes 786440 | tf_op jit(solution)/shard_map/ppermute | solution.py:242
  87.1 12.0 %copy-start.2 = (bf16[384,1024]{1,0:T(8,128)(2,1)}, bf16[384,1024]{1,0:T(8,128)(2,1)S(1)}, u32[]{:S(2)}) copy-start(bf16[384,1024]{1,0:T(8,128)(2,1)S(1)} %get-tuple-element.25) | copy-start | bytes 2359300
  87.1 42.9 %collective-permute-start.8 = (bf16[384,1024]{1,0:T(8,128)(2,1)}, bf16[384,1024]{1,0:T(8,128)(2,1)}, u32[]{:S(2)}, u32[]{:S(2)}) collective-permute-start(bf16[384,1024]{1,0:T(8,128)(2,1)} %get-tuple-element.27), channel_id=1, source_target_pairs={{0,2},{1,3},{2,4},{3,5},{4,6},{5,7},{6,8},{7,9},{8,10},{9,11},{10,... | collective-permute-start | bytes 2359304 | tf_op jit(solution)/shard_map/ppermute | solution.py:242
  90.4 39.6 %collective-permute-start.7 = (bf16[384,1024]{1,0:T(8,128)(2,1)}, bf16[384,1024]{1,0:T(8,128)(2,1)}, u32[]{:S(2)}, u32[]{:S(2)}) collective-permute-start(bf16[384,1024]{1,0:T(8,128)(2,1)} %get-tuple-element.26), channel_id=1, source_target_pairs={{2,0},{3,1},{4,2},{5,3},{6,4},{7,5},{8,6},{9,7},{10,8},{11,9},{12,... | collective-permute-start | bytes 2359304 | tf_op jit(solution)/shard_map/ppermute | solution.py:242
  99.1 14.8 %collective-permute-start.6 = (bf16[128,1024]{1,0:T(8,128)(2,1)S(1)}, bf16[128,1024]{1,0:T(8,128)(2,1)S(1)}, u32[]{:S(2)}, u32[]{:S(2)}) collective-permute-start(bf16[128,1024]{1,0:T(8,128)(2,1)S(1)} %get-tuple-element.20), channel_id=1, source_target_pairs={{0,2},{1,3},{2,4},{3,5},{4,6},{5,7},{6,8},{7,9},{8,10},{9,11},{10,... | collective-permute-start | bytes 786440 | tf_op jit(solution)/shard_map/ppermute | solution.py:242
  104.6 13.4 %collective-permute-start.5 = (bf16[128,1024]{1,0:T(8,128)(2,1)S(1)}, bf16[128,1024]{1,0:T(8,128)(2,1)S(1)}, u32[]{:S(2)}, u32[]{:S(2)}) collective-permute-start(bf16[128,1024]{1,0:T(8,128)(2,1)S(1)} %get-tuple-element.19), channel_id=1, source_target_pairs={{2,0},{3,1},{4,2},{5,3},{6,4},{7,5},{8,6},{9,7},{10,8},{11,9},{12,... | collective-permute-start | bytes 786440 | tf_op jit(solution)/shard_map/ppermute | solution.py:242
  118.1 11.9 %copy-start.3 = (bf16[384,1024]{1,0:T(8,128)(2,1)S(1)}, bf16[384,1024]{1,0:T(8,128)(2,1)}, u32[]{:S(2)}) copy-start(bf16[384,1024]{1,0:T(8,128)(2,1)} %copy-done.2) | copy-start | bytes 2359300
  118.9 27.6 %all-to-all-start.2 = ((bf16[16,48,256]{2,1,0:T(8,128)(2,1)}), bf16[16,48,256]{2,1,0:T(8,128)(2,1)S(1)}, u32[]{:S(2)}, u32[]{:S(2)}) async-start(bf16[16,48,256]{2,1,0:T(8,128)(2,1)} %bitcast.20), calls=%async_computation.2 | async-start | bytes 786432 | tf_op jit(solution)/shard_map/all_to_all | solution.py:239
  131.9 19.8 %collective-permute-start.9 = (bf16[288,1024]{1,0:T(8,128)(2,1)S(1)}, bf16[288,1024]{1,0:T(8,128)(2,1)S(1)}, u32[]{:S(2)}, u32[]{:S(2)}) collective-permute-start(bf16[288,1024]{1,0:T(8,128)(2,1)S(1)} %pad_maximum_fusion.2), channel_id=1, source_target_pairs={{0,1},{1,0},{2,3},{3,2},{4,5},{5,4},{6,7},{7,6},{8,9},{9,8},{10,11... | collective-permute-start | bytes 1769480 | tf_op jit(solution)/shard_map/ppermute | solution.py:247
  147.8 21.7 %all-to-all-start.3 = ((bf16[32,24,256]{2,1,0:T(8,128)(2,1)}), bf16[32,24,256]{2,1,0:T(8,128)(2,1)S(1)}, u32[]{:S(2)}, u32[]{:S(2)}) async-start(bf16[32,24,256]{2,1,0:T(8,128)(2,1)} %bitcast.21), calls=%async_computation.3 | async-start | bytes 786432 | tf_op jit(solution)/shard_map/all_to_all | solution.py:234

commit v4 on v3

--- a/solution.py
+++ b/solution.py
@@ -12,43 +12,58 @@
 BAND = 2
 NEG_BIG = -1e30
 FACTOR = HD ** (-0.5)
-HEADS_PER_STEP = 2
+HEADS_PER_STEP = 4
 INTERPRET = False
 
 
+def contract(left, right, left_dim, right_dim):
+    return lax.dot_general(
+        left,
+        right,
+        (((left_dim,), (right_dim,)), ((), ())),
+        preferred_element_type=jnp.float32,
+    )
+
+
 def attend(queries, keys, values, grads, bias):
-    scores = (
-        lax.dot_general(
-            queries, keys, (((1,), (1,)), ((), ())), preferred_element_type=jnp.float32
-        )
-        * FACTOR
-    )
-    scores = scores + bias
-    largest = jnp.max(scores, axis=-1, keepdims=True)
-    exponent = jnp.exp(scores - largest)
-    weights = exponent * (1.0 / jnp.sum(exponent, axis=-1, keepdims=True))
-    half = weights.astype(jnp.bfloat16)
-    grad_weights = lax.dot_general(
-        grads, values, (((1,), (1,)), ((), ())), preferred_element_type=jnp.float32
-    )
-    delta = jnp.sum(half.astype(jnp.float32) * grad_weights, axis=-1, keepdims=True)
-    grad_scores = (weights * (grad_weights - delta)).astype(jnp.bfloat16)
-    grad_query = (
-        lax.dot_general(
-            grad_scores, keys, (((1,), (0,)), ((), ())), preferred_element_type=jnp.float32
-        )
-        * FACTOR
-    )
-    key_terms = (
-        lax.dot_general(
-            grad_scores, queries, (((0,), (0,)), ((), ())), preferred_element_type=jnp.float32
-        )
-        * FACTOR
-    )
-    value_terms = lax.dot_general(
-        half, grads, (((0,), (0,)), ((), ())), preferred_element_type=jnp.float32
-    )
+    total = range(len(queries))
+    scores = [contract(queries[h], keys[h], 1, 1) * FACTOR + bias[...] for h in total]
+    largest = [jnp.max(scores[h], axis=-1, keepdims=True) for h in total]
+    exponent = [jnp.exp(scores[h] - largest[h]) for h in total]
+    inverse = [1.0 / jnp.sum(exponent[h], axis=-1, keepdims=True) for h in total]
+    weights = [exponent[h] * inverse[h] for h in total]
+    half = [weights[h].astype(jnp.bfloat16) for h in total]
+    grad_weights = [contract(grads[h], values[h], 1, 1) for h in total]
+    delta = [
+        jnp.sum(half[h].astype(jnp.float32) * grad_weights[h], axis=-1, keepdims=True)
+        for h in total
+    ]
+    grad_scores = [
+        (weights[h] * (grad_weights[h] - delta[h])).astype(jnp.bfloat16) for h in total
+    ]
+    value_terms = [contract(half[h], grads[h], 0, 0) for h in total]
+    grad_query = [contract(grad_scores[h], keys[h], 1, 0) * FACTOR for h in total]
+    key_terms = [contract(grad_scores[h], queries[h], 0, 0) * FACTOR for h in total]
     return grad_query, key_terms, value_terms
+
+
+def windows(refs, part, cols):
+    keys = jnp.concatenate([ref[:part, cols] for ref in refs], axis=0)
+    values = jnp.concatenate([ref[part:, cols] for ref in refs], axis=0)
+    return keys, values
+
+
+def write(results, spans, dq_ref, term_refs, part):
+    for cols, dq, kt, vt in zip(spans, *results, strict=True):
+        dq_ref[:, cols] = dq.astype(jnp.bfloat16)
+        for place, out in enumerate(term_refs):
+            rows = slice(place * part, (place + 1) * part)
+            out[:part, cols] = kt[rows].astype(jnp.bfloat16)
+            out[part:, cols] = vt[rows].astype(jnp.bfloat16)
+
+
+def head_spans(wide):
+    return [slice(h * HD, (h + 1) * HD) for h in range(wide // HD)]
 
 
 def video_kernel(group, count, lens, queries, grads, before, here, after, dq_ref, tb, th, ta, bias):
@@ -58,19 +73,12 @@
     def _():
         video_bias(group, count, lens, part, bias)
 
-    def one(head):
-        cols = slice(head * HD, (head + 1) * HD)
-        keys = jnp.concatenate([ref[:part, cols] for ref in (before, here, after)], axis=0)
-        values = jnp.concatenate([ref[part:, cols] for ref in (before, here, after)], axis=0)
-        dq, kt, vt = attend(queries[:, cols], keys, values, grads[:, cols], bias[...])
-        dq_ref[:, cols] = dq.astype(jnp.bfloat16)
-        for place, out in enumerate((tb, th, ta)):
-            span = slice(place * part, (place + 1) * part)
-            out[:part, cols] = kt[span].astype(jnp.bfloat16)
-            out[part:, cols] = vt[span].astype(jnp.bfloat16)
-
-    for head in range(dq_ref.shape[1] // HD):
-        one(head)
+    spans = head_spans(dq_ref.shape[1])
+    keys, values = zip(*[windows((before, here, after), part, cols) for cols in spans])
+    results = attend(
+        [queries[:, cols] for cols in spans], keys, values, [grads[:, cols] for cols in spans], bias
+    )
+    write(results, spans, dq_ref, (tb, th, ta), part)
 
 
 def video_bias(group, count, lens, part, bias):
@@ -124,30 +132,20 @@
     live_mine = (slot < lens[frame, block]).astype(jnp.float32)
     live_other = (slot < lens[frame, other]).astype(jnp.float32)
 
-    def one(head):
-        cols = slice(head * HD, (head + 1) * HD)
+    spans = head_spans(wide)
+    queries, grads = [], []
+    for head, cols in enumerate(spans):
         start = core * half + pl.program_id(0) * wide + head * HD
         mine = pl.ds(pl.multiple_of(start, HD), HD)
-        queries = jnp.concatenate([aud_q[:, mine], their_q[:, cols]], axis=0)
-        zero = jnp.zeros((), jnp.float32)
-        grads = jnp.concatenate(
-            [
-                jnp.where(live_mine > 0, aud_g[:, mine].astype(jnp.float32), zero),
-                jnp.where(live_other > 0, their_g[:, cols].astype(jnp.float32), zero),
-            ],
-            axis=0,
-        ).astype(jnp.bfloat16)
-        keys = jnp.concatenate([ref[:part, cols] for ref in (before, here, after)], axis=0)
-        values = jnp.concatenate([ref[part:, cols] for ref in (before, here, after)], axis=0)
-        dq, kt, vt = attend(queries, keys, values, grads, bias[...])
-        dq_ref[:, cols] = dq.astype(jnp.bfloat16)
-        for place, out in enumerate((tb, th, ta)):
-            span = slice(place * part, (place + 1) * part)
-            out[:part, cols] = kt[span].astype(jnp.bfloat16)
-            out[part:, cols] = vt[span].astype(jnp.bfloat16)
-
-    for head in range(wide // HD):
-        one(head)
+        queries.append(jnp.concatenate([aud_q[:, mine], their_q[:, cols]], axis=0))
+        kept = [
+            jnp.where(live > 0, rows_of.astype(jnp.float32), 0.0)
+            for live, rows_of in ((live_mine, aud_g[:, mine]), (live_other, their_g[:, cols]))
+        ]
+        grads.append(jnp.concatenate(kept, axis=0).astype(jnp.bfloat16))
+    keys, values = zip(*[windows((before, here, after), part, cols) for cols in spans])
+    results = attend(queries, keys, values, grads, bias)
+    write(results, spans, dq_ref, (tb, th, ta), part)
 
 
 def cost(rows, keys, width):
@@ -185,6 +183,27 @@
     return pl.BlockSpec((rows, wide), lambda h: (row, h))
 
 
+def place_kernel(spread, index, x, out):
+    for frame in range(x.shape[0]):
+        if spread:
+            out[index[frame]] = x[frame]
+        else:
+            out[frame] = x[index[frame]]
+
+
+def place(index, x, spread):
+    return pl.pallas_call(
+        functools.partial(place_kernel, spread),
+        in_specs=[SCALARS, ON_CHIP],
+        out_specs=pl.BlockSpec(x.shape, lambda: (0, 0, 0)),
+        out_shape=jax.ShapeDtypeStruct(x.shape, x.dtype),
+        compiler_params=pltpu.CompilerParams(vmem_limit_bytes=GRANT // 4),
+        cost_estimate=pl.CostEstimate(flops=0, bytes_accessed=4 * x.size, transcendentals=0),
+        name="place",
+        interpret=INTERPRET,
+    )(index, x)
+
+
 def assemble_kernel(runs, spreads, group, x, *outs):
     slim = x.shape[2]
     for run in range(runs):
@@ -246,15 +265,10 @@
     def swap(x):
         return lax.ppermute(x, "seq", [(i, i ^ 1) for i in range(count)])
 
-    order = jnp.arange(frames, dtype=jnp.int32)
-    inverse = jnp.sum(
-        jnp.where(match[None, :] == order[:, None], order[None, :], 0), axis=1
-    ).astype(jnp.int32)
-
     packed = jnp.concatenate([vid_q[0], vid_k[0], vid_v[0], vid_dout[0]], axis=0)
     packed = packed.reshape(frames, group, 2, half).transpose(0, 2, 1, 3)
     spread = pair_exchange(packed.reshape(2 * frames, group, half))
-    spread = jnp.take(spread.reshape(frames, 2 * group, half), inverse, axis=0, mode="clip")
+    spread = place(match, spread.reshape(frames, 2 * group, half), True)
     video = exchange(spread).reshape(frames * 2 * group, half)
 
     def halves(x):
@@ -305,15 +319,14 @@
         half,
     )
 
+    from_after, from_before = shift(video_tb, -2), shift(video_ta, 2)
     grad_vkv = (
-        video_th.astype(f32)
-        + shift(video_tb, -2).astype(f32)
-        + shift(video_ta, 2).astype(f32)
+        video_th.astype(f32) + from_after.astype(f32) + from_before.astype(f32)
     ).astype(bf)
     grads = jnp.concatenate([grad_vq, grad_vkv], axis=0)
     grads = grads.reshape(3, runs, 2, group, spreads, slim).transpose(1, 4, 2, 0, 3, 5)
     grads = exchange(grads.reshape(frames, 6 * group, slim))
-    grads = jnp.take(grads, match, axis=0, mode="clip")
+    grads = place(match, grads, False)
     grads = pair_exchange(grads.reshape(2 * frames, 3 * group, slim))
     grads = assemble(grads, runs, spreads, group)
 

time: 171 us -> 169 us (0.988); the launches traced: 170 us -> 166 us
  starting transfers between devices: 64.6 us -> 71.9 us
  waiting for transfers between devices: 79.5 us -> 73.9 us
  Pallas kernels: 14.3 us -> 11.3 us
  local copies, waits for them, and re-layouts: 4.63 us -> 1.95 us
    ppermute x8, starting transfers between devices: 24.9 us -> 32.4 us  [shift(): lax.ppermute(x, 'seq', [(i, i + by) for i in range(count) if 0 <= i + by...]
    pallas_call x2, Pallas kernels: 13.6 us -> 7.83 us  [side(): pl.pallas_call(kernel, grid=(width // wide,), in_specs=[SCALARS] + specs,...]
    ppermute x8, waiting for transfers between devices: 18.6 us -> 15 us  [shift(): lax.ppermute(x, 'seq', [(i, i + by) for i in range(count) if 0 <= i + by...]
    gather x2 -> x0, local copies, waits for them, and re-layouts: 2.68 us -> none  [the longest x1 1.37 us: shards(): jnp.take(spread.reshape(frames, 2 * group, half), inverse, axis=0, mode='...]
    pallas_call x0 -> x2, Pallas kernels: none -> 2.68 us  [place(): pl.pallas_call(functools.partial(place_kernel, spread), in_specs=[SCALARS...]
    all_to_all x2, waiting for transfers between devices: 28.5 us -> 26.4 us  [exchange(): return lax.all_to_all(x, 'frame', split_axis=0, concat_axis=0, tiled=True)]
  transfers between devices with their start and end apart: 14 -> 14, of which waited for: 8 -> 7; matrix products, arithmetic and copies ran while one was open for 5% -> 3% of each run, Pallas kernels for 8% -> 6%
where the time goes in v4:
time: 169 us; the launch traced here: 166 us
  waiting for transfers between devices  73.9 us (44%)
  starting transfers between devices  71.9 us (43%)
  Pallas kernels  11.3 us (7%)
  other arithmetic  6.11 us (4%)
  local copies, waits for them, and re-layouts  1.95 us (1%)
    all_to_all x2, waiting for transfers between devices, pair_exchange(): lax.all_to_all(x, ('frame', 'seq'), split_axis=0, concat_axis=0, tiled=Tr...  32.4 us
    ppermute x8, starting transfers between devices, shift(): lax.ppermute(x, 'seq', [(i, i + by) for i in range(count) if 0 <= i + by...  32.4 us
    all_to_all x2, waiting for transfers between devices, exchange(): return lax.all_to_all(x, 'frame', split_axis=0, concat_axis=0, tiled=True)  26.4 us
    all_to_all x2, starting transfers between devices, pair_exchange(): lax.all_to_all(x, ('frame', 'seq'), split_axis=0, concat_axis=0, tiled=Tr...  20.7 us
    ppermute x8, waiting for transfers between devices, shift(): lax.ppermute(x, 'seq', [(i, i + by) for i in range(count) if 0 <= i + by...  15 us
    all_to_all x2, starting transfers between devices, exchange(): return lax.all_to_all(x, 'frame', split_axis=0, concat_axis=0, tiled=True)  14.7 us
    pallas_call x2, Pallas kernels, side(): pl.pallas_call(kernel, grid=(width // wide,), in_specs=[SCALARS] + specs,...  7.83 us
    ppermute x2, starting transfers between devices, swap(): return lax.ppermute(x, 'seq', [(i, i ^ 1) for i in range(count)])  4.1 us
  transfers between devices with their start and end apart: 14, of which 7 were waited for; matrix products, arithmetic and copies ran while one was open for 3% of the time, Pallas kernels for 6%

profile of v4, /device:TPU:6, one launch (start us, length us, event | category | flops | bytes accessed | tf_op | source)
XLA Modules:
  0.0 166.1 jit_solution(16596617321437488899)
XLA Ops:
  0.6 1.9 %pad_maximum_fusion.3 = bf16[128,2048]{1,0:T(8,128)(2,1)} fusion(bf16[32,2048]{1,0:T(8,128)(2,1)} %bitcast.52, bf16[32,2048]{1,0:T(8,128)(2,1)} %bitcast.53, bf16[32,2048]{1,0:T(8,128)(2,1)} %bitcast.54, bf16[32,2048]{1,0:T(8,128)(2,1)} %bitcast.55), kind=kLoop, calls=%fused_computation.4 | loop fusion | flops 2097152 | bytes 1048576 | tf_op jit(solution)/shard_map/concatenate | solution.py:268
  2.6 16.1 %all-to-all-start = ((bf16[32,8,1024]{2,1,0:T(8,128)(2,1)}), bf16[32,8,1024]{2,1,0:T(8,128)(2,1)S(1)}, u32[]{:S(2)}, u32[]{:S(2)}) async-start(bf16[32,8,1024]{2,1,0:T(8,128)(2,1)} %bitcast.6), calls=%async_computation | async-start | bytes 1048576 | tf_op jit(solution)/shard_map/all_to_all | solution.py:253
  18.8 0.9 copy-done.7
  19.9 2.2 %collective-permute-start = (bf16[384,1024]{1,0:T(8,128)(2,1)S(1)}, bf16[384,1024]{1,0:T(8,128)(2,1)S(1)}, u32[]{:S(2)}, u32[]{:S(2)}) collective-permute-start(bf16[384,1024]{1,0:T(8,128)(2,1)S(1)} %pad_maximum_fusion), channel_id=1, source_target_pairs={{0,1},{1,0},{2,3},{3,2},{4,5},{5,4},{6,7},{7,6},{8,9},{9,8},{10,11... | collective-permute-start | bytes 2359304 | tf_op jit(solution)/shard_map/ppermute | solution.py:266
  22.1 16.7 %all-to-all-done = bf16[32,8,1024]{2,1,0:T(8,128)(2,1)S(1)} async-done(((bf16[32,8,1024]{2,1,0:T(8,128)(2,1)}), bf16[32,8,1024]{2,1,0:T(8,128)(2,1)S(1)}, u32[]{:S(2)}, u32[]{:S(2)}) %all-to-all-start) | async-done | bytes 524320 | tf_op jit(solution)/shard_map/all_to_all | solution.py:253
  38.8 1.4 place.2
  40.2 4.6 %all-to-all-start.1 = ((bf16[16,16,1024]{2,1,0:T(8,128)(2,1)}), bf16[16,16,1024]{2,1,0:T(8,128)(2,1)S(1)}, u32[]{:S(2)}, u32[]{:S(2)}) async-start(bf16[16,16,1024]{2,1,0:T(8,128)(2,1)} %place.2), calls=%async_computation.1 | async-start | bytes 1048576 | tf_op jit(solution)/shard_map/all_to_all | solution.py:258
  44.9 2.7 %collective-permute-start.2 = (bf16[384,1024]{1,0:T(8,128)(2,1)S(1)}, bf16[384,1024]{1,0:T(8,128)(2,1)}, u32[]{:S(2)}, u32[]{:S(2)}) collective-permute-start(bf16[384,1024]{1,0:T(8,128)(2,1)S(1)} %pad_maximum_fusion.1.here), channel_id=1, source_target_pairs={{2,0},{3,1},{4,2},{5,3},{6,4},{7,5},{8,6},{9,7},{10,8},{11,9},{12,... | collective-permute-start | bytes 2359304 | tf_op jit(solution)/shard_map/ppermute | solution.py:261
  47.7 5.2 %collective-permute-start.1 = (bf16[384,1024]{1,0:T(8,128)(2,1)S(1)}, bf16[384,1024]{1,0:T(8,128)(2,1)}, u32[]{:S(2)}, u32[]{:S(2)}) collective-permute-start(bf16[384,1024]{1,0:T(8,128)(2,1)S(1)} %pad_maximum_fusion.1.here), channel_id=1, source_target_pairs={{0,2},{1,3},{2,4},{3,5},{4,6},{5,7},{6,8},{7,9},{8,10},{9,11},{10,... | collective-permute-start | bytes 2359304 | tf_op jit(solution)/shard_map/ppermute | solution.py:261
  52.9 13.7 %all-to-all-done.1 = bf16[16,16,1024]{2,1,0:T(8,128)(2,1)S(1)} async-done(((bf16[16,16,1024]{2,1,0:T(8,128)(2,1)}), bf16[16,16,1024]{2,1,0:T(8,128)(2,1)S(1)}, u32[]{:S(2)}, u32[]{:S(2)}) %all-to-all-start.1) | async-done | bytes 524320 | tf_op jit(solution)/shard_map/all_to_all | solution.py:258
  66.6 2.7 %collective-permute-start.4 = (bf16[128,1024]{1,0:T(8,128)(2,1)S(1)}, bf16[128,1024]{1,0:T(8,128)(2,1)S(1)}, u32[]{:S(2)}, u32[]{:S(2)}) collective-permute-start(bf16[128,1024]{1,0:T(8,128)(2,1)S(1)} %bitcast.48), channel_id=1, source_target_pairs={{2,0},{3,1},{4,2},{5,3},{6,4},{7,5},{8,6},{9,7},{10,8},{11,9},{12,... | collective-permute-start | bytes 786440 | tf_op jit(solution)/shard_map/ppermute | solution.py:261
  69.4 5.2 %collective-permute-start.3 = (bf16[128,1024]{1,0:T(8,128)(2,1)S(1)}, bf16[128,1024]{1,0:T(8,128)(2,1)S(1)}, u32[]{:S(2)}, u32[]{:S(2)}) collective-permute-start(bf16[128,1024]{1,0:T(8,128)(2,1)S(1)} %bitcast.49), channel_id=1, source_target_pairs={{0,2},{1,3},{2,4},{3,5},{4,6},{5,7},{6,8},{7,9},{8,10},{9,11},{10,... | collective-permute-start | bytes 786440 | tf_op jit(solution)/shard_map/ppermute | solution.py:261
  74.6 3.9 %collective-permute-done.2.after = bf16[384,1024]{1,0:T(8,128)(2,1)} collective-permute-done((bf16[384,1024]{1,0:T(8,128)(2,1)S(1)}, bf16[384,1024]{1,0:T(8,128)(2,1)}, u32[]{:S(2)}, u32[]{:S(2)}) %collective-permute-start.2) | collective-permute-done | bytes 786464 | tf_op jit(solution)/shard_map/ppermute | solution.py:261
  78.5 4.8 %shard_map.145 = (bf16[64,1024]{1,0:T(8,128)(2,1)S(1)}, bf16[384,1024]{1,0:T(8,128)(2,1)}, bf16[384,1024]{1,0:T(8,128)(2,1)S(1)}, bf16[384,1024]{1,0:T(8,128)(2,1)}) custom-call(s32[16,32]{1,0:T(8,128)S(1)} %copy-done.4, bf16[256,1024]{1,0:T(8,128)(2,1)S(1)} %bitcast.43, bf16[256,1024]{1,0:T(8,128)(2,1)S(1)} %bitcast.44, ...), custom_call_target="tpu_custom_call" | custom-call | flops 377487360 | bytes 5242880 | tf_op jit(solution)/shard_map/pallas_call | solution.py:168
  83.3 1.9 %collective-permute-start.7 = (bf16[384,1024]{1,0:T(8,128)(2,1)}, bf16[384,1024]{1,0:T(8,128)(2,1)}, u32[]{:S(2)}, u32[]{:S(2)}) collective-permute-start(bf16[384,1024]{1,0:T(8,128)(2,1)} %get-tuple-element.26), channel_id=1, source_target_pairs={{2,0},{3,1},{4,2},{5,3},{6,4},{7,5},{8,6},{9,7},{10,8},{11,9},{12,... | collective-permute-start | bytes 2359304 | tf_op jit(solution)/shard_map/ppermute | solution.py:261
  85.2 6.6 %collective-permute-start.8 = (bf16[384,1024]{1,0:T(8,128)(2,1)}, bf16[384,1024]{1,0:T(8,128)(2,1)}, u32[]{:S(2)}, u32[]{:S(2)}) collective-permute-start(bf16[384,1024]{1,0:T(8,128)(2,1)} %get-tuple-element.27), channel_id=1, source_target_pairs={{0,2},{1,3},{2,4},{3,5},{4,6},{5,7},{6,8},{7,9},{8,10},{9,11},{10,... | collective-permute-start | bytes 2359304 | tf_op jit(solution)/shard_map/ppermute | solution.py:261
  91.9 3.1 %shard_map.146 = (bf16[192,1024]{1,0:T(8,128)(2,1)S(1)}, bf16[128,1024]{1,0:T(8,128)(2,1)S(1)}, bf16[128,1024]{1,0:T(8,128)(2,1)S(1)}, bf16[128,1024]{1,0:T(8,128)(2,1)S(1)}) custom-call(s32[16,32]{1,0:T(8,128)S(1)} %copy-done.4, bf16[96,2048]{1,0:T(8,128)(2,1)S(1)} %bitcast.46, bf16[96,2048]{1,0:T(8,128)(2,1)S(1)} %bitcast.47, ...), custom_call_target="tpu_custom_call" | custom-call | flops 377487360 | bytes 3145728 | tf_op jit(solution)/shard_map/pallas_call | solution.py:168
  95.0 1.9 %collective-permute-start.5 = (bf16[128,1024]{1,0:T(8,128)(2,1)S(1)}, bf16[128,1024]{1,0:T(8,128)(2,1)S(1)}, u32[]{:S(2)}, u32[]{:S(2)}) collective-permute-start(bf16[128,1024]{1,0:T(8,128)(2,1)S(1)} %get-tuple-element.19), channel_id=1, source_target_pairs={{2,0},{3,1},{4,2},{5,3},{6,4},{7,5},{8,6},{9,7},{10,8},{11,9},{12,... | collective-permute-start | bytes 786440 | tf_op jit(solution)/shard_map/ppermute | solution.py:261
  96.9 6.0 %collective-permute-start.6 = (bf16[128,1024]{1,0:T(8,128)(2,1)S(1)}, bf16[128,1024]{1,0:T(8,128)(2,1)S(1)}, u32[]{:S(2)}, u32[]{:S(2)}) collective-permute-start(bf16[128,1024]{1,0:T(8,128)(2,1)S(1)} %get-tuple-element.20), channel_id=1, source_target_pairs={{0,2},{1,3},{2,4},{3,5},{4,6},{5,7},{6,8},{7,9},{8,10},{9,11},{10,... | collective-permute-start | bytes 786440 | tf_op jit(solution)/shard_map/ppermute | solution.py:261
  103.0 9.9 %collective-permute-done.5 = bf16[128,1024]{1,0:T(8,128)(2,1)S(1)} collective-permute-done((bf16[128,1024]{1,0:T(8,128)(2,1)S(1)}, bf16[128,1024]{1,0:T(8,128)(2,1)S(1)}, u32[]{:S(2)}, u32[]{:S(2)}) %collective-permute-start.5) | collective-permute-done | bytes 262176 | tf_op jit(solution)/shard_map/ppermute | solution.py:261
  112.8 1.2 collective-permute-done.6
  114.2 0.8 copy.16
  115.0 10.1 %all-to-all-start.2 = ((bf16[16,48,256]{2,1,0:T(8,128)(2,1)}), bf16[16,48,256]{2,1,0:T(8,128)(2,1)S(1)}, u32[]{:S(2)}, u32[]{:S(2)}) async-start(bf16[16,48,256]{2,1,0:T(8,128)(2,1)} %bitcast.20), calls=%async_computation.2 | async-start | bytes 786432 | tf_op jit(solution)/shard_map/all_to_all | solution.py:258
  125.1 1.8 %add_convert_fusion = bf16[384,1024]{1,0:T(8,128)(2,1)S(1)} fusion(bf16[384,1024]{1,0:T(8,128)(2,1)} %collective-permute-done.8, bf16[384,1024]{1,0:T(8,128)(2,1)} %collective-permute-done.7, bf16[384,1024]{1,0:T(8,128)(2,1)S(1)} %copy-done.3), kind=kLoop, calls=%fused_computation | loop fusion | flops 2359296 | bytes 3145728 | tf_op jit(solution)/shard_map/convert_element_type | solution.py:334
  127.0 1.9 %collective-permute-start.9 = (bf16[288,1024]{1,0:T(8,128)(2,1)S(1)}, bf16[288,1024]{1,0:T(8,128)(2,1)S(1)}, u32[]{:S(2)}, u32[]{:S(2)}) collective-permute-start(bf16[288,1024]{1,0:T(8,128)(2,1)S(1)} %pad_maximum_fusion.2), channel_id=1, source_target_pairs={{0,1},{1,0},{2,3},{3,2},{4,5},{5,4},{6,7},{7,6},{8,9},{9,8},{10,11... | collective-permute-start | bytes 1769480 | tf_op jit(solution)/shard_map/ppermute | solution.py:266
  128.9 12.7 %all-to-all-done.2.x = bf16[16,48,256]{2,1,0:T(8,128)(2,1)S(1)} async-done(((bf16[16,48,256]{2,1,0:T(8,128)(2,1)}), bf16[16,48,256]{2,1,0:T(8,128)(2,1)S(1)}, u32[]{:S(2)}, u32[]{:S(2)}) %all-to-all-start.2) | async-done | bytes 393248 | tf_op jit(solution)/shard_map/all_to_all | solution.py:258
  141.7 1.3 place.3
  143.0 4.6 %all-to-all-start.3 = ((bf16[32,24,256]{2,1,0:T(8,128)(2,1)}), bf16[32,24,256]{2,1,0:T(8,128)(2,1)S(1)}, u32[]{:S(2)}, u32[]{:S(2)}) async-start(bf16[32,24,256]{2,1,0:T(8,128)(2,1)} %bitcast.21), calls=%async_computation.3 | async-start | bytes 786432 | tf_op jit(solution)/shard_map/all_to_all | solution.py:253
  147.7 0.8 maximum_select_fusion.2
  148.5 1.2 maximum_select_fusion
  149.7 15.7 %all-to-all-done.3.x = bf16[32,24,256]{2,1,0:T(8,128)(2,1)S(1)} async-done(((bf16[32,24,256]{2,1,0:T(8,128)(2,1)}), bf16[32,24,256]{2,1,0:T(8,128)(2,1)S(1)}, u32[]{:S(2)}, u32[]{:S(2)}) %all-to-all-start.3) | async-done | bytes 393248 | tf_op jit(solution)/shard_map/all_to_all | solution.py:253
  165.4 0.8 assemble.1
  (36 shorter events, 0.8 us)
Async XLA Ops:
  2.6 16.1 %copy-start = (bf16[1,96,2048]{2,1,0:T(8,128)(2,1)S(1)}, bf16[1,96,2048]{2,1,0:T(8,128)(2,1)}, u32[]{:S(2)}) copy-start(bf16[1,96,2048]{2,1,0:T(8,128)(2,1)} %param.14) | copy-start | bytes 1179652
  2.6 16.1 %copy-start.6 = (bf16[1,96,2048]{2,1,0:T(8,128)(2,1)S(1)}, bf16[1,96,2048]{2,1,0:T(8,128)(2,1)}, u32[]{:S(2)}) copy-start(bf16[1,96,2048]{2,1,0:T(8,128)(2,1)} %param.15) | copy-start | bytes 1179652
  2.6 36.2 %all-to-all-start = ((bf16[32,8,1024]{2,1,0:T(8,128)(2,1)}), bf16[32,8,1024]{2,1,0:T(8,128)(2,1)S(1)}, u32[]{:S(2)}, u32[]{:S(2)}) async-start(bf16[32,8,1024]{2,1,0:T(8,128)(2,1)} %bitcast.6), calls=%async_computation | async-start | bytes 1048576 | tf_op jit(solution)/shard_map/all_to_all | solution.py:253
  18.6 1.0 copy-start.7
  18.7 1.1 copy-start.1
  19.8 19.0 %copy-start.5 = (s32[16]{0:T(128)S(1)}, s32[16]{0:T(128)}, u32[]{:S(2)}) copy-start(s32[16]{0:T(128)} %index.3) | copy-start | bytes 196
  19.9 24.9 %collective-permute-start = (bf16[384,1024]{1,0:T(8,128)(2,1)S(1)}, bf16[384,1024]{1,0:T(8,128)(2,1)S(1)}, u32[]{:S(2)}, u32[]{:S(2)}) collective-permute-start(bf16[384,1024]{1,0:T(8,128)(2,1)S(1)} %pad_maximum_fusion), channel_id=1, source_target_pairs={{0,1},{1,0},{2,3},{3,2},{4,5},{5,4},{6,7},{7,6},{8,9},{9,8},{10,11... | collective-permute-start | bytes 2359304 | tf_op jit(solution)/shard_map/ppermute | solution.py:266
  40.2 26.4 %all-to-all-start.1 = ((bf16[16,16,1024]{2,1,0:T(8,128)(2,1)}), bf16[16,16,1024]{2,1,0:T(8,128)(2,1)S(1)}, u32[]{:S(2)}, u32[]{:S(2)}) async-start(bf16[16,16,1024]{2,1,0:T(8,128)(2,1)} %place.2), calls=%async_computation.1 | async-start | bytes 1048576 | tf_op jit(solution)/shard_map/all_to_all | solution.py:258
  44.8 33.7 %copy-start.4 = (s32[16,32]{1,0:T(8,128)S(1)}, s32[16,32]{1,0:T(8,128)}, u32[]{:S(2)}) copy-start(s32[16,32]{1,0:T(8,128)} %lens.3) | copy-start | bytes 6148
  44.9 33.6 %collective-permute-start.2 = (bf16[384,1024]{1,0:T(8,128)(2,1)S(1)}, bf16[384,1024]{1,0:T(8,128)(2,1)}, u32[]{:S(2)}, u32[]{:S(2)}) collective-permute-start(bf16[384,1024]{1,0:T(8,128)(2,1)S(1)} %pad_maximum_fusion.1.here), channel_id=1, source_target_pairs={{2,0},{3,1},{4,2},{5,3},{6,4},{7,5},{8,6},{9,7},{10,8},{11,9},{12,... | collective-permute-start | bytes 2359304 | tf_op jit(solution)/shard_map/ppermute | solution.py:261
  47.7 30.9 %collective-permute-start.1 = (bf16[384,1024]{1,0:T(8,128)(2,1)S(1)}, bf16[384,1024]{1,0:T(8,128)(2,1)}, u32[]{:S(2)}, u32[]{:S(2)}) collective-permute-start(bf16[384,1024]{1,0:T(8,128)(2,1)S(1)} %pad_maximum_fusion.1.here), channel_id=1, source_target_pairs={{0,2},{1,3},{2,4},{3,5},{4,6},{5,7},{6,8},{7,9},{8,10},{9,11},{10,... | collective-permute-start | bytes 2359304 | tf_op jit(solution)/shard_map/ppermute | solution.py:261
  66.6 25.2 %collective-permute-start.4 = (bf16[128,1024]{1,0:T(8,128)(2,1)S(1)}, bf16[128,1024]{1,0:T(8,128)(2,1)S(1)}, u32[]{:S(2)}, u32[]{:S(2)}) collective-permute-start(bf16[128,1024]{1,0:T(8,128)(2,1)S(1)} %bitcast.48), channel_id=1, source_target_pairs={{2,0},{3,1},{4,2},{5,3},{6,4},{7,5},{8,6},{9,7},{10,8},{11,9},{12,... | collective-permute-start | bytes 786440 | tf_op jit(solution)/shard_map/ppermute | solution.py:261
  69.4 22.5 %collective-permute-start.3 = (bf16[128,1024]{1,0:T(8,128)(2,1)S(1)}, bf16[128,1024]{1,0:T(8,128)(2,1)S(1)}, u32[]{:S(2)}, u32[]{:S(2)}) collective-permute-start(bf16[128,1024]{1,0:T(8,128)(2,1)S(1)} %bitcast.49), channel_id=1, source_target_pairs={{0,2},{1,3},{2,4},{3,5},{4,6},{5,7},{6,8},{7,9},{8,10},{9,11},{10,... | collective-permute-start | bytes 786440 | tf_op jit(solution)/shard_map/ppermute | solution.py:261
  83.3 11.6 %copy-start.2 = (bf16[384,1024]{1,0:T(8,128)(2,1)}, bf16[384,1024]{1,0:T(8,128)(2,1)S(1)}, u32[]{:S(2)}) copy-start(bf16[384,1024]{1,0:T(8,128)(2,1)S(1)} %get-tuple-element.25) | copy-start | bytes 2359300
  83.3 41.8 %collective-permute-start.7 = (bf16[384,1024]{1,0:T(8,128)(2,1)}, bf16[384,1024]{1,0:T(8,128)(2,1)}, u32[]{:S(2)}, u32[]{:S(2)}) collective-permute-start(bf16[384,1024]{1,0:T(8,128)(2,1)} %get-tuple-element.26), channel_id=1, source_target_pairs={{2,0},{3,1},{4,2},{5,3},{6,4},{7,5},{8,6},{9,7},{10,8},{11,9},{12,... | collective-permute-start | bytes 2359304 | tf_op jit(solution)/shard_map/ppermute | solution.py:261
  85.2 39.9 %collective-permute-start.8 = (bf16[384,1024]{1,0:T(8,128)(2,1)}, bf16[384,1024]{1,0:T(8,128)(2,1)}, u32[]{:S(2)}, u32[]{:S(2)}) collective-permute-start(bf16[384,1024]{1,0:T(8,128)(2,1)} %get-tuple-element.27), channel_id=1, source_target_pairs={{0,2},{1,3},{2,4},{3,5},{4,6},{5,7},{6,8},{7,9},{8,10},{9,11},{10,... | collective-permute-start | bytes 2359304 | tf_op jit(solution)/shard_map/ppermute | solution.py:261
  95.0 17.9 %collective-permute-start.5 = (bf16[128,1024]{1,0:T(8,128)(2,1)S(1)}, bf16[128,1024]{1,0:T(8,128)(2,1)S(1)}, u32[]{:S(2)}, u32[]{:S(2)}) collective-permute-start(bf16[128,1024]{1,0:T(8,128)(2,1)S(1)} %get-tuple-element.19), channel_id=1, source_target_pairs={{2,0},{3,1},{4,2},{5,3},{6,4},{7,5},{8,6},{9,7},{10,8},{11,9},{12,... | collective-permute-start | bytes 786440 | tf_op jit(solution)/shard_map/ppermute | solution.py:261
  96.9 17.1 %collective-permute-start.6 = (bf16[128,1024]{1,0:T(8,128)(2,1)S(1)}, bf16[128,1024]{1,0:T(8,128)(2,1)S(1)}, u32[]{:S(2)}, u32[]{:S(2)}) collective-permute-start(bf16[128,1024]{1,0:T(8,128)(2,1)S(1)} %get-tuple-element.20), channel_id=1, source_target_pairs={{0,2},{1,3},{2,4},{3,5},{4,6},{5,7},{6,8},{7,9},{8,10},{9,11},{10,... | collective-permute-start | bytes 786440 | tf_op jit(solution)/shard_map/ppermute | solution.py:261
  114.2 10.9 %copy-start.3 = (bf16[384,1024]{1,0:T(8,128)(2,1)S(1)}, bf16[384,1024]{1,0:T(8,128)(2,1)}, u32[]{:S(2)}) copy-start(bf16[384,1024]{1,0:T(8,128)(2,1)} %copy-done.2) | copy-start | bytes 2359300
  115.0 26.7 %all-to-all-start.2 = ((bf16[16,48,256]{2,1,0:T(8,128)(2,1)}), bf16[16,48,256]{2,1,0:T(8,128)(2,1)S(1)}, u32[]{:S(2)}, u32[]{:S(2)}) async-start(bf16[16,48,256]{2,1,0:T(8,128)(2,1)} %bitcast.20), calls=%async_computation.2 | async-start | bytes 786432 | tf_op jit(solution)/shard_map/all_to_all | solution.py:258
  127.0 20.6 %collective-permute-start.9 = (bf16[288,1024]{1,0:T(8,128)(2,1)S(1)}, bf16[288,1024]{1,0:T(8,128)(2,1)S(1)}, u32[]{:S(2)}, u32[]{:S(2)}) collective-permute-start(bf16[288,1024]{1,0:T(8,128)(2,1)S(1)} %pad_maximum_fusion.2), channel_id=1, source_target_pairs={{0,1},{1,0},{2,3},{3,2},{4,5},{5,4},{6,7},{7,6},{8,9},{9,8},{10,11... | collective-permute-start | bytes 1769480 | tf_op jit(solution)/shard_map/ppermute | solution.py:266
  143.0 22.4 %all-to-all-start.3 = ((bf16[32,24,256]{2,1,0:T(8,128)(2,1)}), bf16[32,24,256]{2,1,0:T(8,128)(2,1)S(1)}, u32[]{:S(2)}, u32[]{:S(2)}) async-start(bf16[32,24,256]{2,1,0:T(8,128)(2,1)} %bitcast.21), calls=%async_computation.3 | async-start | bytes 786432 | tf_op jit(solution)/shard_map/all_to_all | solution.py:253

commit v5 on v4

--- a/solution.py
+++ b/solution.py
@@ -12,7 +12,6 @@
 BAND = 2
 NEG_BIG = -1e30
 FACTOR = HD ** (-0.5)
-HEADS_PER_STEP = 4
 INTERPRET = False
 
 
@@ -66,12 +65,22 @@
     return [slice(h * HD, (h + 1) * HD) for h in range(wide // HD)]
 
 
+def video_whole(group, count, lens, video, *refs):
+    rows = video.shape[0] // 4
+    video_kernel(group, count, lens, video.at[:rows], video.at[3 * rows :], *refs)
+
+
+def audio_whole(group, count, lens, aud_q, aud_g, theirs, *refs):
+    rows = aud_q.shape[0]
+    audio_kernel(
+        group, count, lens, aud_q, aud_g, theirs.at[:rows], theirs.at[3 * rows :], *refs
+    )
+
+
 def video_kernel(group, count, lens, queries, grads, before, here, after, dq_ref, tb, th, ta, bias):
     part = before.shape[0] // 2
 
-    @pl.when(pl.program_id(0) == 0)
-    def _():
-        video_bias(group, count, lens, part, bias)
+    video_bias(group, count, lens, part, bias)
 
     spans = head_spans(dq_ref.shape[1])
     keys, values = zip(*[windows((before, here, after), part, cols) for cols in spans])
@@ -120,13 +129,11 @@
     offset = 2 * (column // part) - 2 + (column // group) % 2
     known = (base + offset >= 0) & (base + offset < count)
 
-    @pl.when(pl.program_id(0) == 0)
-    def _():
-        for j, own in enumerate((core, 1 - core)):
-            seen = known & (jnp.abs(offset - own) <= BAND)
-            bias[j * rows : (j + 1) * rows] = jnp.broadcast_to(
-                jnp.where(seen, 0.0, NEG_BIG), (rows, 3 * part)
-            )
+    for j, own in enumerate((core, 1 - core)):
+        seen = known & (jnp.abs(offset - own) <= BAND)
+        bias[j * rows : (j + 1) * rows] = jnp.broadcast_to(
+            jnp.where(seen, 0.0, NEG_BIG), (rows, 3 * part)
+        )
 
     slot = lax.broadcasted_iota(jnp.int32, (rows, 1), 0)
     live_mine = (slot < lens[frame, block]).astype(jnp.float32)
@@ -135,7 +142,7 @@
     spans = head_spans(wide)
     queries, grads = [], []
     for head, cols in enumerate(spans):
-        start = core * half + pl.program_id(0) * wide + head * HD
+        start = core * half + head * HD
         mine = pl.ds(pl.multiple_of(start, HD), HD)
         queries.append(jnp.concatenate([aud_q[:, mine], their_q[:, cols]], axis=0))
         kept = [
@@ -162,14 +169,12 @@
 SCALARS = pl.BlockSpec(memory_space=pltpu.SMEM)
 
 
-def side(kernel, lens, operands, specs, rows, window, width):
+def side(kernel, lens, operands, rows, window, width):
     bf = jnp.bfloat16
-    wide = min(HEADS_PER_STEP * HD, width)
     return pl.pallas_call(
         kernel,
-        grid=(width // wide,),
-        in_specs=[SCALARS] + specs,
-        out_specs=[columns(rows, wide)] + [columns(window, wide)] * 3,
+        in_specs=[SCALARS] + [ON_CHIP] * len(operands),
+        out_specs=[ON_CHIP] * 4,
         out_shape=[jax.ShapeDtypeStruct((rows, width), bf)]
         + [jax.ShapeDtypeStruct((window, width), bf)] * 3,
         scratch_shapes=[pltpu.VMEM((rows, 3 * window // 2), jnp.float32)],
@@ -177,10 +182,6 @@
         cost_estimate=cost(rows, 3 * window // 2, width),
         interpret=INTERPRET,
     )(lens, *operands)
-
-
-def columns(rows, wide, row=0):
-    return pl.BlockSpec((rows, wide), lambda h: (row, h))
 
 
 def place_kernel(spread, index, x, out):
@@ -297,23 +298,18 @@
     video_here = video[block : 3 * block]
     video_before = shift(video_here, 2)
     video_after = shift(video_here, -2)
-    wide = min(HEADS_PER_STEP * HD, half)
-    full = pl.BlockSpec((audio_rows, width), lambda h: (0, 0))
     grad_vq, audio_tb, audio_th, audio_ta = side(
-        functools.partial(video_kernel, group, count),
+        functools.partial(video_whole, group, count),
         aud_len,
-        (video, video, audio_before, audio_here, audio_after),
-        [columns(block, wide), columns(block, wide, 3)] + [columns(4 * audio_rows, wide)] * 3,
+        (video, audio_before, audio_here, audio_after),
         block,
         4 * audio_rows,
         half,
     )
     grad_aq, video_tb, video_th, video_ta = side(
-        functools.partial(audio_kernel, group, count),
+        functools.partial(audio_whole, group, count),
         aud_len,
-        (aud_q[0], aud_dout[0], theirs, theirs, video_before, video_here, video_after),
-        [full, full, columns(audio_rows, wide), columns(audio_rows, wide, 3)]
-        + [columns(2 * block, wide)] * 3,
+        (aud_q[0], aud_dout[0], theirs, video_before, video_here, video_after),
         2 * audio_rows,
         2 * block,
         half,
@@ -331,7 +327,9 @@
     grads = assemble(grads, runs, spreads, group)
 
     from_after, from_before = shift(audio_tb, -2), shift(audio_ta, 2)
-    grad_akv = (audio_th.astype(f32) + from_after.astype(f32) + from_before.astype(f32)).astype(bf)
+    grad_akv = (
+        audio_th.astype(f32) + from_after.astype(f32) + from_before.astype(f32)
+    ).astype(bf)
     mine = (
         grad_aq[:audio_rows],
         grad_akv[:audio_rows],

time: 169 us -> 169 us (level)
  no operation moved by 1% of the time
where the time goes in v5:
time: 169 us; the launch traced here: 166 us
  waiting for transfers between devices  74.4 us (44%)
  starting transfers between devices  71.9 us (43%)
  Pallas kernels  10.6 us (6%)
  other arithmetic  6.11 us (4%)
  local copies, waits for them, and re-layouts  1.95 us (1%)
    all_to_all x2, waiting for transfers between devices, pair_exchange(): lax.all_to_all(x, ('frame', 'seq'), split_axis=0, concat_axis=0, tiled=Tr...  32.4 us
    ppermute x8, starting transfers between devices, shift(): lax.ppermute(x, 'seq', [(i, i + by) for i in range(count) if 0 <= i + by...  32.4 us
    all_to_all x2, waiting for transfers between devices, exchange(): return lax.all_to_all(x, 'frame', split_axis=0, concat_axis=0, tiled=True)  26.4 us
    all_to_all x2, starting transfers between devices, pair_exchange(): lax.all_to_all(x, ('frame', 'seq'), split_axis=0, concat_axis=0, tiled=Tr...  20.7 us
    ppermute x8, waiting for transfers between devices, shift(): lax.ppermute(x, 'seq', [(i, i + by) for i in range(count) if 0 <= i + by...  15.6 us
    all_to_all x2, starting transfers between devices, exchange(): return lax.all_to_all(x, 'frame', split_axis=0, concat_axis=0, tiled=True)  14.7 us
    pallas_call x2, Pallas kernels, side(): pl.pallas_call(kernel, in_specs=[SCALARS] + [ON_CHIP] * len(operands), ou...  7.11 us
    ppermute x2, starting transfers between devices, swap(): return lax.ppermute(x, 'seq', [(i, i ^ 1) for i in range(count)])  4.1 us
  transfers between devices with their start and end apart: 14, of which 7 were waited for; matrix products, arithmetic and copies ran while one was open for 3% of the time, Pallas kernels for 6%

profile of v5, /device:TPU:6, one launch (start us, length us, event | category | flops | bytes accessed | tf_op | source)
XLA Modules:
  0.0 165.9 jit_solution(11829927713683121061)
XLA Ops:
  0.6 1.9 %pad_maximum_fusion.3 = bf16[128,2048]{1,0:T(8,128)(2,1)} fusion(bf16[32,2048]{1,0:T(8,128)(2,1)} %bitcast.51, bf16[32,2048]{1,0:T(8,128)(2,1)} %bitcast.52, bf16[32,2048]{1,0:T(8,128)(2,1)} %bitcast.53, bf16[32,2048]{1,0:T(8,128)(2,1)} %bitcast.54), kind=kLoop, calls=%fused_computation.4 | loop fusion | flops 2097152 | bytes 1048576 | tf_op jit(solution)/shard_map/concatenate | solution.py:269
  2.6 16.1 %all-to-all-start = ((bf16[32,8,1024]{2,1,0:T(8,128)(2,1)}), bf16[32,8,1024]{2,1,0:T(8,128)(2,1)S(1)}, u32[]{:S(2)}, u32[]{:S(2)}) async-start(bf16[32,8,1024]{2,1,0:T(8,128)(2,1)} %bitcast.6), calls=%async_computation | async-start | bytes 1048576 | tf_op jit(solution)/shard_map/all_to_all | solution.py:254
  18.8 0.9 copy-done.7
  19.9 2.2 %collective-permute-start = (bf16[384,1024]{1,0:T(8,128)(2,1)S(1)}, bf16[384,1024]{1,0:T(8,128)(2,1)S(1)}, u32[]{:S(2)}, u32[]{:S(2)}) collective-permute-start(bf16[384,1024]{1,0:T(8,128)(2,1)S(1)} %pad_maximum_fusion), channel_id=1, source_target_pairs={{0,1},{1,0},{2,3},{3,2},{4,5},{5,4},{6,7},{7,6},{8,9},{9,8},{10,11... | collective-permute-start | bytes 2359304 | tf_op jit(solution)/shard_map/ppermute | solution.py:267
  22.1 16.7 %all-to-all-done = bf16[32,8,1024]{2,1,0:T(8,128)(2,1)S(1)} async-done(((bf16[32,8,1024]{2,1,0:T(8,128)(2,1)}), bf16[32,8,1024]{2,1,0:T(8,128)(2,1)S(1)}, u32[]{:S(2)}, u32[]{:S(2)}) %all-to-all-start) | async-done | bytes 524320 | tf_op jit(solution)/shard_map/all_to_all | solution.py:254
  38.8 1.4 place.2
  40.2 4.6 %all-to-all-start.1 = ((bf16[16,16,1024]{2,1,0:T(8,128)(2,1)}), bf16[16,16,1024]{2,1,0:T(8,128)(2,1)S(1)}, u32[]{:S(2)}, u32[]{:S(2)}) async-start(bf16[16,16,1024]{2,1,0:T(8,128)(2,1)} %place.2), calls=%async_computation.1 | async-start | bytes 1048576 | tf_op jit(solution)/shard_map/all_to_all | solution.py:259
  44.9 2.7 %collective-permute-start.2 = (bf16[384,1024]{1,0:T(8,128)(2,1)S(1)}, bf16[384,1024]{1,0:T(8,128)(2,1)}, u32[]{:S(2)}, u32[]{:S(2)}) collective-permute-start(bf16[384,1024]{1,0:T(8,128)(2,1)S(1)} %pad_maximum_fusion.1.refs_1_), channel_id=1, source_target_pairs={{2,0},{3,1},{4,2},{5,3},{6,4},{7,5},{8,6},{9,7},{10,8},{11,9},{12,... | collective-permute-start | bytes 2359304 | tf_op jit(solution)/shard_map/ppermute | solution.py:262
  47.7 5.2 %collective-permute-start.1 = (bf16[384,1024]{1,0:T(8,128)(2,1)S(1)}, bf16[384,1024]{1,0:T(8,128)(2,1)}, u32[]{:S(2)}, u32[]{:S(2)}) collective-permute-start(bf16[384,1024]{1,0:T(8,128)(2,1)S(1)} %pad_maximum_fusion.1.refs_1_), channel_id=1, source_target_pairs={{0,2},{1,3},{2,4},{3,5},{4,6},{5,7},{6,8},{7,9},{8,10},{9,11},{10,... | collective-permute-start | bytes 2359304 | tf_op jit(solution)/shard_map/ppermute | solution.py:262
  52.9 13.7 %all-to-all-done.1 = bf16[16,16,1024]{2,1,0:T(8,128)(2,1)S(1)} async-done(((bf16[16,16,1024]{2,1,0:T(8,128)(2,1)}), bf16[16,16,1024]{2,1,0:T(8,128)(2,1)S(1)}, u32[]{:S(2)}, u32[]{:S(2)}) %all-to-all-start.1) | async-done | bytes 524320 | tf_op jit(solution)/shard_map/all_to_all | solution.py:259
  66.6 2.7 %collective-permute-start.4 = (bf16[128,1024]{1,0:T(8,128)(2,1)S(1)}, bf16[128,1024]{1,0:T(8,128)(2,1)S(1)}, u32[]{:S(2)}, u32[]{:S(2)}) collective-permute-start(bf16[128,1024]{1,0:T(8,128)(2,1)S(1)} %bitcast.47), channel_id=1, source_target_pairs={{2,0},{3,1},{4,2},{5,3},{6,4},{7,5},{8,6},{9,7},{10,8},{11,9},{12,... | collective-permute-start | bytes 786440 | tf_op jit(solution)/shard_map/ppermute | solution.py:262
  69.4 5.2 %collective-permute-start.3 = (bf16[128,1024]{1,0:T(8,128)(2,1)S(1)}, bf16[128,1024]{1,0:T(8,128)(2,1)S(1)}, u32[]{:S(2)}, u32[]{:S(2)}) collective-permute-start(bf16[128,1024]{1,0:T(8,128)(2,1)S(1)} %bitcast.48), channel_id=1, source_target_pairs={{0,2},{1,3},{2,4},{3,5},{4,6},{5,7},{6,8},{7,9},{8,10},{9,11},{10,... | collective-permute-start | bytes 786440 | tf_op jit(solution)/shard_map/ppermute | solution.py:262
  74.6 3.9 %collective-permute-done.2.refs_2_ = bf16[384,1024]{1,0:T(8,128)(2,1)} collective-permute-done((bf16[384,1024]{1,0:T(8,128)(2,1)S(1)}, bf16[384,1024]{1,0:T(8,128)(2,1)}, u32[]{:S(2)}, u32[]{:S(2)}) %collective-permute-start.2) | collective-permute-done | bytes 786464 | tf_op jit(solution)/shard_map/ppermute | solution.py:262
  78.5 4.6 %shard_map.145 = (bf16[64,1024]{1,0:T(8,128)(2,1)S(1)}, bf16[384,1024]{1,0:T(8,128)(2,1)}, bf16[384,1024]{1,0:T(8,128)(2,1)S(1)}, bf16[384,1024]{1,0:T(8,128)(2,1)}) custom-call(s32[16,32]{1,0:T(8,128)S(1)} %copy-done.4, bf16[256,1024]{1,0:T(8,128)(2,1)S(1)} %bitcast.43, bf16[384,1024]{1,0:T(8,128)(2,1)} %collective-permute-done.1.refs_0_, ...), custom_call_target="tpu_custom_call" | custom-call | flops 377487360 | bytes 5242880 | tf_op jit(solution)/shard_map/pallas_call | solution.py:174
  83.1 1.9 %collective-permute-start.7 = (bf16[384,1024]{1,0:T(8,128)(2,1)}, bf16[384,1024]{1,0:T(8,128)(2,1)}, u32[]{:S(2)}, u32[]{:S(2)}) collective-permute-start(bf16[384,1024]{1,0:T(8,128)(2,1)} %get-tuple-element.26), channel_id=1, source_target_pairs={{2,0},{3,1},{4,2},{5,3},{6,4},{7,5},{8,6},{9,7},{10,8},{11,9},{12,... | collective-permute-start | bytes 2359304 | tf_op jit(solution)/shard_map/ppermute | solution.py:262
  85.0 6.6 %collective-permute-start.8 = (bf16[384,1024]{1,0:T(8,128)(2,1)}, bf16[384,1024]{1,0:T(8,128)(2,1)}, u32[]{:S(2)}, u32[]{:S(2)}) collective-permute-start(bf16[384,1024]{1,0:T(8,128)(2,1)} %get-tuple-element.27), channel_id=1, source_target_pairs={{0,2},{1,3},{2,4},{3,5},{4,6},{5,7},{6,8},{7,9},{8,10},{9,11},{10,... | collective-permute-start | bytes 2359304 | tf_op jit(solution)/shard_map/ppermute | solution.py:262
  91.7 2.5 %shard_map.146 = (bf16[192,1024]{1,0:T(8,128)(2,1)S(1)}, bf16[128,1024]{1,0:T(8,128)(2,1)S(1)}, bf16[128,1024]{1,0:T(8,128)(2,1)S(1)}, bf16[128,1024]{1,0:T(8,128)(2,1)S(1)}) custom-call(s32[16,32]{1,0:T(8,128)S(1)} %copy-done.4, bf16[96,2048]{1,0:T(8,128)(2,1)S(1)} %bitcast.45, bf16[96,2048]{1,0:T(8,128)(2,1)S(1)} %bitcast.46, ...), custom_call_target="tpu_custom_call" | custom-call | flops 377487360 | bytes 3145728 | tf_op jit(solution)/shard_map/pallas_call | solution.py:174
  94.2 1.9 %collective-permute-start.5 = (bf16[128,1024]{1,0:T(8,128)(2,1)S(1)}, bf16[128,1024]{1,0:T(8,128)(2,1)S(1)}, u32[]{:S(2)}, u32[]{:S(2)}) collective-permute-start(bf16[128,1024]{1,0:T(8,128)(2,1)S(1)} %get-tuple-element.19), channel_id=1, source_target_pairs={{2,0},{3,1},{4,2},{5,3},{6,4},{7,5},{8,6},{9,7},{10,8},{11,9},{12,... | collective-permute-start | bytes 786440 | tf_op jit(solution)/shard_map/ppermute | solution.py:262
  96.1 6.0 %collective-permute-start.6 = (bf16[128,1024]{1,0:T(8,128)(2,1)S(1)}, bf16[128,1024]{1,0:T(8,128)(2,1)S(1)}, u32[]{:S(2)}, u32[]{:S(2)}) collective-permute-start(bf16[128,1024]{1,0:T(8,128)(2,1)S(1)} %get-tuple-element.20), channel_id=1, source_target_pairs={{0,2},{1,3},{2,4},{3,5},{4,6},{5,7},{6,8},{7,9},{8,10},{9,11},{10,... | collective-permute-start | bytes 786440 | tf_op jit(solution)/shard_map/ppermute | solution.py:262
  102.2 10.4 %collective-permute-done.5 = bf16[128,1024]{1,0:T(8,128)(2,1)S(1)} collective-permute-done((bf16[128,1024]{1,0:T(8,128)(2,1)S(1)}, bf16[128,1024]{1,0:T(8,128)(2,1)S(1)}, u32[]{:S(2)}, u32[]{:S(2)}) %collective-permute-start.5) | collective-permute-done | bytes 262176 | tf_op jit(solution)/shard_map/ppermute | solution.py:262
  112.6 1.2 collective-permute-done.6
  114.0 0.8 copy.16
  114.8 10.1 %all-to-all-start.2 = ((bf16[16,48,256]{2,1,0:T(8,128)(2,1)}), bf16[16,48,256]{2,1,0:T(8,128)(2,1)S(1)}, u32[]{:S(2)}, u32[]{:S(2)}) async-start(bf16[16,48,256]{2,1,0:T(8,128)(2,1)} %bitcast.20), calls=%async_computation.2 | async-start | bytes 786432 | tf_op jit(solution)/shard_map/all_to_all | solution.py:259
  124.9 1.8 %add_convert_fusion = bf16[384,1024]{1,0:T(8,128)(2,1)S(1)} fusion(bf16[384,1024]{1,0:T(8,128)(2,1)} %collective-permute-done.8, bf16[384,1024]{1,0:T(8,128)(2,1)} %collective-permute-done.7, bf16[384,1024]{1,0:T(8,128)(2,1)S(1)} %copy-done.3), kind=kLoop, calls=%fused_computation | loop fusion | flops 2359296 | bytes 3145728 | tf_op jit(solution)/shard_map/convert_element_type | solution.py:332
  126.8 1.9 %collective-permute-start.9 = (bf16[288,1024]{1,0:T(8,128)(2,1)S(1)}, bf16[288,1024]{1,0:T(8,128)(2,1)S(1)}, u32[]{:S(2)}, u32[]{:S(2)}) collective-permute-start(bf16[288,1024]{1,0:T(8,128)(2,1)S(1)} %pad_maximum_fusion.2), channel_id=1, source_target_pairs={{0,1},{1,0},{2,3},{3,2},{4,5},{5,4},{6,7},{7,6},{8,9},{9,8},{10,11... | collective-permute-start | bytes 1769480 | tf_op jit(solution)/shard_map/ppermute | solution.py:267
  128.7 12.7 %all-to-all-done.2.x = bf16[16,48,256]{2,1,0:T(8,128)(2,1)S(1)} async-done(((bf16[16,48,256]{2,1,0:T(8,128)(2,1)}), bf16[16,48,256]{2,1,0:T(8,128)(2,1)S(1)}, u32[]{:S(2)}, u32[]{:S(2)}) %all-to-all-start.2) | async-done | bytes 393248 | tf_op jit(solution)/shard_map/all_to_all | solution.py:259
  141.4 1.3 place.3
  142.8 4.6 %all-to-all-start.3 = ((bf16[32,24,256]{2,1,0:T(8,128)(2,1)}), bf16[32,24,256]{2,1,0:T(8,128)(2,1)S(1)}, u32[]{:S(2)}, u32[]{:S(2)}) async-start(bf16[32,24,256]{2,1,0:T(8,128)(2,1)} %bitcast.21), calls=%async_computation.3 | async-start | bytes 786432 | tf_op jit(solution)/shard_map/all_to_all | solution.py:254
  147.5 0.8 maximum_select_fusion.2
  148.3 1.2 maximum_select_fusion
  149.5 15.7 %all-to-all-done.3.x = bf16[32,24,256]{2,1,0:T(8,128)(2,1)S(1)} async-done(((bf16[32,24,256]{2,1,0:T(8,128)(2,1)}), bf16[32,24,256]{2,1,0:T(8,128)(2,1)S(1)}, u32[]{:S(2)}, u32[]{:S(2)}) %all-to-all-start.3) | async-done | bytes 393248 | tf_op jit(solution)/shard_map/all_to_all | solution.py:254
  165.2 0.8 assemble.1
  (36 shorter events, 0.8 us)
Async XLA Ops:
  2.6 16.1 %copy-start = (bf16[1,96,2048]{2,1,0:T(8,128)(2,1)S(1)}, bf16[1,96,2048]{2,1,0:T(8,128)(2,1)}, u32[]{:S(2)}) copy-start(bf16[1,96,2048]{2,1,0:T(8,128)(2,1)} %param.14) | copy-start | bytes 1179652
  2.6 16.1 %copy-start.6 = (bf16[1,96,2048]{2,1,0:T(8,128)(2,1)S(1)}, bf16[1,96,2048]{2,1,0:T(8,128)(2,1)}, u32[]{:S(2)}) copy-start(bf16[1,96,2048]{2,1,0:T(8,128)(2,1)} %param.15) | copy-start | bytes 1179652
  2.6 36.2 %all-to-all-start = ((bf16[32,8,1024]{2,1,0:T(8,128)(2,1)}), bf16[32,8,1024]{2,1,0:T(8,128)(2,1)S(1)}, u32[]{:S(2)}, u32[]{:S(2)}) async-start(bf16[32,8,1024]{2,1,0:T(8,128)(2,1)} %bitcast.6), calls=%async_computation | async-start | bytes 1048576 | tf_op jit(solution)/shard_map/all_to_all | solution.py:254
  18.6 1.0 copy-start.7
  18.7 1.1 copy-start.1
  19.8 19.0 %copy-start.5 = (s32[16]{0:T(128)S(1)}, s32[16]{0:T(128)}, u32[]{:S(2)}) copy-start(s32[16]{0:T(128)} %index.3) | copy-start | bytes 196
  19.9 24.9 %collective-permute-start = (bf16[384,1024]{1,0:T(8,128)(2,1)S(1)}, bf16[384,1024]{1,0:T(8,128)(2,1)S(1)}, u32[]{:S(2)}, u32[]{:S(2)}) collective-permute-start(bf16[384,1024]{1,0:T(8,128)(2,1)S(1)} %pad_maximum_fusion), channel_id=1, source_target_pairs={{0,1},{1,0},{2,3},{3,2},{4,5},{5,4},{6,7},{7,6},{8,9},{9,8},{10,11... | collective-permute-start | bytes 2359304 | tf_op jit(solution)/shard_map/ppermute | solution.py:267
  40.2 26.4 %all-to-all-start.1 = ((bf16[16,16,1024]{2,1,0:T(8,128)(2,1)}), bf16[16,16,1024]{2,1,0:T(8,128)(2,1)S(1)}, u32[]{:S(2)}, u32[]{:S(2)}) async-start(bf16[16,16,1024]{2,1,0:T(8,128)(2,1)} %place.2), calls=%async_computation.1 | async-start | bytes 1048576 | tf_op jit(solution)/shard_map/all_to_all | solution.py:259
  44.8 33.7 %copy-start.4 = (s32[16,32]{1,0:T(8,128)S(1)}, s32[16,32]{1,0:T(8,128)}, u32[]{:S(2)}) copy-start(s32[16,32]{1,0:T(8,128)} %lens.3) | copy-start | bytes 6148
  44.9 33.6 %collective-permute-start.2 = (bf16[384,1024]{1,0:T(8,128)(2,1)S(1)}, bf16[384,1024]{1,0:T(8,128)(2,1)}, u32[]{:S(2)}, u32[]{:S(2)}) collective-permute-start(bf16[384,1024]{1,0:T(8,128)(2,1)S(1)} %pad_maximum_fusion.1.refs_1_), channel_id=1, source_target_pairs={{2,0},{3,1},{4,2},{5,3},{6,4},{7,5},{8,6},{9,7},{10,8},{11,9},{12,... | collective-permute-start | bytes 2359304 | tf_op jit(solution)/shard_map/ppermute | solution.py:262
  47.7 30.9 %collective-permute-start.1 = (bf16[384,1024]{1,0:T(8,128)(2,1)S(1)}, bf16[384,1024]{1,0:T(8,128)(2,1)}, u32[]{:S(2)}, u32[]{:S(2)}) collective-permute-start(bf16[384,1024]{1,0:T(8,128)(2,1)S(1)} %pad_maximum_fusion.1.refs_1_), channel_id=1, source_target_pairs={{0,2},{1,3},{2,4},{3,5},{4,6},{5,7},{6,8},{7,9},{8,10},{9,11},{10,... | collective-permute-start | bytes 2359304 | tf_op jit(solution)/shard_map/ppermute | solution.py:262
  66.6 25.0 %collective-permute-start.4 = (bf16[128,1024]{1,0:T(8,128)(2,1)S(1)}, bf16[128,1024]{1,0:T(8,128)(2,1)S(1)}, u32[]{:S(2)}, u32[]{:S(2)}) collective-permute-start(bf16[128,1024]{1,0:T(8,128)(2,1)S(1)} %bitcast.47), channel_id=1, source_target_pairs={{2,0},{3,1},{4,2},{5,3},{6,4},{7,5},{8,6},{9,7},{10,8},{11,9},{12,... | collective-permute-start | bytes 786440 | tf_op jit(solution)/shard_map/ppermute | solution.py:262
  69.4 22.3 %collective-permute-start.3 = (bf16[128,1024]{1,0:T(8,128)(2,1)S(1)}, bf16[128,1024]{1,0:T(8,128)(2,1)S(1)}, u32[]{:S(2)}, u32[]{:S(2)}) collective-permute-start(bf16[128,1024]{1,0:T(8,128)(2,1)S(1)} %bitcast.48), channel_id=1, source_target_pairs={{0,2},{1,3},{2,4},{3,5},{4,6},{5,7},{6,8},{7,9},{8,10},{9,11},{10,... | collective-permute-start | bytes 786440 | tf_op jit(solution)/shard_map/ppermute | solution.py:262
  83.1 11.1 %copy-start.2 = (bf16[384,1024]{1,0:T(8,128)(2,1)}, bf16[384,1024]{1,0:T(8,128)(2,1)S(1)}, u32[]{:S(2)}) copy-start(bf16[384,1024]{1,0:T(8,128)(2,1)S(1)} %get-tuple-element.25) | copy-start | bytes 2359300
  83.1 41.7 %collective-permute-start.7 = (bf16[384,1024]{1,0:T(8,128)(2,1)}, bf16[384,1024]{1,0:T(8,128)(2,1)}, u32[]{:S(2)}, u32[]{:S(2)}) collective-permute-start(bf16[384,1024]{1,0:T(8,128)(2,1)} %get-tuple-element.26), channel_id=1, source_target_pairs={{2,0},{3,1},{4,2},{5,3},{6,4},{7,5},{8,6},{9,7},{10,8},{11,9},{12,... | collective-permute-start | bytes 2359304 | tf_op jit(solution)/shard_map/ppermute | solution.py:262
  85.0 39.8 %collective-permute-start.8 = (bf16[384,1024]{1,0:T(8,128)(2,1)}, bf16[384,1024]{1,0:T(8,128)(2,1)}, u32[]{:S(2)}, u32[]{:S(2)}) collective-permute-start(bf16[384,1024]{1,0:T(8,128)(2,1)} %get-tuple-element.27), channel_id=1, source_target_pairs={{0,2},{1,3},{2,4},{3,5},{4,6},{5,7},{6,8},{7,9},{8,10},{9,11},{10,... | collective-permute-start | bytes 2359304 | tf_op jit(solution)/shard_map/ppermute | solution.py:262
  94.2 18.4 %collective-permute-start.5 = (bf16[128,1024]{1,0:T(8,128)(2,1)S(1)}, bf16[128,1024]{1,0:T(8,128)(2,1)S(1)}, u32[]{:S(2)}, u32[]{:S(2)}) collective-permute-start(bf16[128,1024]{1,0:T(8,128)(2,1)S(1)} %get-tuple-element.19), channel_id=1, source_target_pairs={{2,0},{3,1},{4,2},{5,3},{6,4},{7,5},{8,6},{9,7},{10,8},{11,9},{12,... | collective-permute-start | bytes 786440 | tf_op jit(solution)/shard_map/ppermute | solution.py:262
  96.1 17.7 %collective-permute-start.6 = (bf16[128,1024]{1,0:T(8,128)(2,1)S(1)}, bf16[128,1024]{1,0:T(8,128)(2,1)S(1)}, u32[]{:S(2)}, u32[]{:S(2)}) collective-permute-start(bf16[128,1024]{1,0:T(8,128)(2,1)S(1)} %get-tuple-element.20), channel_id=1, source_target_pairs={{0,2},{1,3},{2,4},{3,5},{4,6},{5,7},{6,8},{7,9},{8,10},{9,11},{10,... | collective-permute-start | bytes 786440 | tf_op jit(solution)/shard_map/ppermute | solution.py:262
  114.0 10.9 %copy-start.3 = (bf16[384,1024]{1,0:T(8,128)(2,1)S(1)}, bf16[384,1024]{1,0:T(8,128)(2,1)}, u32[]{:S(2)}) copy-start(bf16[384,1024]{1,0:T(8,128)(2,1)} %copy-done.2) | copy-start | bytes 2359300
  114.8 26.7 %all-to-all-start.2 = ((bf16[16,48,256]{2,1,0:T(8,128)(2,1)}), bf16[16,48,256]{2,1,0:T(8,128)(2,1)S(1)}, u32[]{:S(2)}, u32[]{:S(2)}) async-start(bf16[16,48,256]{2,1,0:T(8,128)(2,1)} %bitcast.20), calls=%async_computation.2 | async-start | bytes 786432 | tf_op jit(solution)/shard_map/all_to_all | solution.py:259
  126.8 20.6 %collective-permute-start.9 = (bf16[288,1024]{1,0:T(8,128)(2,1)S(1)}, bf16[288,1024]{1,0:T(8,128)(2,1)S(1)}, u32[]{:S(2)}, u32[]{:S(2)}) collective-permute-start(bf16[288,1024]{1,0:T(8,128)(2,1)S(1)} %pad_maximum_fusion.2), channel_id=1, source_target_pairs={{0,1},{1,0},{2,3},{3,2},{4,5},{5,4},{6,7},{7,6},{8,9},{9,8},{10,11... | collective-permute-start | bytes 1769480 | tf_op jit(solution)/shard_map/ppermute | solution.py:267
  142.8 22.4 %all-to-all-start.3 = ((bf16[32,24,256]{2,1,0:T(8,128)(2,1)}), bf16[32,24,256]{2,1,0:T(8,128)(2,1)S(1)}, u32[]{:S(2)}, u32[]{:S(2)}) async-start(bf16[32,24,256]{2,1,0:T(8,128)(2,1)} %bitcast.21), calls=%async_computation.3 | async-start | bytes 786432 | tf_op jit(solution)/shard_map/all_to_all | solution.py:254

commit v6 on v5

--- a/solution.py
+++ b/solution.py
@@ -40,10 +40,23 @@
     grad_scores = [
         (weights[h] * (grad_weights[h] - delta[h])).astype(jnp.bfloat16) for h in total
     ]
+    grad_query = [contract(grad_scores[h], keys[h], 1, 0) * FACTOR for h in total]
+    return grad_query, half, grad_scores, (largest, inverse, delta)
+
+
+def terms(queries, grads, half, grad_scores):
+    total = range(len(queries))
     value_terms = [contract(half[h], grads[h], 0, 0) for h in total]
-    grad_query = [contract(grad_scores[h], keys[h], 1, 0) * FACTOR for h in total]
     key_terms = [contract(grad_scores[h], queries[h], 0, 0) * FACTOR for h in total]
-    return grad_query, key_terms, value_terms
+    return key_terms, value_terms
+
+
+def split_stats(value):
+    high = value.astype(jnp.bfloat16)
+    rest = value - high.astype(jnp.float32)
+    middle = rest.astype(jnp.bfloat16)
+    low = (rest - middle.astype(jnp.float32)).astype(jnp.bfloat16)
+    return high, middle, low
 
 
 def windows(refs, part, cols):
@@ -52,42 +65,88 @@
     return keys, values
 
 
-def write(results, spans, dq_ref, term_refs, part):
-    for cols, dq, kt, vt in zip(spans, *results, strict=True):
-        dq_ref[:, cols] = dq.astype(jnp.bfloat16)
-        for place, out in enumerate(term_refs):
-            rows = slice(place * part, (place + 1) * part)
-            out[:part, cols] = kt[rows].astype(jnp.bfloat16)
-            out[part:, cols] = vt[rows].astype(jnp.bfloat16)
-
-
 def head_spans(wide):
     return [slice(h * HD, (h + 1) * HD) for h in range(wide // HD)]
 
 
-def video_whole(group, count, lens, video, *refs):
+STAT_ROWS = 8
+
+
+def video_kernel(group, count, lens, video, before, here, after, dq_ref, out, bias):
     rows = video.shape[0] // 4
-    video_kernel(group, count, lens, video.at[:rows], video.at[3 * rows :], *refs)
-
-
-def audio_whole(group, count, lens, aud_q, aud_g, theirs, *refs):
-    rows = aud_q.shape[0]
-    audio_kernel(
-        group, count, lens, aud_q, aud_g, theirs.at[:rows], theirs.at[3 * rows :], *refs
-    )
-
-
-def video_kernel(group, count, lens, queries, grads, before, here, after, dq_ref, tb, th, ta, bias):
     part = before.shape[0] // 2
-
     video_bias(group, count, lens, part, bias)
-
     spans = head_spans(dq_ref.shape[1])
     keys, values = zip(*[windows((before, here, after), part, cols) for cols in spans])
-    results = attend(
-        [queries[:, cols] for cols in spans], keys, values, [grads[:, cols] for cols in spans], bias
-    )
-    write(results, spans, dq_ref, (tb, th, ta), part)
+    queries = [video[:rows, cols] for cols in spans]
+    grads = [video[3 * rows :, cols] for cols in spans]
+    grad_query, _, _, stats = attend(queries, keys, values, grads, bias)
+    lane = lax.broadcasted_iota(jnp.int32, (rows, HD), 1)
+    table = jnp.zeros((rows, HD), jnp.float32)
+    for j, stat in enumerate(stats):
+        for h, value in enumerate(stat):
+            table = jnp.where(lane == j * len(spans) + h, value, table)
+    for cols, dq in zip(spans, grad_query, strict=True):
+        dq_ref[:, cols] = dq.astype(jnp.bfloat16)
+    out[:rows] = video[:rows]
+    out[rows : 2 * rows] = video[3 * rows :]
+    for j, piece in enumerate(split_stats(table)):
+        top = 2 * rows + j * STAT_ROWS
+        for k in range(rows // STAT_ROWS):
+            out[top : top + STAT_ROWS, k * HD : (k + 1) * HD] = piece[
+                k * STAT_ROWS : (k + 1) * STAT_ROWS
+            ]
+
+
+def terms_kernel(group, count, lens, before, here, after, audio, dkv_ref, bias):
+    rows = (before.shape[0] - 3 * STAT_ROWS) // 2
+    part = audio.shape[0] // 2
+    slots = part // 2
+    frame = lax.axis_index("frame")
+    block = lax.axis_index("seq")
+    core = lax.rem(block, 2)
+    base = block - core
+    place = lax.broadcasted_iota(jnp.int32, (3 * rows, 1), 0)
+    offset = 2 * (place // rows) - 2 + (place // group) % 2
+    known = (base + offset >= 0) & (base + offset < count)
+    column = lax.broadcasted_iota(jnp.int32, (1, part), 1)
+    mine = column < slots
+    slot = jnp.where(mine, column, column - slots)
+    live = slot < jnp.where(mine, lens[frame, block], lens[frame, base + 1 - core])
+    own = jnp.where(mine, core, 1 - core)
+    near = jnp.where(known, 0.0, NEG_BIG) + jnp.where(live, 0.0, NEG_BIG)
+    bias[...] = jnp.where(jnp.abs(offset - own) <= BAND, near, NEG_BIG)
+    refs = (before, here, after)
+    spans = head_spans(dkv_ref.shape[1])
+    total = range(len(spans))
+    queries = [jnp.concatenate([ref[:rows, cols] for ref in refs], axis=0) for cols in spans]
+    grads = [
+        jnp.concatenate([ref[rows : 2 * rows, cols] for ref in refs], axis=0) for cols in spans
+    ]
+    tables = []
+    for ref in refs:
+        value = 0.0
+        for j in range(3):
+            top = 2 * rows + j * STAT_ROWS
+            wide = ref[top : top + STAT_ROWS, : rows // STAT_ROWS * HD].astype(jnp.float32)
+            value = value + wide
+        for k in range(rows // STAT_ROWS):
+            tables.append(value[:, k * HD : (k + 1) * HD])
+    table = jnp.concatenate(tables, axis=0)
+    largest, inverse, delta = [
+        [table[:, j * len(spans) + h : j * len(spans) + h + 1] for h in total] for j in range(3)
+    ]
+    scores = [contract(queries[h], audio[:part, spans[h]], 1, 1) * FACTOR + bias[...] for h in total]
+    weights = [jnp.exp(scores[h] - largest[h]) * inverse[h] for h in total]
+    half = [weights[h].astype(jnp.bfloat16) for h in total]
+    grad_weights = [contract(grads[h], audio[part:, spans[h]], 1, 1) for h in total]
+    grad_scores = [
+        (weights[h] * (grad_weights[h] - delta[h])).astype(jnp.bfloat16) for h in total
+    ]
+    key_terms, value_terms = terms(queries, grads, half, grad_scores)
+    for h in total:
+        dkv_ref[:part, spans[h]] = key_terms[h].astype(jnp.bfloat16)
+        dkv_ref[part:, spans[h]] = value_terms[h].astype(jnp.bfloat16)
 
 
 def video_bias(group, count, lens, part, bias):
@@ -114,6 +173,13 @@
     bias[...] = jnp.where(is_late == 0, early_row, late_row)
 
 
+def audio_whole(group, count, lens, aud_q, aud_g, theirs, *refs):
+    rows = aud_q.shape[0]
+    audio_kernel(
+        group, count, lens, aud_q, aud_g, theirs.at[:rows], theirs.at[3 * rows :], *refs
+    )
+
+
 def audio_kernel(
     group, count, lens, aud_q, aud_g, their_q, their_g, before, here, after, dq_ref, tb, th, ta, bias
 ):
@@ -151,8 +217,14 @@
         ]
         grads.append(jnp.concatenate(kept, axis=0).astype(jnp.bfloat16))
     keys, values = zip(*[windows((before, here, after), part, cols) for cols in spans])
-    results = attend(queries, keys, values, grads, bias)
-    write(results, spans, dq_ref, (tb, th, ta), part)
+    grad_query, weights, grad_scores, _ = attend(queries, keys, values, grads, bias)
+    key_terms, value_terms = terms(queries, grads, weights, grad_scores)
+    for h, cols in enumerate(spans):
+        dq_ref[:, cols] = grad_query[h].astype(jnp.bfloat16)
+        for place, out in enumerate((tb, th, ta)):
+            span = slice(place * part, (place + 1) * part)
+            out[:part, cols] = key_terms[h][span].astype(jnp.bfloat16)
+            out[part:, cols] = value_terms[h][span].astype(jnp.bfloat16)
 
 
 def cost(rows, keys, width):
@@ -169,19 +241,54 @@
 SCALARS = pl.BlockSpec(memory_space=pltpu.SMEM)
 
 
-def side(kernel, lens, operands, rows, window, width):
-    bf = jnp.bfloat16
+def side(kernel, lens, operands, outs, scores):
+    width = outs[0][1]
     return pl.pallas_call(
         kernel,
         in_specs=[SCALARS] + [ON_CHIP] * len(operands),
-        out_specs=[ON_CHIP] * 4,
-        out_shape=[jax.ShapeDtypeStruct((rows, width), bf)]
-        + [jax.ShapeDtypeStruct((window, width), bf)] * 3,
-        scratch_shapes=[pltpu.VMEM((rows, 3 * window // 2), jnp.float32)],
+        out_specs=[ON_CHIP] * len(outs),
+        out_shape=[jax.ShapeDtypeStruct(shape, jnp.bfloat16) for shape in outs],
+        scratch_shapes=[pltpu.VMEM(scores, jnp.float32)],
         compiler_params=pltpu.CompilerParams(vmem_limit_bytes=GRANT),
-        cost_estimate=cost(rows, 3 * window // 2, width),
+        cost_estimate=cost(*scores, width),
         interpret=INTERPRET,
     )(lens, *operands)
+
+
+def gather_kernel(runs, spreads, group, dq, th, t1, t2, out):
+    rows, slim = dq.shape[0], out.shape[2]
+    core = lax.rem(lax.axis_index("seq"), 2)
+    for run in range(runs):
+        here = slice(run * 2 * group, (run + 1) * 2 * group)
+        values = [dq[here]]
+        for start in (0, rows):
+            there = slice(start + here.start, start + here.stop)
+            total = th[there].astype(jnp.float32) + t1[there].astype(jnp.float32)
+            values.append((total + t2[there].astype(jnp.float32)).astype(jnp.bfloat16))
+        for spread in range(spreads):
+            cols = slice(spread * slim, (spread + 1) * slim)
+            for late in range(2):
+                for j, value in enumerate(values):
+                    other = core if late == 0 else 1 - core
+                    left = pl.multiple_of((other * 3 + j) * group, group)
+                    out[run * spreads + spread, pl.ds(left, group)] = value[
+                        late * group : (late + 1) * group, cols
+                    ]
+
+
+def gather(dq, th, t1, t2, runs, spreads, group):
+    return pl.pallas_call(
+        functools.partial(gather_kernel, runs, spreads, group),
+        in_specs=[ON_CHIP] * 4,
+        out_specs=ON_CHIP,
+        out_shape=jax.ShapeDtypeStruct(
+            (runs * spreads, 6 * group, dq.shape[1] // spreads), jnp.bfloat16
+        ),
+        compiler_params=pltpu.CompilerParams(vmem_limit_bytes=GRANT // 4),
+        cost_estimate=pl.CostEstimate(flops=0, bytes_accessed=16 * dq.size, transcendentals=0),
+        name="gather",
+        interpret=INTERPRET,
+    )(dq, th, t1, t2)
 
 
 def place_kernel(spread, index, x, out):
@@ -196,7 +303,7 @@
     return pl.pallas_call(
         functools.partial(place_kernel, spread),
         in_specs=[SCALARS, ON_CHIP],
-        out_specs=pl.BlockSpec(x.shape, lambda: (0, 0, 0)),
+        out_specs=ON_CHIP,
         out_shape=jax.ShapeDtypeStruct(x.shape, x.dtype),
         compiler_params=pltpu.CompilerParams(vmem_limit_bytes=GRANT // 4),
         cost_estimate=pl.CostEstimate(flops=0, bytes_accessed=4 * x.size, transcendentals=0),
@@ -205,30 +312,31 @@
     )(index, x)
 
 
-def assemble_kernel(runs, spreads, group, x, *outs):
+def assemble_kernel(runs, spreads, group, x, other, *outs):
     slim = x.shape[2]
+    half = spreads * slim
+    core = lax.rem(lax.axis_index("seq"), 2)
     for run in range(runs):
+        rows = slice(run * group, (run + 1) * group)
         for spread in range(spreads):
-            for core in range(2):
-                piece = (run * spreads + spread) * 2 + core
+            piece = run * spreads + spread
+            for source, start in ((x, core * half), (other, (1 - core) * half)):
+                cols = pl.ds(pl.multiple_of(start + spread * slim, HD), slim)
                 for j, out in enumerate(outs):
-                    left = (core * spreads + spread) * slim
-                    out[0, run * group : (run + 1) * group, left : left + slim] = x[
-                        piece, j * group : (j + 1) * group, :
-                    ]
-
-
-def assemble(x, runs, spreads, group):
+                    out[0, rows, cols] = source[piece, j * group : (j + 1) * group]
+
+
+def assemble(x, other, runs, spreads, group):
     shape = (1, runs * group, 2 * spreads * x.shape[2])
     return pl.pallas_call(
         functools.partial(assemble_kernel, runs, spreads, group),
-        in_specs=[ON_CHIP],
+        in_specs=[ON_CHIP] * 2,
         out_specs=[ON_CHIP] * 3,
         out_shape=[jax.ShapeDtypeStruct(shape, jnp.bfloat16)] * 3,
-        compiler_params=pltpu.CompilerParams(vmem_limit_bytes=GRANT),
+        compiler_params=pltpu.CompilerParams(vmem_limit_bytes=GRANT // 4),
         name="assemble",
         interpret=INTERPRET,
-    )(x)
+    )(x, other)
 
 
 def shards(vid_q, vid_k, vid_v, vid_dout, aud_q, aud_k, aud_v, aud_dout, aud_len, match):
@@ -242,8 +350,6 @@
     group = 4 * video_rows // frames
     runs = frames // 4
     spreads = frames // runs
-    slim = half // spreads
-    f32, bf = jnp.float32, jnp.bfloat16
 
     pairs = [
         [f * count + 2 * c + k for f in range(frames) for k in range(2)]
@@ -298,38 +404,37 @@
     video_here = video[block : 3 * block]
     video_before = shift(video_here, 2)
     video_after = shift(video_here, -2)
-    grad_vq, audio_tb, audio_th, audio_ta = side(
-        functools.partial(video_whole, group, count),
+    grad_vq, shared = side(
+        functools.partial(video_kernel, group, count),
         aud_len,
         (video, audio_before, audio_here, audio_after),
-        block,
-        4 * audio_rows,
-        half,
+        [(block, half), (2 * block + 3 * STAT_ROWS, half)],
+        (block, 6 * audio_rows),
     )
     grad_aq, video_tb, video_th, video_ta = side(
         functools.partial(audio_whole, group, count),
         aud_len,
         (aud_q[0], aud_dout[0], theirs, video_before, video_here, video_after),
-        2 * audio_rows,
-        2 * block,
-        half,
+        [(2 * audio_rows, half)] + [(2 * block, half)] * 3,
+        (2 * audio_rows, 3 * block),
     )
 
     from_after, from_before = shift(video_tb, -2), shift(video_ta, 2)
-    grad_vkv = (
-        video_th.astype(f32) + from_after.astype(f32) + from_before.astype(f32)
-    ).astype(bf)
-    grads = jnp.concatenate([grad_vq, grad_vkv], axis=0)
-    grads = grads.reshape(3, runs, 2, group, spreads, slim).transpose(1, 4, 2, 0, 3, 5)
-    grads = exchange(grads.reshape(frames, 6 * group, slim))
+    grads = gather(grad_vq, video_th, from_after, from_before, runs, spreads, group)
+    grads = exchange(grads)
     grads = place(match, grads, False)
-    grads = pair_exchange(grads.reshape(2 * frames, 3 * group, slim))
-    grads = assemble(grads, runs, spreads, group)
-
-    from_after, from_before = shift(audio_tb, -2), shift(audio_ta, 2)
-    grad_akv = (
-        audio_th.astype(f32) + from_after.astype(f32) + from_before.astype(f32)
-    ).astype(bf)
+    grads = exchange(grads)
+    other = swap(grads[:, 3 * group :])
+    grads = assemble(grads, other, runs, spreads, group)
+
+    shared_before, shared_after = shift(shared, 2), shift(shared, -2)
+    (grad_akv,) = side(
+        functools.partial(terms_kernel, group, count),
+        aud_len,
+        (shared_before, shared, shared_after, audio_here),
+        [(4 * audio_rows, half)],
+        (3 * block, 2 * audio_rows),
+    )
     mine = (
         grad_aq[:audio_rows],
         grad_akv[:audio_rows],

time: 169 us -> 162 us (0.959)
  starting transfers between devices: 71.9 us -> 66.8 us
  waiting for transfers between devices: 74.4 us -> 72 us
  Pallas kernels: 10.6 us -> 12.4 us
    all_to_all x2 -> x3, waiting for transfers between devices: 26.4 us -> 43.9 us  [exchange(): return lax.all_to_all(x, 'frame', split_axis=0, concat_axis=0, tiled=True)]
    all_to_all x2 -> x1, waiting for transfers between devices: 32.4 us -> 15.8 us  [pair_exchange(): lax.all_to_all(x, ('frame', 'seq'), split_axis=0, concat_axis=0, tiled=Tr...]
    ppermute x8, starting transfers between devices: 32.4 us -> 25.5 us  [shift(): lax.ppermute(x, 'seq', [(i, i + by) for i in range(count) if 0 <= i + by...]
    all_to_all x2 -> x1, starting transfers between devices: 20.7 us -> 16.1 us  [pair_exchange(): lax.all_to_all(x, ('frame', 'seq'), split_axis=0, concat_axis=0, tiled=Tr...]
    all_to_all x2 -> x3, starting transfers between devices: 14.7 us -> 19.3 us  [exchange(): return lax.all_to_all(x, 'frame', split_axis=0, concat_axis=0, tiled=True)]
    ppermute x8, waiting for transfers between devices: 15.6 us -> 11.7 us  [shift(): lax.ppermute(x, 'seq', [(i, i + by) for i in range(count) if 0 <= i + by...]
    convert_element_type x2 -> x0, other arithmetic: 1.91 us -> none  [the longest x1 1.79 us: shards(): grad_akv = (audio_th.astype(f32) + from_after.astype(f32) + from_before.a...]
    ppermute x2 -> x3, starting transfers between devices: 4.1 us -> 6.01 us  [swap(): return lax.ppermute(x, 'seq', [(i, i ^ 1) for i in range(count)])]
  transfers between devices with their start and end apart: 14 -> 15, of which waited for: 7 -> 9; matrix products, arithmetic and copies ran while one was open for 3% -> 2% of each run, Pallas kernels for 6% -> 7%
where the time goes in v6:
time: 162 us; the launch traced here: 159 us
  waiting for transfers between devices  72 us (44%)
  starting transfers between devices  66.8 us (41%)
  Pallas kernels  12.4 us (8%)
  other arithmetic  5.12 us (3%)
    all_to_all x3, waiting for transfers between devices, exchange(): return lax.all_to_all(x, 'frame', split_axis=0, concat_axis=0, tiled=True)  43.9 us
    ppermute x8, starting transfers between devices, shift(): lax.ppermute(x, 'seq', [(i, i + by) for i in range(count) if 0 <= i + by...  25.5 us
    all_to_all x3, starting transfers between devices, exchange(): return lax.all_to_all(x, 'frame', split_axis=0, concat_axis=0, tiled=True)  19.3 us
    all_to_all x1, starting transfers between devices, pair_exchange(): lax.all_to_all(x, ('frame', 'seq'), split_axis=0, concat_axis=0, tiled=Tr...  16.1 us
    all_to_all x1, waiting for transfers between devices, pair_exchange(): lax.all_to_all(x, ('frame', 'seq'), split_axis=0, concat_axis=0, tiled=Tr...  15.8 us
    ppermute x8, waiting for transfers between devices, shift(): lax.ppermute(x, 'seq', [(i, i + by) for i in range(count) if 0 <= i + by...  11.7 us
    pallas_call x3, Pallas kernels, side(): pl.pallas_call(kernel, in_specs=[SCALARS] + [ON_CHIP] * len(operands), ou...  8.13 us
    ppermute x3, starting transfers between devices, swap(): return lax.ppermute(x, 'seq', [(i, i ^ 1) for i in range(count)])  6.01 us
  transfers between devices with their start and end apart: 15, of which 9 were waited for; matrix products, arithmetic and copies ran while one was open for 2% of the time, Pallas kernels for 7%

profile of v6, /device:TPU:6, one launch (start us, length us, event | category | flops | bytes accessed | tf_op | source)
XLA Modules:
  0.0 158.5 jit_solution(6742721793549533667)
XLA Ops:
  0.6 2.0 %pad_maximum_fusion.3 = bf16[128,2048]{1,0:T(8,128)(2,1)} fusion(bf16[32,2048]{1,0:T(8,128)(2,1)} %bitcast.45, bf16[32,2048]{1,0:T(8,128)(2,1)} %bitcast.46, bf16[32,2048]{1,0:T(8,128)(2,1)} %bitcast.47, bf16[32,2048]{1,0:T(8,128)(2,1)} %bitcast.48), kind=kLoop, calls=%fused_computation.3 | loop fusion | flops 2097152 | bytes 1048576 | tf_op jit(solution)/shard_map/concatenate | solution.py:375
  2.6 16.1 %all-to-all-start = ((bf16[32,8,1024]{2,1,0:T(8,128)(2,1)}), bf16[32,8,1024]{2,1,0:T(8,128)(2,1)S(1)}, u32[]{:S(2)}, u32[]{:S(2)}) async-start(bf16[32,8,1024]{2,1,0:T(8,128)(2,1)} %bitcast.6), calls=%async_computation | async-start | bytes 1048576 | tf_op jit(solution)/shard_map/all_to_all | solution.py:360
  18.8 0.9 copy-done.5
  19.8 1.0 pad_maximum_fusion
  20.8 2.2 %collective-permute-start = (bf16[384,1024]{1,0:T(8,128)(2,1)}, bf16[384,1024]{1,0:T(8,128)(2,1)S(1)}, u32[]{:S(2)}, u32[]{:S(2)}) collective-permute-start(bf16[384,1024]{1,0:T(8,128)(2,1)} %pad_maximum_fusion), channel_id=1, source_target_pairs={{0,1},{1,0},{2,3},{3,2},{4,5},{5,4},{6,7},{7,6},{8,9},{9,8},{10,11... | collective-permute-start | bytes 2359304 | tf_op jit(solution)/shard_map/ppermute | solution.py:373
  23.0 15.8 %all-to-all-done = bf16[32,8,1024]{2,1,0:T(8,128)(2,1)S(1)} async-done(((bf16[32,8,1024]{2,1,0:T(8,128)(2,1)}), bf16[32,8,1024]{2,1,0:T(8,128)(2,1)S(1)}, u32[]{:S(2)}, u32[]{:S(2)}) %all-to-all-start) | async-done | bytes 524320 | tf_op jit(solution)/shard_map/all_to_all | solution.py:360
  38.8 1.4 place.2
  40.2 4.6 %all-to-all-start.1 = ((bf16[16,16,1024]{2,1,0:T(8,128)(2,1)}), bf16[16,16,1024]{2,1,0:T(8,128)(2,1)S(1)}, u32[]{:S(2)}, u32[]{:S(2)}) async-start(bf16[16,16,1024]{2,1,0:T(8,128)(2,1)} %place.2), calls=%async_computation.1 | async-start | bytes 1048576 | tf_op jit(solution)/shard_map/all_to_all | solution.py:365
  45.0 3.3 %collective-permute-start.1 = (bf16[384,1024]{1,0:T(8,128)(2,1)S(1)}, bf16[384,1024]{1,0:T(8,128)(2,1)}, u32[]{:S(2)}, u32[]{:S(2)}) collective-permute-start(bf16[384,1024]{1,0:T(8,128)(2,1)S(1)} %pad_maximum_fusion.1.here.audio), channel_id=1, source_target_pairs={{0,2},{1,3},{2,4},{3,5},{4,6},{5,7},{6,8},{7,9},{8,10},{9,11},{10,... | collective-permute-start | bytes 2359304 | tf_op jit(solution)/shard_map/ppermute | solution.py:368
  48.3 2.5 %collective-permute-start.2 = (bf16[384,1024]{1,0:T(8,128)(2,1)S(1)}, bf16[384,1024]{1,0:T(8,128)(2,1)}, u32[]{:S(2)}, u32[]{:S(2)}) collective-permute-start(bf16[384,1024]{1,0:T(8,128)(2,1)S(1)} %pad_maximum_fusion.1.here.audio), channel_id=1, source_target_pairs={{2,0},{3,1},{4,2},{5,3},{6,4},{7,5},{8,6},{9,7},{10,8},{11,9},{12,... | collective-permute-start | bytes 2359304 | tf_op jit(solution)/shard_map/ppermute | solution.py:368
  50.8 15.8 %all-to-all-done.1 = bf16[16,16,1024]{2,1,0:T(8,128)(2,1)S(1)} async-done(((bf16[16,16,1024]{2,1,0:T(8,128)(2,1)}), bf16[16,16,1024]{2,1,0:T(8,128)(2,1)S(1)}, u32[]{:S(2)}, u32[]{:S(2)}) %all-to-all-start.1) | async-done | bytes 524320 | tf_op jit(solution)/shard_map/all_to_all | solution.py:365
  66.7 3.3 %collective-permute-start.3 = (bf16[128,1024]{1,0:T(8,128)(2,1)S(1)}, bf16[128,1024]{1,0:T(8,128)(2,1)S(1)}, u32[]{:S(2)}, u32[]{:S(2)}) collective-permute-start(bf16[128,1024]{1,0:T(8,128)(2,1)S(1)} %bitcast.42), channel_id=1, source_target_pairs={{0,2},{1,3},{2,4},{3,5},{4,6},{5,7},{6,8},{7,9},{8,10},{9,11},{10,... | collective-permute-start | bytes 786440 | tf_op jit(solution)/shard_map/ppermute | solution.py:368
  70.0 2.5 %collective-permute-start.4 = (bf16[128,1024]{1,0:T(8,128)(2,1)S(1)}, bf16[128,1024]{1,0:T(8,128)(2,1)S(1)}, u32[]{:S(2)}, u32[]{:S(2)}) collective-permute-start(bf16[128,1024]{1,0:T(8,128)(2,1)S(1)} %bitcast.43), channel_id=1, source_target_pairs={{2,0},{3,1},{4,2},{5,3},{6,4},{7,5},{8,6},{9,7},{10,8},{11,9},{12,... | collective-permute-start | bytes 786440 | tf_op jit(solution)/shard_map/ppermute | solution.py:368
  72.5 3.9 %collective-permute-done.1.before = bf16[384,1024]{1,0:T(8,128)(2,1)} collective-permute-done((bf16[384,1024]{1,0:T(8,128)(2,1)S(1)}, bf16[384,1024]{1,0:T(8,128)(2,1)}, u32[]{:S(2)}, u32[]{:S(2)}) %collective-permute-start.1) | collective-permute-done | bytes 786464 | tf_op jit(solution)/shard_map/ppermute | solution.py:368
  76.4 3.3 %collective-permute-done.2.after = bf16[384,1024]{1,0:T(8,128)(2,1)} collective-permute-done((bf16[384,1024]{1,0:T(8,128)(2,1)S(1)}, bf16[384,1024]{1,0:T(8,128)(2,1)}, u32[]{:S(2)}, u32[]{:S(2)}) %collective-permute-start.2) | collective-permute-done | bytes 786464 | tf_op jit(solution)/shard_map/ppermute | solution.py:368
  79.7 2.8 %shard_map.145 = (bf16[64,1024]{1,0:T(8,128)(2,1)S(1)}, bf16[152,1024]{1,0:T(8,128)(2,1)S(1)}) custom-call(s32[16,32]{1,0:T(8,128)S(1)} %copy-done.2, bf16[256,1024]{1,0:T(8,128)(2,1)S(1)} %bitcast.38, bf16[384,1024]{1,0:T(8,128)(2,1)} %collective-permute-done.1.before, bf16[384,1024]{1,0:T(8,128)(2,1)S(1)} %pad_maximum_fusion.1.here.audio, ...), custom_call_target="tpu_custom_call" | custom-call | flops 377487360 | bytes 5242880 | tf_op jit(solution)/shard_map/pallas_call | solution.py:246
  82.6 3.3 %collective-permute-start.8 = (bf16[152,1024]{1,0:T(8,128)(2,1)S(1)}, bf16[152,1024]{1,0:T(8,128)(2,1)S(1)}, u32[]{:S(2)}, u32[]{:S(2)}) collective-permute-start(bf16[152,1024]{1,0:T(8,128)(2,1)S(1)} %get-tuple-element.23.here), channel_id=1, source_target_pairs={{0,2},{1,3},{2,4},{3,5},{4,6},{5,7},{6,8},{7,9},{8,10},{9,11},{10,... | collective-permute-start | bytes 933896 | tf_op jit(solution)/shard_map/ppermute | solution.py:368
  85.9 2.5 %collective-permute-start.9 = (bf16[152,1024]{1,0:T(8,128)(2,1)S(1)}, bf16[152,1024]{1,0:T(8,128)(2,1)}, u32[]{:S(2)}, u32[]{:S(2)}) collective-permute-start(bf16[152,1024]{1,0:T(8,128)(2,1)S(1)} %get-tuple-element.23.here), channel_id=1, source_target_pairs={{2,0},{3,1},{4,2},{5,3},{6,4},{7,5},{8,6},{9,7},{10,8},{11,9},{12,... | collective-permute-start | bytes 933896 | tf_op jit(solution)/shard_map/ppermute | solution.py:368
  88.4 2.6 %shard_map.146 = (bf16[192,1024]{1,0:T(8,128)(2,1)S(1)}, bf16[128,1024]{1,0:T(8,128)(2,1)S(1)}, bf16[128,1024]{1,0:T(8,128)(2,1)S(1)}, bf16[128,1024]{1,0:T(8,128)(2,1)S(1)}) custom-call(s32[16,32]{1,0:T(8,128)S(1)} %copy-done.2, bf16[96,2048]{1,0:T(8,128)(2,1)S(1)} %bitcast.41, bf16[96,2048]{1,0:T(8,128)(2,1)S(1)} %bitcast.40, ...), custom_call_target="tpu_custom_call" | custom-call | flops 377487360 | bytes 3145728 | tf_op jit(solution)/shard_map/pallas_call | solution.py:246
  91.1 1.9 %collective-permute-start.5 = (bf16[128,1024]{1,0:T(8,128)(2,1)S(1)}, bf16[128,1024]{1,0:T(8,128)(2,1)S(1)}, u32[]{:S(2)}, u32[]{:S(2)}) collective-permute-start(bf16[128,1024]{1,0:T(8,128)(2,1)S(1)} %get-tuple-element.17), channel_id=1, source_target_pairs={{2,0},{3,1},{4,2},{5,3},{6,4},{7,5},{8,6},{9,7},{10,8},{11,9},{12,... | collective-permute-start | bytes 786440 | tf_op jit(solution)/shard_map/ppermute | solution.py:368
  93.0 6.0 %collective-permute-start.6 = (bf16[128,1024]{1,0:T(8,128)(2,1)S(1)}, bf16[128,1024]{1,0:T(8,128)(2,1)S(1)}, u32[]{:S(2)}, u32[]{:S(2)}) collective-permute-start(bf16[128,1024]{1,0:T(8,128)(2,1)S(1)} %get-tuple-element.18), channel_id=1, source_target_pairs={{0,2},{1,3},{2,4},{3,5},{4,6},{5,7},{6,8},{7,9},{8,10},{9,11},{10,... | collective-permute-start | bytes 786440 | tf_op jit(solution)/shard_map/ppermute | solution.py:368
  99.1 3.9 %collective-permute-done.5.t1 = bf16[128,1024]{1,0:T(8,128)(2,1)S(1)} collective-permute-done((bf16[128,1024]{1,0:T(8,128)(2,1)S(1)}, bf16[128,1024]{1,0:T(8,128)(2,1)S(1)}, u32[]{:S(2)}, u32[]{:S(2)}) %collective-permute-start.5) | collective-permute-done | bytes 262176 | tf_op jit(solution)/shard_map/ppermute | solution.py:368
  103.5 0.8 gather.1
  104.4 11.1 %all-to-all-start.2 = ((bf16[16,48,256]{2,1,0:T(8,128)(2,1)}), bf16[16,48,256]{2,1,0:T(8,128)(2,1)S(1)}, u32[]{:S(2)}, u32[]{:S(2)}) async-start(bf16[16,48,256]{2,1,0:T(8,128)(2,1)} %gather.1), calls=%async_computation.2 | async-start | bytes 786432 | tf_op jit(solution)/shard_map/all_to_all | solution.py:365
  115.5 2.7 %shard_map.147 = bf16[384,1024]{1,0:T(8,128)(2,1)S(1)} custom-call(s32[16,32]{1,0:T(8,128)S(1)} %copy-done.2, bf16[152,1024]{1,0:T(8,128)(2,1)S(1)} %collective-permute-done.8.before, bf16[152,1024]{1,0:T(8,128)(2,1)S(1)} %get-tuple-element.23.here, bf16[152,1024]{1,0:T(8,128)(2,1)} %collective-permute-done.9.after, ...), custom_call_target="tpu_custom_call" | custom-call | flops 377487360 | bytes 3145728 | tf_op jit(solution)/shard_map/pallas_call | solution.py:246
  118.3 1.9 %collective-permute-start.10 = (bf16[288,1024]{1,0:T(8,128)(2,1)S(1)}, bf16[288,1024]{1,0:T(8,128)(2,1)S(1)}, u32[]{:S(2)}, u32[]{:S(2)}) collective-permute-start(bf16[288,1024]{1,0:T(8,128)(2,1)S(1)} %pad_maximum_fusion.2), channel_id=1, source_target_pairs={{0,1},{1,0},{2,3},{3,2},{4,5},{5,4},{6,7},{7,6},{8,9},{9,8},{10,11... | collective-permute-start | bytes 1769480 | tf_op jit(solution)/shard_map/ppermute | solution.py:373
  120.2 12.6 %all-to-all-done.2.x = bf16[16,48,256]{2,1,0:T(8,128)(2,1)S(1)} async-done(((bf16[16,48,256]{2,1,0:T(8,128)(2,1)}), bf16[16,48,256]{2,1,0:T(8,128)(2,1)S(1)}, u32[]{:S(2)}, u32[]{:S(2)}) %all-to-all-start.2) | async-done | bytes 393248 | tf_op jit(solution)/shard_map/all_to_all | solution.py:365
  132.8 1.3 place.3
  134.1 3.6 %all-to-all-start.3 = ((bf16[16,48,256]{2,1,0:T(8,128)(2,1)}), bf16[16,48,256]{2,1,0:T(8,128)(2,1)S(1)}, u32[]{:S(2)}, u32[]{:S(2)}) async-start(bf16[16,48,256]{2,1,0:T(8,128)(2,1)} %place.3), calls=%async_computation.3 | async-start | bytes 786432 | tf_op jit(solution)/shard_map/all_to_all | solution.py:365
  137.8 1.2 maximum_select_fusion
  138.9 15.5 %all-to-all-done.3.x = bf16[16,48,256]{2,1,0:T(8,128)(2,1)S(1)} async-done(((bf16[16,48,256]{2,1,0:T(8,128)(2,1)}), bf16[16,48,256]{2,1,0:T(8,128)(2,1)S(1)}, u32[]{:S(2)}, u32[]{:S(2)}) %all-to-all-start.3) | async-done | bytes 393248 | tf_op jit(solution)/shard_map/all_to_all | solution.py:365
  154.4 1.9 %collective-permute-start.7 = (bf16[16,24,256]{2,1,0:T(8,128)(2,1)S(1)}, bf16[16,24,256]{2,1,0:T(8,128)(2,1)S(1)}, u32[]{:S(2)}, u32[]{:S(2)}) collective-permute-start(bf16[16,24,256]{2,1,0:T(8,128)(2,1)S(1)} %slice.91), channel_id=1, source_target_pairs={{0,1},{1,0},{2,3},{3,2},{4,5},{5,4},{6,7},{7,6},{8,9},{9,8},{10,11... | collective-permute-start | bytes 589832 | tf_op jit(solution)/shard_map/ppermute | solution.py:373
  (33 shorter events, 3.3 us)
Async XLA Ops:
  2.6 16.1 %copy-start = (bf16[1,96,2048]{2,1,0:T(8,128)(2,1)S(1)}, bf16[1,96,2048]{2,1,0:T(8,128)(2,1)}, u32[]{:S(2)}) copy-start(bf16[1,96,2048]{2,1,0:T(8,128)(2,1)} %param.17) | copy-start | bytes 1179652
  2.6 16.1 %copy-start.4 = (bf16[1,96,2048]{2,1,0:T(8,128)(2,1)S(1)}, bf16[1,96,2048]{2,1,0:T(8,128)(2,1)}, u32[]{:S(2)}) copy-start(bf16[1,96,2048]{2,1,0:T(8,128)(2,1)} %param.16) | copy-start | bytes 1179652
  2.6 36.2 %all-to-all-start = ((bf16[32,8,1024]{2,1,0:T(8,128)(2,1)}), bf16[32,8,1024]{2,1,0:T(8,128)(2,1)S(1)}, u32[]{:S(2)}, u32[]{:S(2)}) async-start(bf16[32,8,1024]{2,1,0:T(8,128)(2,1)} %bitcast.6), calls=%async_computation | async-start | bytes 1048576 | tf_op jit(solution)/shard_map/all_to_all | solution.py:360
  18.7 1.0 copy-start.5
  18.8 1.1 copy-start.1
  19.8 19.0 %copy-start.3 = (s32[16]{0:T(128)S(1)}, s32[16]{0:T(128)}, u32[]{:S(2)}) copy-start(s32[16]{0:T(128)} %index.3) | copy-start | bytes 196
  20.8 24.0 %collective-permute-start = (bf16[384,1024]{1,0:T(8,128)(2,1)}, bf16[384,1024]{1,0:T(8,128)(2,1)S(1)}, u32[]{:S(2)}, u32[]{:S(2)}) collective-permute-start(bf16[384,1024]{1,0:T(8,128)(2,1)} %pad_maximum_fusion), channel_id=1, source_target_pairs={{0,1},{1,0},{2,3},{3,2},{4,5},{5,4},{6,7},{7,6},{8,9},{9,8},{10,11... | collective-permute-start | bytes 2359304 | tf_op jit(solution)/shard_map/ppermute | solution.py:373
  40.2 26.4 %all-to-all-start.1 = ((bf16[16,16,1024]{2,1,0:T(8,128)(2,1)}), bf16[16,16,1024]{2,1,0:T(8,128)(2,1)S(1)}, u32[]{:S(2)}, u32[]{:S(2)}) async-start(bf16[16,16,1024]{2,1,0:T(8,128)(2,1)} %place.2), calls=%async_computation.1 | async-start | bytes 1048576 | tf_op jit(solution)/shard_map/all_to_all | solution.py:365
  44.9 34.8 %copy-start.2 = (s32[16,32]{1,0:T(8,128)S(1)}, s32[16,32]{1,0:T(8,128)}, u32[]{:S(2)}) copy-start(s32[16,32]{1,0:T(8,128)} %lens.5) | copy-start | bytes 6148
  45.0 31.5 %collective-permute-start.1 = (bf16[384,1024]{1,0:T(8,128)(2,1)S(1)}, bf16[384,1024]{1,0:T(8,128)(2,1)}, u32[]{:S(2)}, u32[]{:S(2)}) collective-permute-start(bf16[384,1024]{1,0:T(8,128)(2,1)S(1)} %pad_maximum_fusion.1.here.audio), channel_id=1, source_target_pairs={{0,2},{1,3},{2,4},{3,5},{4,6},{5,7},{6,8},{7,9},{8,10},{9,11},{10,... | collective-permute-start | bytes 2359304 | tf_op jit(solution)/shard_map/ppermute | solution.py:368
  48.3 31.4 %collective-permute-start.2 = (bf16[384,1024]{1,0:T(8,128)(2,1)S(1)}, bf16[384,1024]{1,0:T(8,128)(2,1)}, u32[]{:S(2)}, u32[]{:S(2)}) collective-permute-start(bf16[384,1024]{1,0:T(8,128)(2,1)S(1)} %pad_maximum_fusion.1.here.audio), channel_id=1, source_target_pairs={{2,0},{3,1},{4,2},{5,3},{6,4},{7,5},{8,6},{9,7},{10,8},{11,9},{12,... | collective-permute-start | bytes 2359304 | tf_op jit(solution)/shard_map/ppermute | solution.py:368
  66.7 21.8 %collective-permute-start.3 = (bf16[128,1024]{1,0:T(8,128)(2,1)S(1)}, bf16[128,1024]{1,0:T(8,128)(2,1)S(1)}, u32[]{:S(2)}, u32[]{:S(2)}) collective-permute-start(bf16[128,1024]{1,0:T(8,128)(2,1)S(1)} %bitcast.42), channel_id=1, source_target_pairs={{0,2},{1,3},{2,4},{3,5},{4,6},{5,7},{6,8},{7,9},{8,10},{9,11},{10,... | collective-permute-start | bytes 786440 | tf_op jit(solution)/shard_map/ppermute | solution.py:368
  70.0 18.4 %collective-permute-start.4 = (bf16[128,1024]{1,0:T(8,128)(2,1)S(1)}, bf16[128,1024]{1,0:T(8,128)(2,1)S(1)}, u32[]{:S(2)}, u32[]{:S(2)}) collective-permute-start(bf16[128,1024]{1,0:T(8,128)(2,1)S(1)} %bitcast.43), channel_id=1, source_target_pairs={{2,0},{3,1},{4,2},{5,3},{6,4},{7,5},{8,6},{9,7},{10,8},{11,9},{12,... | collective-permute-start | bytes 786440 | tf_op jit(solution)/shard_map/ppermute | solution.py:368
  82.6 32.9 %collective-permute-start.8 = (bf16[152,1024]{1,0:T(8,128)(2,1)S(1)}, bf16[152,1024]{1,0:T(8,128)(2,1)S(1)}, u32[]{:S(2)}, u32[]{:S(2)}) collective-permute-start(bf16[152,1024]{1,0:T(8,128)(2,1)S(1)} %get-tuple-element.23.here), channel_id=1, source_target_pairs={{0,2},{1,3},{2,4},{3,5},{4,6},{5,7},{6,8},{7,9},{8,10},{9,11},{10,... | collective-permute-start | bytes 933896 | tf_op jit(solution)/shard_map/ppermute | solution.py:368
  85.9 29.6 %collective-permute-start.9 = (bf16[152,1024]{1,0:T(8,128)(2,1)S(1)}, bf16[152,1024]{1,0:T(8,128)(2,1)}, u32[]{:S(2)}, u32[]{:S(2)}) collective-permute-start(bf16[152,1024]{1,0:T(8,128)(2,1)S(1)} %get-tuple-element.23.here), channel_id=1, source_target_pairs={{2,0},{3,1},{4,2},{5,3},{6,4},{7,5},{8,6},{9,7},{10,8},{11,9},{12,... | collective-permute-start | bytes 933896 | tf_op jit(solution)/shard_map/ppermute | solution.py:368
  91.1 11.9 %collective-permute-start.5 = (bf16[128,1024]{1,0:T(8,128)(2,1)S(1)}, bf16[128,1024]{1,0:T(8,128)(2,1)S(1)}, u32[]{:S(2)}, u32[]{:S(2)}) collective-permute-start(bf16[128,1024]{1,0:T(8,128)(2,1)S(1)} %get-tuple-element.17), channel_id=1, source_target_pairs={{2,0},{3,1},{4,2},{5,3},{6,4},{7,5},{8,6},{9,7},{10,8},{11,9},{12,... | collective-permute-start | bytes 786440 | tf_op jit(solution)/shard_map/ppermute | solution.py:368
  93.0 10.5 %collective-permute-start.6 = (bf16[128,1024]{1,0:T(8,128)(2,1)S(1)}, bf16[128,1024]{1,0:T(8,128)(2,1)S(1)}, u32[]{:S(2)}, u32[]{:S(2)}) collective-permute-start(bf16[128,1024]{1,0:T(8,128)(2,1)S(1)} %get-tuple-element.18), channel_id=1, source_target_pairs={{0,2},{1,3},{2,4},{3,5},{4,6},{5,7},{6,8},{7,9},{8,10},{9,11},{10,... | collective-permute-start | bytes 786440 | tf_op jit(solution)/shard_map/ppermute | solution.py:368
  104.4 28.4 %all-to-all-start.2 = ((bf16[16,48,256]{2,1,0:T(8,128)(2,1)}), bf16[16,48,256]{2,1,0:T(8,128)(2,1)S(1)}, u32[]{:S(2)}, u32[]{:S(2)}) async-start(bf16[16,48,256]{2,1,0:T(8,128)(2,1)} %gather.1), calls=%async_computation.2 | async-start | bytes 786432 | tf_op jit(solution)/shard_map/all_to_all | solution.py:365
  118.3 19.4 %collective-permute-start.10 = (bf16[288,1024]{1,0:T(8,128)(2,1)S(1)}, bf16[288,1024]{1,0:T(8,128)(2,1)S(1)}, u32[]{:S(2)}, u32[]{:S(2)}) collective-permute-start(bf16[288,1024]{1,0:T(8,128)(2,1)S(1)} %pad_maximum_fusion.2), channel_id=1, source_target_pairs={{0,1},{1,0},{2,3},{3,2},{4,5},{5,4},{6,7},{7,6},{8,9},{9,8},{10,11... | collective-permute-start | bytes 1769480 | tf_op jit(solution)/shard_map/ppermute | solution.py:373
  134.1 20.2 %all-to-all-start.3 = ((bf16[16,48,256]{2,1,0:T(8,128)(2,1)}), bf16[16,48,256]{2,1,0:T(8,128)(2,1)S(1)}, u32[]{:S(2)}, u32[]{:S(2)}) async-start(bf16[16,48,256]{2,1,0:T(8,128)(2,1)} %place.3), calls=%async_computation.3 | async-start | bytes 786432 | tf_op jit(solution)/shard_map/all_to_all | solution.py:365
  154.4 3.3 %collective-permute-start.7 = (bf16[16,24,256]{2,1,0:T(8,128)(2,1)S(1)}, bf16[16,24,256]{2,1,0:T(8,128)(2,1)S(1)}, u32[]{:S(2)}, u32[]{:S(2)}) collective-permute-start(bf16[16,24,256]{2,1,0:T(8,128)(2,1)S(1)} %slice.91), channel_id=1, source_target_pairs={{0,1},{1,0},{2,3},{3,2},{4,5},{5,4},{6,7},{7,6},{8,9},{9,8},{10,11... | collective-permute-start | bytes 589832 | tf_op jit(solution)/shard_map/ppermute | solution.py:373

commit v7 on v6

--- a/solution.py
+++ b/solution.py
@@ -257,7 +257,6 @@
 
 def gather_kernel(runs, spreads, group, dq, th, t1, t2, out):
     rows, slim = dq.shape[0], out.shape[2]
-    core = lax.rem(lax.axis_index("seq"), 2)
     for run in range(runs):
         here = slice(run * 2 * group, (run + 1) * 2 * group)
         values = [dq[here]]
@@ -269,9 +268,8 @@
             cols = slice(spread * slim, (spread + 1) * slim)
             for late in range(2):
                 for j, value in enumerate(values):
-                    other = core if late == 0 else 1 - core
-                    left = pl.multiple_of((other * 3 + j) * group, group)
-                    out[run * spreads + spread, pl.ds(left, group)] = value[
+                    left = (late * 3 + j) * group
+                    out[run * spreads + spread, left : left + group] = value[
                         late * group : (late + 1) * group, cols
                     ]
 
@@ -312,31 +310,30 @@
     )(index, x)
 
 
-def assemble_kernel(runs, spreads, group, x, other, *outs):
+def assemble_kernel(runs, spreads, group, x, *outs):
     slim = x.shape[2]
-    half = spreads * slim
-    core = lax.rem(lax.axis_index("seq"), 2)
     for run in range(runs):
-        rows = slice(run * group, (run + 1) * group)
         for spread in range(spreads):
-            piece = run * spreads + spread
-            for source, start in ((x, core * half), (other, (1 - core) * half)):
-                cols = pl.ds(pl.multiple_of(start + spread * slim, HD), slim)
+            for core in range(2):
+                piece = (run * spreads + spread) * 2 + core
                 for j, out in enumerate(outs):
-                    out[0, rows, cols] = source[piece, j * group : (j + 1) * group]
-
-
-def assemble(x, other, runs, spreads, group):
+                    left = (core * spreads + spread) * slim
+                    out[0, run * group : (run + 1) * group, left : left + slim] = x[
+                        piece, j * group : (j + 1) * group, :
+                    ]
+
+
+def assemble(x, runs, spreads, group):
     shape = (1, runs * group, 2 * spreads * x.shape[2])
     return pl.pallas_call(
         functools.partial(assemble_kernel, runs, spreads, group),
-        in_specs=[ON_CHIP] * 2,
+        in_specs=[ON_CHIP],
         out_specs=[ON_CHIP] * 3,
         out_shape=[jax.ShapeDtypeStruct(shape, jnp.bfloat16)] * 3,
-        compiler_params=pltpu.CompilerParams(vmem_limit_bytes=GRANT // 4),
+        compiler_params=pltpu.CompilerParams(vmem_limit_bytes=GRANT),
         name="assemble",
         interpret=INTERPRET,
-    )(x, other)
+    )(x)
 
 
 def shards(vid_q, vid_k, vid_v, vid_dout, aud_q, aud_k, aud_v, aud_dout, aud_len, match):
@@ -350,6 +347,7 @@
     group = 4 * video_rows // frames
     runs = frames // 4
     spreads = frames // runs
+    slim = half // spreads
 
     pairs = [
         [f * count + 2 * c + k for f in range(frames) for k in range(2)]
@@ -423,9 +421,8 @@
     grads = gather(grad_vq, video_th, from_after, from_before, runs, spreads, group)
     grads = exchange(grads)
     grads = place(match, grads, False)
-    grads = exchange(grads)
-    other = swap(grads[:, 3 * group :])
-    grads = assemble(grads, other, runs, spreads, group)
+    grads = pair_exchange(grads.reshape(2 * frames, 3 * group, slim))
+    grads = assemble(grads, runs, spreads, group)
 
     shared_before, shared_after = shift(shared, 2), shift(shared, -2)
     (grad_akv,) = side(

time: 162 us -> 159 us (0.981)
    all_to_all x1 -> x2, waiting for transfers between devices: 15.8 us -> 31.6 us  [pair_exchange(): lax.all_to_all(x, ('frame', 'seq'), split_axis=0, concat_axis=0, tiled=Tr...]
    all_to_all x3 -> x2, waiting for transfers between devices: 43.9 us -> 31.1 us  [exchange(): return lax.all_to_all(x, 'frame', split_axis=0, concat_axis=0, tiled=True)]
    all_to_all x1 -> x2, starting transfers between devices: 16.1 us -> 19.9 us  [pair_exchange(): lax.all_to_all(x, ('frame', 'seq'), split_axis=0, concat_axis=0, tiled=Tr...]
    all_to_all x3 -> x2, starting transfers between devices: 19.3 us -> 15.7 us  [exchange(): return lax.all_to_all(x, 'frame', split_axis=0, concat_axis=0, tiled=True)]
    ppermute x8, waiting for transfers between devices: 11.7 us -> 9.25 us  [shift(): lax.ppermute(x, 'seq', [(i, i + by) for i in range(count) if 0 <= i + by...]
    ppermute x3 -> x2, starting transfers between devices: 6.01 us -> 4.09 us  [swap(): return lax.ppermute(x, 'seq', [(i, i ^ 1) for i in range(count)])]
  transfers between devices with their start and end apart: 15 -> 14, of which waited for: 9 -> 8; matrix products, arithmetic and copies ran while one was open for 2% -> 2% of each run, Pallas kernels for 7% -> 7%
where the time goes in v7:
time: 159 us; the launch traced here: 157 us
  waiting for transfers between devices  72 us (45%)
  starting transfers between devices  65.2 us (41%)
  Pallas kernels  12.1 us (8%)
  other arithmetic  5.12 us (3%)
    all_to_all x2, waiting for transfers between devices, pair_exchange(): lax.all_to_all(x, ('frame', 'seq'), split_axis=0, concat_axis=0, tiled=Tr...  31.6 us
    all_to_all x2, waiting for transfers between devices, exchange(): return lax.all_to_all(x, 'frame', split_axis=0, concat_axis=0, tiled=True)  31.1 us
    ppermute x8, starting transfers between devices, shift(): lax.ppermute(x, 'seq', [(i, i + by) for i in range(count) if 0 <= i + by...  25.5 us
    all_to_all x2, starting transfers between devices, pair_exchange(): lax.all_to_all(x, ('frame', 'seq'), split_axis=0, concat_axis=0, tiled=Tr...  19.9 us
    all_to_all x2, starting transfers between devices, exchange(): return lax.all_to_all(x, 'frame', split_axis=0, concat_axis=0, tiled=True)  15.7 us
    ppermute x8, waiting for transfers between devices, shift(): lax.ppermute(x, 'seq', [(i, i + by) for i in range(count) if 0 <= i + by...  9.25 us
    pallas_call x3, Pallas kernels, side(): pl.pallas_call(kernel, in_specs=[SCALARS] + [ON_CHIP] * len(operands), ou...  7.85 us
    ppermute x2, starting transfers between devices, swap(): return lax.ppermute(x, 'seq', [(i, i ^ 1) for i in range(count)])  4.09 us
  transfers between devices with their start and end apart: 14, of which 8 were waited for; matrix products, arithmetic and copies ran while one was open for 2% of the time, Pallas kernels for 7%

profile of v7, /device:TPU:6, one launch (start us, length us, event | category | flops | bytes accessed | tf_op | source)
XLA Modules:
  0.0 156.6 jit_solution(18341052201349020389)
XLA Ops:
  0.6 2.0 %pad_maximum_fusion.3 = bf16[128,2048]{1,0:T(8,128)(2,1)} fusion(bf16[32,2048]{1,0:T(8,128)(2,1)} %bitcast.46, bf16[32,2048]{1,0:T(8,128)(2,1)} %bitcast.47, bf16[32,2048]{1,0:T(8,128)(2,1)} %bitcast.48, bf16[32,2048]{1,0:T(8,128)(2,1)} %bitcast.49), kind=kLoop, calls=%fused_computation.3 | loop fusion | flops 2097152 | bytes 1048576 | tf_op jit(solution)/shard_map/concatenate | solution.py:373
  2.6 16.1 %all-to-all-start = ((bf16[32,8,1024]{2,1,0:T(8,128)(2,1)}), bf16[32,8,1024]{2,1,0:T(8,128)(2,1)S(1)}, u32[]{:S(2)}, u32[]{:S(2)}) async-start(bf16[32,8,1024]{2,1,0:T(8,128)(2,1)} %bitcast.6), calls=%async_computation | async-start | bytes 1048576 | tf_op jit(solution)/shard_map/all_to_all | solution.py:358
  18.8 0.9 copy-done.5
  19.8 1.0 pad_maximum_fusion
  20.8 2.2 %collective-permute-start = (bf16[384,1024]{1,0:T(8,128)(2,1)}, bf16[384,1024]{1,0:T(8,128)(2,1)S(1)}, u32[]{:S(2)}, u32[]{:S(2)}) collective-permute-start(bf16[384,1024]{1,0:T(8,128)(2,1)} %pad_maximum_fusion), channel_id=1, source_target_pairs={{0,1},{1,0},{2,3},{3,2},{4,5},{5,4},{6,7},{7,6},{8,9},{9,8},{10,11... | collective-permute-start | bytes 2359304 | tf_op jit(solution)/shard_map/ppermute | solution.py:371
  23.0 15.8 %all-to-all-done = bf16[32,8,1024]{2,1,0:T(8,128)(2,1)S(1)} async-done(((bf16[32,8,1024]{2,1,0:T(8,128)(2,1)}), bf16[32,8,1024]{2,1,0:T(8,128)(2,1)S(1)}, u32[]{:S(2)}, u32[]{:S(2)}) %all-to-all-start) | async-done | bytes 524320 | tf_op jit(solution)/shard_map/all_to_all | solution.py:358
  38.8 1.4 place.2
  40.2 4.6 %all-to-all-start.1 = ((bf16[16,16,1024]{2,1,0:T(8,128)(2,1)}), bf16[16,16,1024]{2,1,0:T(8,128)(2,1)S(1)}, u32[]{:S(2)}, u32[]{:S(2)}) async-start(bf16[16,16,1024]{2,1,0:T(8,128)(2,1)} %place.2), calls=%async_computation.1 | async-start | bytes 1048576 | tf_op jit(solution)/shard_map/all_to_all | solution.py:363
  45.0 3.3 %collective-permute-start.1 = (bf16[384,1024]{1,0:T(8,128)(2,1)S(1)}, bf16[384,1024]{1,0:T(8,128)(2,1)}, u32[]{:S(2)}, u32[]{:S(2)}) collective-permute-start(bf16[384,1024]{1,0:T(8,128)(2,1)S(1)} %pad_maximum_fusion.1.here.audio), channel_id=1, source_target_pairs={{0,2},{1,3},{2,4},{3,5},{4,6},{5,7},{6,8},{7,9},{8,10},{9,11},{10,... | collective-permute-start | bytes 2359304 | tf_op jit(solution)/shard_map/ppermute | solution.py:366
  48.3 2.5 %collective-permute-start.2 = (bf16[384,1024]{1,0:T(8,128)(2,1)S(1)}, bf16[384,1024]{1,0:T(8,128)(2,1)}, u32[]{:S(2)}, u32[]{:S(2)}) collective-permute-start(bf16[384,1024]{1,0:T(8,128)(2,1)S(1)} %pad_maximum_fusion.1.here.audio), channel_id=1, source_target_pairs={{2,0},{3,1},{4,2},{5,3},{6,4},{7,5},{8,6},{9,7},{10,8},{11,9},{12,... | collective-permute-start | bytes 2359304 | tf_op jit(solution)/shard_map/ppermute | solution.py:366
  50.8 15.8 %all-to-all-done.1 = bf16[16,16,1024]{2,1,0:T(8,128)(2,1)S(1)} async-done(((bf16[16,16,1024]{2,1,0:T(8,128)(2,1)}), bf16[16,16,1024]{2,1,0:T(8,128)(2,1)S(1)}, u32[]{:S(2)}, u32[]{:S(2)}) %all-to-all-start.1) | async-done | bytes 524320 | tf_op jit(solution)/shard_map/all_to_all | solution.py:363
  66.7 3.3 %collective-permute-start.3 = (bf16[128,1024]{1,0:T(8,128)(2,1)S(1)}, bf16[128,1024]{1,0:T(8,128)(2,1)S(1)}, u32[]{:S(2)}, u32[]{:S(2)}) collective-permute-start(bf16[128,1024]{1,0:T(8,128)(2,1)S(1)} %bitcast.43), channel_id=1, source_target_pairs={{0,2},{1,3},{2,4},{3,5},{4,6},{5,7},{6,8},{7,9},{8,10},{9,11},{10,... | collective-permute-start | bytes 786440 | tf_op jit(solution)/shard_map/ppermute | solution.py:366
  70.0 2.5 %collective-permute-start.4 = (bf16[128,1024]{1,0:T(8,128)(2,1)S(1)}, bf16[128,1024]{1,0:T(8,128)(2,1)S(1)}, u32[]{:S(2)}, u32[]{:S(2)}) collective-permute-start(bf16[128,1024]{1,0:T(8,128)(2,1)S(1)} %bitcast.44), channel_id=1, source_target_pairs={{2,0},{3,1},{4,2},{5,3},{6,4},{7,5},{8,6},{9,7},{10,8},{11,9},{12,... | collective-permute-start | bytes 786440 | tf_op jit(solution)/shard_map/ppermute | solution.py:366
  72.5 3.9 %collective-permute-done.1.before = bf16[384,1024]{1,0:T(8,128)(2,1)} collective-permute-done((bf16[384,1024]{1,0:T(8,128)(2,1)S(1)}, bf16[384,1024]{1,0:T(8,128)(2,1)}, u32[]{:S(2)}, u32[]{:S(2)}) %collective-permute-start.1) | collective-permute-done | bytes 786464 | tf_op jit(solution)/shard_map/ppermute | solution.py:366
  76.4 3.3 %collective-permute-done.2.after = bf16[384,1024]{1,0:T(8,128)(2,1)} collective-permute-done((bf16[384,1024]{1,0:T(8,128)(2,1)S(1)}, bf16[384,1024]{1,0:T(8,128)(2,1)}, u32[]{:S(2)}, u32[]{:S(2)}) %collective-permute-start.2) | collective-permute-done | bytes 786464 | tf_op jit(solution)/shard_map/ppermute | solution.py:366
  79.7 2.8 %shard_map.145 = (bf16[64,1024]{1,0:T(8,128)(2,1)S(1)}, bf16[152,1024]{1,0:T(8,128)(2,1)S(1)}) custom-call(s32[16,32]{1,0:T(8,128)S(1)} %copy-done.2, bf16[256,1024]{1,0:T(8,128)(2,1)S(1)} %bitcast.39, bf16[384,1024]{1,0:T(8,128)(2,1)} %collective-permute-done.1.before, bf16[384,1024]{1,0:T(8,128)(2,1)S(1)} %pad_maximum_fusion.1.here.audio, ...), custom_call_target="tpu_custom_call" | custom-call | flops 377487360 | bytes 5242880 | tf_op jit(solution)/shard_map/pallas_call | solution.py:246
  82.6 3.3 %collective-permute-start.7 = (bf16[152,1024]{1,0:T(8,128)(2,1)S(1)}, bf16[152,1024]{1,0:T(8,128)(2,1)S(1)}, u32[]{:S(2)}, u32[]{:S(2)}) collective-permute-start(bf16[152,1024]{1,0:T(8,128)(2,1)S(1)} %get-tuple-element.23.here), channel_id=1, source_target_pairs={{0,2},{1,3},{2,4},{3,5},{4,6},{5,7},{6,8},{7,9},{8,10},{9,11},{10,... | collective-permute-start | bytes 933896 | tf_op jit(solution)/shard_map/ppermute | solution.py:366
  85.9 2.5 %collective-permute-start.8 = (bf16[152,1024]{1,0:T(8,128)(2,1)S(1)}, bf16[152,1024]{1,0:T(8,128)(2,1)S(1)}, u32[]{:S(2)}, u32[]{:S(2)}) collective-permute-start(bf16[152,1024]{1,0:T(8,128)(2,1)S(1)} %get-tuple-element.23.here), channel_id=1, source_target_pairs={{2,0},{3,1},{4,2},{5,3},{6,4},{7,5},{8,6},{9,7},{10,8},{11,9},{12,... | collective-permute-start | bytes 933896 | tf_op jit(solution)/shard_map/ppermute | solution.py:366
  88.4 2.6 %shard_map.146 = (bf16[192,1024]{1,0:T(8,128)(2,1)S(1)}, bf16[128,1024]{1,0:T(8,128)(2,1)S(1)}, bf16[128,1024]{1,0:T(8,128)(2,1)S(1)}, bf16[128,1024]{1,0:T(8,128)(2,1)S(1)}) custom-call(s32[16,32]{1,0:T(8,128)S(1)} %copy-done.2, bf16[96,2048]{1,0:T(8,128)(2,1)S(1)} %bitcast.42, bf16[96,2048]{1,0:T(8,128)(2,1)S(1)} %bitcast.41, ...), custom_call_target="tpu_custom_call" | custom-call | flops 377487360 | bytes 3145728 | tf_op jit(solution)/shard_map/pallas_call | solution.py:246
  91.1 1.9 %collective-permute-start.5 = (bf16[128,1024]{1,0:T(8,128)(2,1)S(1)}, bf16[128,1024]{1,0:T(8,128)(2,1)S(1)}, u32[]{:S(2)}, u32[]{:S(2)}) collective-permute-start(bf16[128,1024]{1,0:T(8,128)(2,1)S(1)} %get-tuple-element.17), channel_id=1, source_target_pairs={{2,0},{3,1},{4,2},{5,3},{6,4},{7,5},{8,6},{9,7},{10,8},{11,9},{12,... | collective-permute-start | bytes 786440 | tf_op jit(solution)/shard_map/ppermute | solution.py:366
  93.0 6.0 %collective-permute-start.6 = (bf16[128,1024]{1,0:T(8,128)(2,1)S(1)}, bf16[128,1024]{1,0:T(8,128)(2,1)S(1)}, u32[]{:S(2)}, u32[]{:S(2)}) collective-permute-start(bf16[128,1024]{1,0:T(8,128)(2,1)S(1)} %get-tuple-element.18), channel_id=1, source_target_pairs={{0,2},{1,3},{2,4},{3,5},{4,6},{5,7},{6,8},{7,9},{8,10},{9,11},{10,... | collective-permute-start | bytes 786440 | tf_op jit(solution)/shard_map/ppermute | solution.py:366
  99.1 2.4 %shard_map.147 = bf16[384,1024]{1,0:T(8,128)(2,1)S(1)} custom-call(s32[16,32]{1,0:T(8,128)S(1)} %copy-done.2, bf16[152,1024]{1,0:T(8,128)(2,1)S(1)} %collective-permute-done.7.before, bf16[152,1024]{1,0:T(8,128)(2,1)S(1)} %get-tuple-element.23.here, bf16[152,1024]{1,0:T(8,128)(2,1)S(1)} %collective-permute-done.8.after, ...), custom_call_target="tpu_custom_call" | custom-call | flops 377487360 | bytes 3145728 | tf_op jit(solution)/shard_map/pallas_call | solution.py:246
  101.5 1.5 collective-permute-done.5.t1
  103.5 0.8 gather.1
  104.4 11.1 %all-to-all-start.2 = ((bf16[16,48,256]{2,1,0:T(8,128)(2,1)}), bf16[16,48,256]{2,1,0:T(8,128)(2,1)S(1)}, u32[]{:S(2)}, u32[]{:S(2)}) async-start(bf16[16,48,256]{2,1,0:T(8,128)(2,1)} %gather.1), calls=%async_computation.2 | async-start | bytes 786432 | tf_op jit(solution)/shard_map/all_to_all | solution.py:363
  115.6 1.9 %collective-permute-start.9 = (bf16[288,1024]{1,0:T(8,128)(2,1)S(1)}, bf16[288,1024]{1,0:T(8,128)(2,1)S(1)}, u32[]{:S(2)}, u32[]{:S(2)}) collective-permute-start(bf16[288,1024]{1,0:T(8,128)(2,1)S(1)} %pad_maximum_fusion.2), channel_id=1, source_target_pairs={{0,1},{1,0},{2,3},{3,2},{4,5},{5,4},{6,7},{7,6},{8,9},{9,8},{10,11... | collective-permute-start | bytes 1769480 | tf_op jit(solution)/shard_map/ppermute | solution.py:371
  117.5 15.3 %all-to-all-done.2.x = bf16[16,48,256]{2,1,0:T(8,128)(2,1)S(1)} async-done(((bf16[16,48,256]{2,1,0:T(8,128)(2,1)}), bf16[16,48,256]{2,1,0:T(8,128)(2,1)S(1)}, u32[]{:S(2)}, u32[]{:S(2)}) %all-to-all-start.2) | async-done | bytes 393248 | tf_op jit(solution)/shard_map/all_to_all | solution.py:363
  132.8 1.3 place.3
  134.1 3.9 %all-to-all-start.3 = ((bf16[32,24,256]{2,1,0:T(8,128)(2,1)}), bf16[32,24,256]{2,1,0:T(8,128)(2,1)S(1)}, u32[]{:S(2)}, u32[]{:S(2)}) async-start(bf16[32,24,256]{2,1,0:T(8,128)(2,1)} %bitcast.18), calls=%async_computation.3 | async-start | bytes 786432 | tf_op jit(solution)/shard_map/all_to_all | solution.py:358
  138.1 0.8 maximum_select_fusion.2
  138.9 1.2 maximum_select_fusion
  140.1 15.7 %all-to-all-done.3.x = bf16[32,24,256]{2,1,0:T(8,128)(2,1)S(1)} async-done(((bf16[32,24,256]{2,1,0:T(8,128)(2,1)}), bf16[32,24,256]{2,1,0:T(8,128)(2,1)S(1)}, u32[]{:S(2)}, u32[]{:S(2)}) %all-to-all-start.3) | async-done | bytes 393248 | tf_op jit(solution)/shard_map/all_to_all | solution.py:358
  (30 shorter events, 1.8 us)
Async XLA Ops:
  2.6 16.1 %copy-start = (bf16[1,96,2048]{2,1,0:T(8,128)(2,1)S(1)}, bf16[1,96,2048]{2,1,0:T(8,128)(2,1)}, u32[]{:S(2)}) copy-start(bf16[1,96,2048]{2,1,0:T(8,128)(2,1)} %param.17) | copy-start | bytes 1179652
  2.6 16.1 %copy-start.4 = (bf16[1,96,2048]{2,1,0:T(8,128)(2,1)S(1)}, bf16[1,96,2048]{2,1,0:T(8,128)(2,1)}, u32[]{:S(2)}) copy-start(bf16[1,96,2048]{2,1,0:T(8,128)(2,1)} %param.16) | copy-start | bytes 1179652
  2.6 36.2 %all-to-all-start = ((bf16[32,8,1024]{2,1,0:T(8,128)(2,1)}), bf16[32,8,1024]{2,1,0:T(8,128)(2,1)S(1)}, u32[]{:S(2)}, u32[]{:S(2)}) async-start(bf16[32,8,1024]{2,1,0:T(8,128)(2,1)} %bitcast.6), calls=%async_computation | async-start | bytes 1048576 | tf_op jit(solution)/shard_map/all_to_all | solution.py:358
  18.7 1.0 copy-start.5
  18.7 1.1 copy-start.1
  19.8 19.0 %copy-start.3 = (s32[16]{0:T(128)S(1)}, s32[16]{0:T(128)}, u32[]{:S(2)}) copy-start(s32[16]{0:T(128)} %index.3) | copy-start | bytes 196
  20.8 24.0 %collective-permute-start = (bf16[384,1024]{1,0:T(8,128)(2,1)}, bf16[384,1024]{1,0:T(8,128)(2,1)S(1)}, u32[]{:S(2)}, u32[]{:S(2)}) collective-permute-start(bf16[384,1024]{1,0:T(8,128)(2,1)} %pad_maximum_fusion), channel_id=1, source_target_pairs={{0,1},{1,0},{2,3},{3,2},{4,5},{5,4},{6,7},{7,6},{8,9},{9,8},{10,11... | collective-permute-start | bytes 2359304 | tf_op jit(solution)/shard_map/ppermute | solution.py:371
  40.2 26.4 %all-to-all-start.1 = ((bf16[16,16,1024]{2,1,0:T(8,128)(2,1)}), bf16[16,16,1024]{2,1,0:T(8,128)(2,1)S(1)}, u32[]{:S(2)}, u32[]{:S(2)}) async-start(bf16[16,16,1024]{2,1,0:T(8,128)(2,1)} %place.2), calls=%async_computation.1 | async-start | bytes 1048576 | tf_op jit(solution)/shard_map/all_to_all | solution.py:363
  44.9 34.8 %copy-start.2 = (s32[16,32]{1,0:T(8,128)S(1)}, s32[16,32]{1,0:T(8,128)}, u32[]{:S(2)}) copy-start(s32[16,32]{1,0:T(8,128)} %lens.5) | copy-start | bytes 6148
  45.0 31.5 %collective-permute-start.1 = (bf16[384,1024]{1,0:T(8,128)(2,1)S(1)}, bf16[384,1024]{1,0:T(8,128)(2,1)}, u32[]{:S(2)}, u32[]{:S(2)}) collective-permute-start(bf16[384,1024]{1,0:T(8,128)(2,1)S(1)} %pad_maximum_fusion.1.here.audio), channel_id=1, source_target_pairs={{0,2},{1,3},{2,4},{3,5},{4,6},{5,7},{6,8},{7,9},{8,10},{9,11},{10,... | collective-permute-start | bytes 2359304 | tf_op jit(solution)/shard_map/ppermute | solution.py:366
  48.3 31.4 %collective-permute-start.2 = (bf16[384,1024]{1,0:T(8,128)(2,1)S(1)}, bf16[384,1024]{1,0:T(8,128)(2,1)}, u32[]{:S(2)}, u32[]{:S(2)}) collective-permute-start(bf16[384,1024]{1,0:T(8,128)(2,1)S(1)} %pad_maximum_fusion.1.here.audio), channel_id=1, source_target_pairs={{2,0},{3,1},{4,2},{5,3},{6,4},{7,5},{8,6},{9,7},{10,8},{11,9},{12,... | collective-permute-start | bytes 2359304 | tf_op jit(solution)/shard_map/ppermute | solution.py:366
  66.7 21.8 %collective-permute-start.3 = (bf16[128,1024]{1,0:T(8,128)(2,1)S(1)}, bf16[128,1024]{1,0:T(8,128)(2,1)S(1)}, u32[]{:S(2)}, u32[]{:S(2)}) collective-permute-start(bf16[128,1024]{1,0:T(8,128)(2,1)S(1)} %bitcast.43), channel_id=1, source_target_pairs={{0,2},{1,3},{2,4},{3,5},{4,6},{5,7},{6,8},{7,9},{8,10},{9,11},{10,... | collective-permute-start | bytes 786440 | tf_op jit(solution)/shard_map/ppermute | solution.py:366
  70.0 18.4 %collective-permute-start.4 = (bf16[128,1024]{1,0:T(8,128)(2,1)S(1)}, bf16[128,1024]{1,0:T(8,128)(2,1)S(1)}, u32[]{:S(2)}, u32[]{:S(2)}) collective-permute-start(bf16[128,1024]{1,0:T(8,128)(2,1)S(1)} %bitcast.44), channel_id=1, source_target_pairs={{2,0},{3,1},{4,2},{5,3},{6,4},{7,5},{8,6},{9,7},{10,8},{11,9},{12,... | collective-permute-start | bytes 786440 | tf_op jit(solution)/shard_map/ppermute | solution.py:366
  82.6 16.5 %collective-permute-start.7 = (bf16[152,1024]{1,0:T(8,128)(2,1)S(1)}, bf16[152,1024]{1,0:T(8,128)(2,1)S(1)}, u32[]{:S(2)}, u32[]{:S(2)}) collective-permute-start(bf16[152,1024]{1,0:T(8,128)(2,1)S(1)} %get-tuple-element.23.here), channel_id=1, source_target_pairs={{0,2},{1,3},{2,4},{3,5},{4,6},{5,7},{6,8},{7,9},{8,10},{9,11},{10,... | collective-permute-start | bytes 933896 | tf_op jit(solution)/shard_map/ppermute | solution.py:366
  85.9 13.2 %collective-permute-start.8 = (bf16[152,1024]{1,0:T(8,128)(2,1)S(1)}, bf16[152,1024]{1,0:T(8,128)(2,1)S(1)}, u32[]{:S(2)}, u32[]{:S(2)}) collective-permute-start(bf16[152,1024]{1,0:T(8,128)(2,1)S(1)} %get-tuple-element.23.here), channel_id=1, source_target_pairs={{2,0},{3,1},{4,2},{5,3},{6,4},{7,5},{8,6},{9,7},{10,8},{11,9},{12,... | collective-permute-start | bytes 933896 | tf_op jit(solution)/shard_map/ppermute | solution.py:366
  91.1 11.9 %collective-permute-start.5 = (bf16[128,1024]{1,0:T(8,128)(2,1)S(1)}, bf16[128,1024]{1,0:T(8,128)(2,1)S(1)}, u32[]{:S(2)}, u32[]{:S(2)}) collective-permute-start(bf16[128,1024]{1,0:T(8,128)(2,1)S(1)} %get-tuple-element.17), channel_id=1, source_target_pairs={{2,0},{3,1},{4,2},{5,3},{6,4},{7,5},{8,6},{9,7},{10,8},{11,9},{12,... | collective-permute-start | bytes 786440 | tf_op jit(solution)/shard_map/ppermute | solution.py:366
  93.0 10.5 %collective-permute-start.6 = (bf16[128,1024]{1,0:T(8,128)(2,1)S(1)}, bf16[128,1024]{1,0:T(8,128)(2,1)S(1)}, u32[]{:S(2)}, u32[]{:S(2)}) collective-permute-start(bf16[128,1024]{1,0:T(8,128)(2,1)S(1)} %get-tuple-element.18), channel_id=1, source_target_pairs={{0,2},{1,3},{2,4},{3,5},{4,6},{5,7},{6,8},{7,9},{8,10},{9,11},{10,... | collective-permute-start | bytes 786440 | tf_op jit(solution)/shard_map/ppermute | solution.py:366
  104.4 28.4 %all-to-all-start.2 = ((bf16[16,48,256]{2,1,0:T(8,128)(2,1)}), bf16[16,48,256]{2,1,0:T(8,128)(2,1)S(1)}, u32[]{:S(2)}, u32[]{:S(2)}) async-start(bf16[16,48,256]{2,1,0:T(8,128)(2,1)} %gather.1), calls=%async_computation.2 | async-start | bytes 786432 | tf_op jit(solution)/shard_map/all_to_all | solution.py:363
  115.6 22.4 %collective-permute-start.9 = (bf16[288,1024]{1,0:T(8,128)(2,1)S(1)}, bf16[288,1024]{1,0:T(8,128)(2,1)S(1)}, u32[]{:S(2)}, u32[]{:S(2)}) collective-permute-start(bf16[288,1024]{1,0:T(8,128)(2,1)S(1)} %pad_maximum_fusion.2), channel_id=1, source_target_pairs={{0,1},{1,0},{2,3},{3,2},{4,5},{5,4},{6,7},{7,6},{8,9},{9,8},{10,11... | collective-permute-start | bytes 1769480 | tf_op jit(solution)/shard_map/ppermute | solution.py:371
  134.1 21.7 %all-to-all-start.3 = ((bf16[32,24,256]{2,1,0:T(8,128)(2,1)}), bf16[32,24,256]{2,1,0:T(8,128)(2,1)S(1)}, u32[]{:S(2)}, u32[]{:S(2)}) async-start(bf16[32,24,256]{2,1,0:T(8,128)(2,1)} %bitcast.18), calls=%async_computation.3 | async-start | bytes 786432 | tf_op jit(solution)/shard_map/all_to_all | solution.py:358

commit v8 on v7

--- a/solution.py
+++ b/solution.py
@@ -22,6 +22,30 @@
         (((left_dim,), (right_dim,)), ((), ())),
         preferred_element_type=jnp.float32,
     )
+
+
+def attend_turned(queries, keys, values, grads, bias):
+    total = len(queries)
+    scores, grad_weights, half, grad_scores, results = {}, {}, {}, {}, []
+    for step in range(total + 2):
+        if step < total:
+            scores[step] = contract(keys[step], queries[step], 1, 1) * FACTOR + bias[...]
+            grad_weights[step] = contract(values[step], grads[step], 1, 1)
+        h = step - 1
+        if 0 <= h < total:
+            exponent = jnp.exp(scores[h] - jnp.max(scores[h], axis=0, keepdims=True))
+            weights = exponent * (1.0 / jnp.sum(exponent, axis=0, keepdims=True))
+            half[h] = weights.astype(jnp.bfloat16)
+            delta = jnp.sum(
+                half[h].astype(jnp.float32) * grad_weights[h], axis=0, keepdims=True
+            )
+            grad_scores[h] = (weights * (grad_weights[h] - delta)).astype(jnp.bfloat16)
+        h = step - 2
+        if 0 <= h < total:
+            key_terms = contract(grad_scores[h], queries[h], 1, 0) * FACTOR
+            value_terms = contract(half[h], grads[h], 1, 0)
+            results.append((contract(grad_scores[h], keys[h], 0, 0) * FACTOR, key_terms, value_terms))
+    return zip(*results)
 
 
 def attend(queries, keys, values, grads, bias):
@@ -191,16 +215,13 @@
     core = lax.rem(block, 2)
     base = block - core
     other = base + 1 - core
-    column = lax.broadcasted_iota(jnp.int32, (1, 3 * part), 1)
-    offset = 2 * (column // part) - 2 + (column // group) % 2
+    key = lax.broadcasted_iota(jnp.int32, (3 * part, 1), 0)
+    offset = 2 * (key // part) - 2 + (key // group) % 2
     known = (base + offset >= 0) & (base + offset < count)
-
-    for j, own in enumerate((core, 1 - core)):
-        seen = known & (jnp.abs(offset - own) <= BAND)
-        bias[j * rows : (j + 1) * rows] = jnp.broadcast_to(
-            jnp.where(seen, 0.0, NEG_BIG), (rows, 3 * part)
-        )
-
+    query = lax.broadcasted_iota(jnp.int32, (1, 2 * rows), 1)
+    own = jnp.where(query < rows, core, 1 - core)
+    near = jnp.where(known, 0.0, NEG_BIG)
+    bias[...] = jnp.where(jnp.abs(offset - own) <= BAND, near, NEG_BIG)
     slot = lax.broadcasted_iota(jnp.int32, (rows, 1), 0)
     live_mine = (slot < lens[frame, block]).astype(jnp.float32)
     live_other = (slot < lens[frame, other]).astype(jnp.float32)
@@ -217,8 +238,7 @@
         ]
         grads.append(jnp.concatenate(kept, axis=0).astype(jnp.bfloat16))
     keys, values = zip(*[windows((before, here, after), part, cols) for cols in spans])
-    grad_query, weights, grad_scores, _ = attend(queries, keys, values, grads, bias)
-    key_terms, value_terms = terms(queries, grads, weights, grad_scores)
+    grad_query, key_terms, value_terms = attend_turned(queries, keys, values, grads, bias)
     for h, cols in enumerate(spans):
         dq_ref[:, cols] = grad_query[h].astype(jnp.bfloat16)
         for place, out in enumerate((tb, th, ta)):
@@ -289,19 +309,24 @@
     )(dq, th, t1, t2)
 
 
-def place_kernel(spread, index, x, out):
+def place_kernel(spread, index, x, out, sems):
+    copies = []
     for frame in range(x.shape[0]):
-        if spread:
-            out[index[frame]] = x[frame]
-        else:
-            out[frame] = x[index[frame]]
+        source = x.at[frame] if spread else x.at[index[frame]]
+        target = out.at[index[frame]] if spread else out.at[frame]
+        copies.append(pltpu.make_async_copy(source, target, sems.at[frame]))
+    for copy in copies:
+        copy.start()
+    for copy in copies:
+        copy.wait()
 
 
 def place(index, x, spread):
     return pl.pallas_call(
         functools.partial(place_kernel, spread),
         in_specs=[SCALARS, ON_CHIP],
-        out_specs=ON_CHIP,
+        out_specs=pl.BlockSpec(memory_space=pl.ANY),
+        scratch_shapes=[pltpu.SemaphoreType.DMA((x.shape[0],))],
         out_shape=jax.ShapeDtypeStruct(x.shape, x.dtype),
         compiler_params=pltpu.CompilerParams(vmem_limit_bytes=GRANT // 4),
         cost_estimate=pl.CostEstimate(flops=0, bytes_accessed=4 * x.size, transcendentals=0),
@@ -414,7 +439,7 @@
         aud_len,
         (aud_q[0], aud_dout[0], theirs, video_before, video_here, video_after),
         [(2 * audio_rows, half)] + [(2 * block, half)] * 3,
-        (2 * audio_rows, 3 * block),
+        (3 * block, 2 * audio_rows),
     )
 
     from_after, from_before = shift(video_tb, -2), shift(video_ta, 2)

time: 159 us -> 159 us (level)
  no operation moved by 1% of the time
where the time goes in v8:
time: 159 us; the launch traced here: 157 us
  waiting for transfers between devices  72.2 us (45%)
  starting transfers between devices  65.3 us (41%)
  Pallas kernels  12.1 us (8%)
  other arithmetic  5.12 us (3%)
    all_to_all x2, waiting for transfers between devices, pair_exchange(): lax.all_to_all(x, ('frame', 'seq'), split_axis=0, concat_axis=0, tiled=Tr...  31.5 us
    all_to_all x2, waiting for transfers between devices, exchange(): return lax.all_to_all(x, 'frame', split_axis=0, concat_axis=0, tiled=True)  31.4 us
    ppermute x8, starting transfers between devices, shift(): lax.ppermute(x, 'seq', [(i, i + by) for i in range(count) if 0 <= i + by...  25.5 us
    all_to_all x2, starting transfers between devices, pair_exchange(): lax.all_to_all(x, ('frame', 'seq'), split_axis=0, concat_axis=0, tiled=Tr...  20 us
    all_to_all x2, starting transfers between devices, exchange(): return lax.all_to_all(x, 'frame', split_axis=0, concat_axis=0, tiled=True)  15.7 us
    ppermute x8, waiting for transfers between devices, shift(): lax.ppermute(x, 'seq', [(i, i + by) for i in range(count) if 0 <= i + by...  9.25 us
    pallas_call x3, Pallas kernels, side(): pl.pallas_call(kernel, in_specs=[SCALARS] + [ON_CHIP] * len(operands), ou...  7.63 us
    ppermute x2, starting transfers between devices, swap(): return lax.ppermute(x, 'seq', [(i, i ^ 1) for i in range(count)])  4.09 us
  transfers between devices with their start and end apart: 14, of which 8 were waited for; matrix products, arithmetic and copies ran while one was open for 2% of the time, Pallas kernels for 7%

profile of v8, /device:TPU:6, one launch (start us, length us, event | category | flops | bytes accessed | tf_op | source)
XLA Modules:
  0.0 156.9 jit_solution(2128375902660767028)
XLA Ops:
  0.6 2.0 %pad_maximum_fusion.3 = bf16[128,2048]{1,0:T(8,128)(2,1)} fusion(bf16[32,2048]{1,0:T(8,128)(2,1)} %bitcast.46, bf16[32,2048]{1,0:T(8,128)(2,1)} %bitcast.47, bf16[32,2048]{1,0:T(8,128)(2,1)} %bitcast.48, bf16[32,2048]{1,0:T(8,128)(2,1)} %bitcast.49), kind=kLoop, calls=%fused_computation.3 | loop fusion | flops 2097152 | bytes 1048576 | tf_op jit(solution)/shard_map/concatenate | solution.py:398
  2.6 16.1 %all-to-all-start = ((bf16[32,8,1024]{2,1,0:T(8,128)(2,1)}), bf16[32,8,1024]{2,1,0:T(8,128)(2,1)S(1)}, u32[]{:S(2)}, u32[]{:S(2)}) async-start(bf16[32,8,1024]{2,1,0:T(8,128)(2,1)} %bitcast.6), calls=%async_computation | async-start | bytes 1048576 | tf_op jit(solution)/shard_map/all_to_all | solution.py:383
  18.8 0.9 copy-done.5
  19.8 1.0 pad_maximum_fusion
  20.8 2.2 %collective-permute-start = (bf16[384,1024]{1,0:T(8,128)(2,1)}, bf16[384,1024]{1,0:T(8,128)(2,1)S(1)}, u32[]{:S(2)}, u32[]{:S(2)}) collective-permute-start(bf16[384,1024]{1,0:T(8,128)(2,1)} %pad_maximum_fusion), channel_id=1, source_target_pairs={{0,1},{1,0},{2,3},{3,2},{4,5},{5,4},{6,7},{7,6},{8,9},{9,8},{10,11... | collective-permute-start | bytes 2359304 | tf_op jit(solution)/shard_map/ppermute | solution.py:396
  23.0 15.8 %all-to-all-done = bf16[32,8,1024]{2,1,0:T(8,128)(2,1)S(1)} async-done(((bf16[32,8,1024]{2,1,0:T(8,128)(2,1)}), bf16[32,8,1024]{2,1,0:T(8,128)(2,1)S(1)}, u32[]{:S(2)}, u32[]{:S(2)}) %all-to-all-start) | async-done | bytes 524320 | tf_op jit(solution)/shard_map/all_to_all | solution.py:383
  38.8 1.5 place.2
  40.3 4.6 %all-to-all-start.1 = ((bf16[16,16,1024]{2,1,0:T(8,128)(2,1)}), bf16[16,16,1024]{2,1,0:T(8,128)(2,1)S(1)}, u32[]{:S(2)}, u32[]{:S(2)}) async-start(bf16[16,16,1024]{2,1,0:T(8,128)(2,1)} %place.2), calls=%async_computation.1 | async-start | bytes 1048576 | tf_op jit(solution)/shard_map/all_to_all | solution.py:388
  45.1 3.3 %collective-permute-start.1 = (bf16[384,1024]{1,0:T(8,128)(2,1)S(1)}, bf16[384,1024]{1,0:T(8,128)(2,1)}, u32[]{:S(2)}, u32[]{:S(2)}) collective-permute-start(bf16[384,1024]{1,0:T(8,128)(2,1)S(1)} %pad_maximum_fusion.1.here.audio), channel_id=1, source_target_pairs={{0,2},{1,3},{2,4},{3,5},{4,6},{5,7},{6,8},{7,9},{8,10},{9,11},{10,... | collective-permute-start | bytes 2359304 | tf_op jit(solution)/shard_map/ppermute | solution.py:391
  48.4 2.5 %collective-permute-start.2 = (bf16[384,1024]{1,0:T(8,128)(2,1)S(1)}, bf16[384,1024]{1,0:T(8,128)(2,1)}, u32[]{:S(2)}, u32[]{:S(2)}) collective-permute-start(bf16[384,1024]{1,0:T(8,128)(2,1)S(1)} %pad_maximum_fusion.1.here.audio), channel_id=1, source_target_pairs={{2,0},{3,1},{4,2},{5,3},{6,4},{7,5},{8,6},{9,7},{10,8},{11,9},{12,... | collective-permute-start | bytes 2359304 | tf_op jit(solution)/shard_map/ppermute | solution.py:391
  50.9 15.8 %all-to-all-done.1 = bf16[16,16,1024]{2,1,0:T(8,128)(2,1)S(1)} async-done(((bf16[16,16,1024]{2,1,0:T(8,128)(2,1)}), bf16[16,16,1024]{2,1,0:T(8,128)(2,1)S(1)}, u32[]{:S(2)}, u32[]{:S(2)}) %all-to-all-start.1) | async-done | bytes 524320 | tf_op jit(solution)/shard_map/all_to_all | solution.py:388
  66.8 3.3 %collective-permute-start.3 = (bf16[128,1024]{1,0:T(8,128)(2,1)S(1)}, bf16[128,1024]{1,0:T(8,128)(2,1)S(1)}, u32[]{:S(2)}, u32[]{:S(2)}) collective-permute-start(bf16[128,1024]{1,0:T(8,128)(2,1)S(1)} %bitcast.43), channel_id=1, source_target_pairs={{0,2},{1,3},{2,4},{3,5},{4,6},{5,7},{6,8},{7,9},{8,10},{9,11},{10,... | collective-permute-start | bytes 786440 | tf_op jit(solution)/shard_map/ppermute | solution.py:391
  70.1 2.5 %collective-permute-start.4 = (bf16[128,1024]{1,0:T(8,128)(2,1)S(1)}, bf16[128,1024]{1,0:T(8,128)(2,1)S(1)}, u32[]{:S(2)}, u32[]{:S(2)}) collective-permute-start(bf16[128,1024]{1,0:T(8,128)(2,1)S(1)} %bitcast.44), channel_id=1, source_target_pairs={{2,0},{3,1},{4,2},{5,3},{6,4},{7,5},{8,6},{9,7},{10,8},{11,9},{12,... | collective-permute-start | bytes 786440 | tf_op jit(solution)/shard_map/ppermute | solution.py:391
  72.6 3.9 %collective-permute-done.1.before = bf16[384,1024]{1,0:T(8,128)(2,1)} collective-permute-done((bf16[384,1024]{1,0:T(8,128)(2,1)S(1)}, bf16[384,1024]{1,0:T(8,128)(2,1)}, u32[]{:S(2)}, u32[]{:S(2)}) %collective-permute-start.1) | collective-permute-done | bytes 786464 | tf_op jit(solution)/shard_map/ppermute | solution.py:391
  76.5 3.3 %collective-permute-done.2.after = bf16[384,1024]{1,0:T(8,128)(2,1)} collective-permute-done((bf16[384,1024]{1,0:T(8,128)(2,1)S(1)}, bf16[384,1024]{1,0:T(8,128)(2,1)}, u32[]{:S(2)}, u32[]{:S(2)}) %collective-permute-start.2) | collective-permute-done | bytes 786464 | tf_op jit(solution)/shard_map/ppermute | solution.py:391
  79.8 2.8 %shard_map.145 = (bf16[64,1024]{1,0:T(8,128)(2,1)S(1)}, bf16[152,1024]{1,0:T(8,128)(2,1)S(1)}) custom-call(s32[16,32]{1,0:T(8,128)S(1)} %copy-done.2, bf16[256,1024]{1,0:T(8,128)(2,1)S(1)} %bitcast.39, bf16[384,1024]{1,0:T(8,128)(2,1)} %collective-permute-done.1.before, bf16[384,1024]{1,0:T(8,128)(2,1)S(1)} %pad_maximum_fusion.1.here.audio, ...), custom_call_target="tpu_custom_call" | custom-call | flops 377487360 | bytes 5242880 | tf_op jit(solution)/shard_map/pallas_call | solution.py:266
  82.7 3.3 %collective-permute-start.7 = (bf16[152,1024]{1,0:T(8,128)(2,1)S(1)}, bf16[152,1024]{1,0:T(8,128)(2,1)S(1)}, u32[]{:S(2)}, u32[]{:S(2)}) collective-permute-start(bf16[152,1024]{1,0:T(8,128)(2,1)S(1)} %get-tuple-element.23.here), channel_id=1, source_target_pairs={{0,2},{1,3},{2,4},{3,5},{4,6},{5,7},{6,8},{7,9},{8,10},{9,11},{10,... | collective-permute-start | bytes 933896 | tf_op jit(solution)/shard_map/ppermute | solution.py:391
  86.0 2.5 %collective-permute-start.8 = (bf16[152,1024]{1,0:T(8,128)(2,1)S(1)}, bf16[152,1024]{1,0:T(8,128)(2,1)S(1)}, u32[]{:S(2)}, u32[]{:S(2)}) collective-permute-start(bf16[152,1024]{1,0:T(8,128)(2,1)S(1)} %get-tuple-element.23.here), channel_id=1, source_target_pairs={{2,0},{3,1},{4,2},{5,3},{6,4},{7,5},{8,6},{9,7},{10,8},{11,9},{12,... | collective-permute-start | bytes 933896 | tf_op jit(solution)/shard_map/ppermute | solution.py:391
  88.6 2.4 %shard_map.146 = (bf16[192,1024]{1,0:T(8,128)(2,1)S(1)}, bf16[128,1024]{1,0:T(8,128)(2,1)S(1)}, bf16[128,1024]{1,0:T(8,128)(2,1)S(1)}, bf16[128,1024]{1,0:T(8,128)(2,1)S(1)}) custom-call(s32[16,32]{1,0:T(8,128)S(1)} %copy-done.2, bf16[96,2048]{1,0:T(8,128)(2,1)S(1)} %bitcast.42, bf16[96,2048]{1,0:T(8,128)(2,1)S(1)} %bitcast.41, ...), custom_call_target="tpu_custom_call" | custom-call | flops 377487360 | bytes 3145728 | tf_op jit(solution)/shard_map/pallas_call | solution.py:266
  91.0 1.9 %collective-permute-start.5 = (bf16[128,1024]{1,0:T(8,128)(2,1)S(1)}, bf16[128,1024]{1,0:T(8,128)(2,1)S(1)}, u32[]{:S(2)}, u32[]{:S(2)}) collective-permute-start(bf16[128,1024]{1,0:T(8,128)(2,1)S(1)} %get-tuple-element.17), channel_id=1, source_target_pairs={{2,0},{3,1},{4,2},{5,3},{6,4},{7,5},{8,6},{9,7},{10,8},{11,9},{12,... | collective-permute-start | bytes 786440 | tf_op jit(solution)/shard_map/ppermute | solution.py:391
  92.9 6.0 %collective-permute-start.6 = (bf16[128,1024]{1,0:T(8,128)(2,1)S(1)}, bf16[128,1024]{1,0:T(8,128)(2,1)S(1)}, u32[]{:S(2)}, u32[]{:S(2)}) collective-permute-start(bf16[128,1024]{1,0:T(8,128)(2,1)S(1)} %get-tuple-element.18), channel_id=1, source_target_pairs={{0,2},{1,3},{2,4},{3,5},{4,6},{5,7},{6,8},{7,9},{8,10},{9,11},{10,... | collective-permute-start | bytes 786440 | tf_op jit(solution)/shard_map/ppermute | solution.py:391
  99.0 2.4 %shard_map.147 = bf16[384,1024]{1,0:T(8,128)(2,1)S(1)} custom-call(s32[16,32]{1,0:T(8,128)S(1)} %copy-done.2, bf16[152,1024]{1,0:T(8,128)(2,1)S(1)} %collective-permute-done.7.before, bf16[152,1024]{1,0:T(8,128)(2,1)S(1)} %get-tuple-element.23.here, bf16[152,1024]{1,0:T(8,128)(2,1)S(1)} %collective-permute-done.8.after, ...), custom_call_target="tpu_custom_call" | custom-call | flops 377487360 | bytes 3145728 | tf_op jit(solution)/shard_map/pallas_call | solution.py:266
  101.4 1.7 %collective-permute-done.5.t1 = bf16[128,1024]{1,0:T(8,128)(2,1)S(1)} collective-permute-done((bf16[128,1024]{1,0:T(8,128)(2,1)S(1)}, bf16[128,1024]{1,0:T(8,128)(2,1)S(1)}, u32[]{:S(2)}, u32[]{:S(2)}) %collective-permute-start.5) | collective-permute-done | bytes 262176 | tf_op jit(solution)/shard_map/ppermute | solution.py:391
  103.5 0.8 gather.1
  104.3 11.1 %all-to-all-start.2 = ((bf16[16,48,256]{2,1,0:T(8,128)(2,1)}), bf16[16,48,256]{2,1,0:T(8,128)(2,1)S(1)}, u32[]{:S(2)}, u32[]{:S(2)}) async-start(bf16[16,48,256]{2,1,0:T(8,128)(2,1)} %gather.1), calls=%async_computation.2 | async-start | bytes 786432 | tf_op jit(solution)/shard_map/all_to_all | solution.py:388
  115.5 1.9 %collective-permute-start.9 = (bf16[288,1024]{1,0:T(8,128)(2,1)S(1)}, bf16[288,1024]{1,0:T(8,128)(2,1)S(1)}, u32[]{:S(2)}, u32[]{:S(2)}) collective-permute-start(bf16[288,1024]{1,0:T(8,128)(2,1)S(1)} %pad_maximum_fusion.2), channel_id=1, source_target_pairs={{0,1},{1,0},{2,3},{3,2},{4,5},{5,4},{6,7},{7,6},{8,9},{9,8},{10,11... | collective-permute-start | bytes 1769480 | tf_op jit(solution)/shard_map/ppermute | solution.py:396
  117.4 15.6 %all-to-all-done.2.x = bf16[16,48,256]{2,1,0:T(8,128)(2,1)S(1)} async-done(((bf16[16,48,256]{2,1,0:T(8,128)(2,1)}), bf16[16,48,256]{2,1,0:T(8,128)(2,1)S(1)}, u32[]{:S(2)}, u32[]{:S(2)}) %all-to-all-start.2) | async-done | bytes 393248 | tf_op jit(solution)/shard_map/all_to_all | solution.py:388
  133.0 1.4 place.3
  134.5 3.9 %all-to-all-start.3 = ((bf16[32,24,256]{2,1,0:T(8,128)(2,1)}), bf16[32,24,256]{2,1,0:T(8,128)(2,1)S(1)}, u32[]{:S(2)}, u32[]{:S(2)}) async-start(bf16[32,24,256]{2,1,0:T(8,128)(2,1)} %bitcast.18), calls=%async_computation.3 | async-start | bytes 786432 | tf_op jit(solution)/shard_map/all_to_all | solution.py:383
  138.4 0.8 maximum_select_fusion.2
  139.3 1.2 maximum_select_fusion
  140.4 15.7 %all-to-all-done.3.x = bf16[32,24,256]{2,1,0:T(8,128)(2,1)S(1)} async-done(((bf16[32,24,256]{2,1,0:T(8,128)(2,1)}), bf16[32,24,256]{2,1,0:T(8,128)(2,1)S(1)}, u32[]{:S(2)}, u32[]{:S(2)}) %all-to-all-start.3) | async-done | bytes 393248 | tf_op jit(solution)/shard_map/all_to_all | solution.py:383
  (30 shorter events, 1.6 us)
Async XLA Ops:
  2.6 16.1 %copy-start = (bf16[1,96,2048]{2,1,0:T(8,128)(2,1)S(1)}, bf16[1,96,2048]{2,1,0:T(8,128)(2,1)}, u32[]{:S(2)}) copy-start(bf16[1,96,2048]{2,1,0:T(8,128)(2,1)} %param.17) | copy-start | bytes 1179652
  2.6 16.1 %copy-start.4 = (bf16[1,96,2048]{2,1,0:T(8,128)(2,1)S(1)}, bf16[1,96,2048]{2,1,0:T(8,128)(2,1)}, u32[]{:S(2)}) copy-start(bf16[1,96,2048]{2,1,0:T(8,128)(2,1)} %param.16) | copy-start | bytes 1179652
  2.6 36.2 %all-to-all-start = ((bf16[32,8,1024]{2,1,0:T(8,128)(2,1)}), bf16[32,8,1024]{2,1,0:T(8,128)(2,1)S(1)}, u32[]{:S(2)}, u32[]{:S(2)}) async-start(bf16[32,8,1024]{2,1,0:T(8,128)(2,1)} %bitcast.6), calls=%async_computation | async-start | bytes 1048576 | tf_op jit(solution)/shard_map/all_to_all | solution.py:383
  18.7 1.0 copy-start.5
  18.7 1.1 copy-start.1
  19.8 19.0 %copy-start.3 = (s32[16]{0:T(128)S(1)}, s32[16]{0:T(128)}, u32[]{:S(2)}) copy-start(s32[16]{0:T(128)} %index.3) | copy-start | bytes 196
  20.8 24.2 %collective-permute-start = (bf16[384,1024]{1,0:T(8,128)(2,1)}, bf16[384,1024]{1,0:T(8,128)(2,1)S(1)}, u32[]{:S(2)}, u32[]{:S(2)}) collective-permute-start(bf16[384,1024]{1,0:T(8,128)(2,1)} %pad_maximum_fusion), channel_id=1, source_target_pairs={{0,1},{1,0},{2,3},{3,2},{4,5},{5,4},{6,7},{7,6},{8,9},{9,8},{10,11... | collective-permute-start | bytes 2359304 | tf_op jit(solution)/shard_map/ppermute | solution.py:396
  40.3 26.5 %all-to-all-start.1 = ((bf16[16,16,1024]{2,1,0:T(8,128)(2,1)}), bf16[16,16,1024]{2,1,0:T(8,128)(2,1)S(1)}, u32[]{:S(2)}, u32[]{:S(2)}) async-start(bf16[16,16,1024]{2,1,0:T(8,128)(2,1)} %place.2), calls=%async_computation.1 | async-start | bytes 1048576 | tf_op jit(solution)/shard_map/all_to_all | solution.py:388
  45.0 34.8 %copy-start.2 = (s32[16,32]{1,0:T(8,128)S(1)}, s32[16,32]{1,0:T(8,128)}, u32[]{:S(2)}) copy-start(s32[16,32]{1,0:T(8,128)} %lens.5) | copy-start | bytes 6148
  45.1 31.5 %collective-permute-start.1 = (bf16[384,1024]{1,0:T(8,128)(2,1)S(1)}, bf16[384,1024]{1,0:T(8,128)(2,1)}, u32[]{:S(2)}, u32[]{:S(2)}) collective-permute-start(bf16[384,1024]{1,0:T(8,128)(2,1)S(1)} %pad_maximum_fusion.1.here.audio), channel_id=1, source_target_pairs={{0,2},{1,3},{2,4},{3,5},{4,6},{5,7},{6,8},{7,9},{8,10},{9,11},{10,... | collective-permute-start | bytes 2359304 | tf_op jit(solution)/shard_map/ppermute | solution.py:391
  48.4 31.4 %collective-permute-start.2 = (bf16[384,1024]{1,0:T(8,128)(2,1)S(1)}, bf16[384,1024]{1,0:T(8,128)(2,1)}, u32[]{:S(2)}, u32[]{:S(2)}) collective-permute-start(bf16[384,1024]{1,0:T(8,128)(2,1)S(1)} %pad_maximum_fusion.1.here.audio), channel_id=1, source_target_pairs={{2,0},{3,1},{4,2},{5,3},{6,4},{7,5},{8,6},{9,7},{10,8},{11,9},{12,... | collective-permute-start | bytes 2359304 | tf_op jit(solution)/shard_map/ppermute | solution.py:391
  66.8 21.8 %collective-permute-start.3 = (bf16[128,1024]{1,0:T(8,128)(2,1)S(1)}, bf16[128,1024]{1,0:T(8,128)(2,1)S(1)}, u32[]{:S(2)}, u32[]{:S(2)}) collective-permute-start(bf16[128,1024]{1,0:T(8,128)(2,1)S(1)} %bitcast.43), channel_id=1, source_target_pairs={{0,2},{1,3},{2,4},{3,5},{4,6},{5,7},{6,8},{7,9},{8,10},{9,11},{10,... | collective-permute-start | bytes 786440 | tf_op jit(solution)/shard_map/ppermute | solution.py:391
  70.1 18.4 %collective-permute-start.4 = (bf16[128,1024]{1,0:T(8,128)(2,1)S(1)}, bf16[128,1024]{1,0:T(8,128)(2,1)S(1)}, u32[]{:S(2)}, u32[]{:S(2)}) collective-permute-start(bf16[128,1024]{1,0:T(8,128)(2,1)S(1)} %bitcast.44), channel_id=1, source_target_pairs={{2,0},{3,1},{4,2},{5,3},{6,4},{7,5},{8,6},{9,7},{10,8},{11,9},{12,... | collective-permute-start | bytes 786440 | tf_op jit(solution)/shard_map/ppermute | solution.py:391
  82.7 16.3 %collective-permute-start.7 = (bf16[152,1024]{1,0:T(8,128)(2,1)S(1)}, bf16[152,1024]{1,0:T(8,128)(2,1)S(1)}, u32[]{:S(2)}, u32[]{:S(2)}) collective-permute-start(bf16[152,1024]{1,0:T(8,128)(2,1)S(1)} %get-tuple-element.23.here), channel_id=1, source_target_pairs={{0,2},{1,3},{2,4},{3,5},{4,6},{5,7},{6,8},{7,9},{8,10},{9,11},{10,... | collective-permute-start | bytes 933896 | tf_op jit(solution)/shard_map/ppermute | solution.py:391
  86.0 13.0 %collective-permute-start.8 = (bf16[152,1024]{1,0:T(8,128)(2,1)S(1)}, bf16[152,1024]{1,0:T(8,128)(2,1)S(1)}, u32[]{:S(2)}, u32[]{:S(2)}) collective-permute-start(bf16[152,1024]{1,0:T(8,128)(2,1)S(1)} %get-tuple-element.23.here), channel_id=1, source_target_pairs={{2,0},{3,1},{4,2},{5,3},{6,4},{7,5},{8,6},{9,7},{10,8},{11,9},{12,... | collective-permute-start | bytes 933896 | tf_op jit(solution)/shard_map/ppermute | solution.py:391
  91.0 12.1 %collective-permute-start.5 = (bf16[128,1024]{1,0:T(8,128)(2,1)S(1)}, bf16[128,1024]{1,0:T(8,128)(2,1)S(1)}, u32[]{:S(2)}, u32[]{:S(2)}) collective-permute-start(bf16[128,1024]{1,0:T(8,128)(2,1)S(1)} %get-tuple-element.17), channel_id=1, source_target_pairs={{2,0},{3,1},{4,2},{5,3},{6,4},{7,5},{8,6},{9,7},{10,8},{11,9},{12,... | collective-permute-start | bytes 786440 | tf_op jit(solution)/shard_map/ppermute | solution.py:391
  92.9 10.5 %collective-permute-start.6 = (bf16[128,1024]{1,0:T(8,128)(2,1)S(1)}, bf16[128,1024]{1,0:T(8,128)(2,1)S(1)}, u32[]{:S(2)}, u32[]{:S(2)}) collective-permute-start(bf16[128,1024]{1,0:T(8,128)(2,1)S(1)} %get-tuple-element.18), channel_id=1, source_target_pairs={{0,2},{1,3},{2,4},{3,5},{4,6},{5,7},{6,8},{7,9},{8,10},{9,11},{10,... | collective-permute-start | bytes 786440 | tf_op jit(solution)/shard_map/ppermute | solution.py:391
  104.3 28.7 %all-to-all-start.2 = ((bf16[16,48,256]{2,1,0:T(8,128)(2,1)}), bf16[16,48,256]{2,1,0:T(8,128)(2,1)S(1)}, u32[]{:S(2)}, u32[]{:S(2)}) async-start(bf16[16,48,256]{2,1,0:T(8,128)(2,1)} %gather.1), calls=%async_computation.2 | async-start | bytes 786432 | tf_op jit(solution)/shard_map/all_to_all | solution.py:388
  115.5 22.9 %collective-permute-start.9 = (bf16[288,1024]{1,0:T(8,128)(2,1)S(1)}, bf16[288,1024]{1,0:T(8,128)(2,1)S(1)}, u32[]{:S(2)}, u32[]{:S(2)}) collective-permute-start(bf16[288,1024]{1,0:T(8,128)(2,1)S(1)} %pad_maximum_fusion.2), channel_id=1, source_target_pairs={{0,1},{1,0},{2,3},{3,2},{4,5},{5,4},{6,7},{7,6},{8,9},{9,8},{10,11... | collective-permute-start | bytes 1769480 | tf_op jit(solution)/shard_map/ppermute | solution.py:396
  134.5 21.7 %all-to-all-start.3 = ((bf16[32,24,256]{2,1,0:T(8,128)(2,1)}), bf16[32,24,256]{2,1,0:T(8,128)(2,1)S(1)}, u32[]{:S(2)}, u32[]{:S(2)}) async-start(bf16[32,24,256]{2,1,0:T(8,128)(2,1)} %bitcast.18), calls=%async_computation.3 | async-start | bytes 786432 | tf_op jit(solution)/shard_map/all_to_all | solution.py:383
